TPU v7x, 32 devices: a whole 2x2x4 slice. The times are simulated.
32 devices in a mesh: dp: 8 (over z, x), tensor: 4 (over y, core).
Axes of the slice: x: 2, y: 2, z: 4, core: 2. Of those that a mesh axis runs over, the one named last changes fastest.
Arguments:
- layer_input: bfloat16 [16, 512, 2048], P('dp'), may hold values from -6 to 6
- segments: int32 [16, 512], P('dp'), may hold values from 0 to 3, never falling along the last dimension, each value on 1 to 256 neighbouring positions
- query_weight: bfloat16 [2048, 2048], P('dp', 'tensor'), may hold values from -0.125 to 0.125
- key_matrix: bfloat16 [2048, 1024], P('dp', 'tensor'), may hold values from -0.125 to 0.125
- value_matrix: bfloat16 [2048, 1024], P('dp', 'tensor'), may hold values from -0.125 to 0.125
- gate_weight: bfloat16 [2048, 2048], P('dp', 'tensor'), may hold values from -0.125 to 0.125
- out_weight: bfloat16 [2048, 2048], P('tensor', 'dp'), may hold values from -1 to 1
- ffn_gate_weight: bfloat16 [2048, 6144], P('dp', 'tensor'), may hold values from -0.125 to 0.125
- ffn_up_weight: bfloat16 [2048, 6144], P('dp', 'tensor'), may hold values from -0.125 to 0.125
- ffn_down_weight: bfloat16 [6144, 2048], P('tensor', 'dp'), may hold values from -0.109375 to 0.109375
- attn_gain: float32 [2048], replicated, may hold values from 0.5 to 1.5
- ffn_gain: float32 [2048], replicated, may hold values from 0.5 to 1.5
- query_gain: float32 [128], replicated, may hold values from 0.1 to 1.9
- key_norm_gain: float32 [128], replicated, may hold values from 0.1 to 1.9
- cotangent: bfloat16 [16, 512, 2048], P('dp'), may hold values from -6 to 6
Outputs:
- output: bfloat16 [16, 512, 2048], P('dp')
- input_grad: float32 [16, 512, 2048], P('dp')
- grad_query_weight: float32 [2048, 2048], P('dp', 'tensor')
- grad_key_weight: float32 [2048, 1024], P('dp', 'tensor')
- grad_value_weight: float32 [2048, 1024], P('dp', 'tensor')
- grad_gate_weight: float32 [2048, 2048], P('dp', 'tensor')
- grad_out_weight: float32 [2048, 2048], P('tensor', 'dp')
- grad_ffn_gate_weight: float32 [2048, 6144], P('dp', 'tensor')
- grad_ffn_up_weight: float32 [2048, 6144], P('dp', 'tensor')
- grad_ffn_down_weight: float32 [6144, 2048], P('tensor', 'dp')
- grad_attn_gain: float32 [2048], replicated
- grad_ffn_gain: float32 [2048], replicated
- grad_query_gain: float32 [128], replicated
- grad_key_gain: float32 [128], replicated
Inputs may be any that keep to these rules, and one draw needn't show every extreme that they name: `segments`: segment numbers never fall along a sequence; each document holds 1 to 256 tokens and some document holds exactly 256.
All inputs are finite; a program needn't handle non-finite values.
Results may differ from a plain program's by a relative error of at most 0.02.
Values may be sent and summed in bfloat16 or wider, within the bound.
No kernel may reach another device: no remote copies, remote signals or barrier semaphores. Data moves between devices by JAX's collectives and lax.ppermute only.
A program may use at most 256 MiB of HBM per device.

v0:
```python
import math

import jax
import jax.numpy as jnp
from jax import lax
from jax.experimental import pallas as pl
from jax.experimental.pallas import tpu as pltpu
from jax.sharding import PartitionSpec as P


epsilon = 1e-06
low_type = jnp.bfloat16
wide_type = jnp.float32


def norm_fwd(vector_in):
    scale_inv = lax.rsqrt(jnp.mean(vector_in * vector_in, axis=-1, keepdims=True) + epsilon)
    return (vector_in * scale_inv, scale_inv)


def norm_back(normal, scale_inv, gain_vec, grad_in_rows):
    scaled = grad_in_rows * gain_vec
    grad_rows = scale_inv * (scaled - normal * jnp.mean(scaled * normal, axis=-1, keepdims=True))
    return (grad_rows, jnp.sum(grad_in_rows * normal, axis=0))


def tables(segment_row, head_size):
    token_length = segment_row.shape[0]
    places = jnp.arange(token_length, dtype=jnp.int32)
    changed = jnp.concatenate(
        [jnp.ones((1,), dtype=jnp.bool_), segment_row[1:] != segment_row[:-1]]
    )
    starts = lax.cummax(jnp.where(changed, places, jnp.zeros_like(places)), axis=0)
    position = (places - starts).astype(jnp.float32)
    frequency = jnp.exp(
        jnp.arange(head_size // 2, dtype=jnp.float32) * (-2.0 * math.log(1000000.0) / head_size)
    )
    angles = position[:, None] * frequency[None, :]
    sine = jnp.sin(angles)
    return (
        jnp.concatenate([jnp.cos(angles), jnp.cos(angles)], axis=-1),
        jnp.concatenate([-sine, sine], axis=-1),
    )


def head_norm(projected):
    inverse = lax.rsqrt(jnp.mean(projected * projected, axis=-1, keepdims=True) + epsilon)
    return projected * inverse, inverse


def rotate(rows, cosine, signed_sine):
    return rows * cosine + pltpu.roll(rows, rows.shape[-1] // 2, 1) * signed_sine


def rotate_back(grad, cosine, signed_sine):
    return grad * cosine + pltpu.roll(grad * signed_sine, grad.shape[-1] // 2, 1)


def norm_rows_back(normal, inverse, gain, grad):
    scaled = grad * gain
    return inverse * (scaled - normal * jnp.mean(scaled * normal, axis=-1, keepdims=True))


def dot_nt(left, right):
    return lax.dot_general(left, right, (((1,), (1,)), ((), ())), preferred_element_type=wide_type)


def dot_tn(left, right):
    return lax.dot_general(left, right, (((0,), (0,)), ((), ())), preferred_element_type=wide_type)


def allowed_pairs(seg_col, seg_row):
    shape = (seg_col.shape[0], seg_row.shape[1])
    later = lax.broadcasted_iota(jnp.int32, shape, 0) >= lax.broadcasted_iota(jnp.int32, shape, 1)
    return (seg_col == seg_row) & later


def softmax_rows(query, key, allowed, scaling):
    scores = jnp.where(allowed, dot_nt(query, key) * scaling, -1000000000.0)
    exponent = jnp.exp(scores - jnp.max(scores, axis=-1, keepdims=True))
    return exponent / jnp.sum(exponent, axis=-1, keepdims=True)


def attention_forward(
    q_ref, k_ref, v_ref, g_ref, cos_ref, sin_ref, col_ref, row_ref, gq_ref, gk_ref, out_ref
):
    head = k_ref.shape[1]
    scaling = head ** (-0.5)
    cosine, sine = cos_ref[...], sin_ref[...]
    allowed = allowed_pairs(col_ref[0], row_ref[0])
    key = rotate(head_norm(k_ref[...])[0] * gk_ref[...], cosine, sine).astype(low_type)
    value = v_ref[...].astype(low_type)
    for member in range(q_ref.shape[1] // head):
        cols = pl.ds(member * head, head)
        query = rotate(head_norm(q_ref[:, cols])[0] * gq_ref[...], cosine, sine).astype(low_type)
        probs = softmax_rows(query, key, allowed, scaling).astype(low_type)
        attended = jnp.dot(probs, value, preferred_element_type=wide_type)
        out_ref[:, cols] = (attended * jax.nn.sigmoid(g_ref[:, cols])).astype(low_type)


def attention_backward(
    q_ref,
    k_ref,
    v_ref,
    g_ref,
    cos_ref,
    sin_ref,
    col_ref,
    row_ref,
    gq_ref,
    gk_ref,
    grad_ref,
    dq_ref,
    dk_ref,
    dv_ref,
    dg_ref,
    gain_ref,
):
    head = k_ref.shape[1]
    scaling = head ** (-0.5)
    cosine, sine = cos_ref[...], sin_ref[...]
    allowed = allowed_pairs(col_ref[0], row_ref[0])
    key_normal, key_inverse = head_norm(k_ref[...])
    key = rotate(key_normal * gk_ref[...], cosine, sine).astype(low_type)
    value = v_ref[...].astype(low_type)
    grad_value = jnp.zeros(value.shape, wide_type)
    grad_key = jnp.zeros(value.shape, wide_type)
    query_gain = jnp.zeros((1, head), wide_type)
    for member in range(q_ref.shape[1] // head):
        cols = pl.ds(member * head, head)
        query_normal, query_inverse = head_norm(q_ref[:, cols])
        query = rotate(query_normal * gq_ref[...], cosine, sine).astype(low_type)
        probs = softmax_rows(query, key, allowed, scaling)
        probs_low = probs.astype(low_type)
        attended = jnp.dot(probs_low, value, preferred_element_type=wide_type)
        gate = jax.nn.sigmoid(g_ref[:, cols])
        grad_gated = grad_ref[:, cols].astype(wide_type)
        grad_attended = (grad_gated * gate).astype(low_type)
        dg_ref[:, cols] = (grad_gated * attended * gate * (1.0 - gate)).astype(low_type)
        grad_value = grad_value + dot_tn(probs_low, grad_attended)
        grad_probs = dot_nt(grad_attended, value)
        mixed = jnp.sum(probs * grad_probs, axis=-1, keepdims=True)
        grad_scores = (probs * (grad_probs - mixed) * scaling).astype(low_type)
        grad_query = rotate_back(
            jnp.dot(grad_scores, key, preferred_element_type=wide_type), cosine, sine
        )
        grad_key = grad_key + dot_tn(grad_scores, query)
        query_gain = query_gain + jnp.sum(grad_query * query_normal, axis=0, keepdims=True)
        dq_ref[:, cols] = norm_rows_back(
            query_normal, query_inverse, gq_ref[...], grad_query
        ).astype(low_type)
    grad_key = rotate_back(grad_key, cosine, sine)
    dk_ref[...] = norm_rows_back(key_normal, key_inverse, gk_ref[...], grad_key).astype(low_type)
    dv_ref[...] = grad_value.astype(low_type)
    gain_ref[0, 0, 0:1] = query_gain
    gain_ref[0, 0, 1:2] = jnp.sum(grad_key * key_normal, axis=0, keepdims=True)


def attention_specs(length, head, group, kv_heads):
    wide = group * head
    specs = [
        pl.BlockSpec((length, wide), lambda s, k: (s, k)),
        pl.BlockSpec((length, head), lambda s, k: (s, kv_heads * group + k)),
        pl.BlockSpec((length, head), lambda s, k: (s, kv_heads * (group + 1) + k)),
        pl.BlockSpec((length, wide), lambda s, k: (s, kv_heads * (group + 2) // group + k)),
        pl.BlockSpec((length, head), lambda s, k: (s, 0)),
        pl.BlockSpec((length, head), lambda s, k: (s, 0)),
        pl.BlockSpec((1, length, 1), lambda s, k: (s, 0, 0)),
        pl.BlockSpec((1, 1, length), lambda s, k: (s, 0, 0)),
        pl.BlockSpec((1, head), lambda s, k: (0, 0)),
        pl.BlockSpec((1, head), lambda s, k: (0, 0)),
    ]
    return specs, specs[0], pl.BlockSpec((length, head), lambda s, k: (s, k))


def attention_calls(seqs, length, head, group, kv_heads, interpret=False):
    specs, wide_spec, head_spec = attention_specs(length, head, group, kv_heads)
    tokens = seqs * length
    wide = jax.ShapeDtypeStruct((tokens, kv_heads * group * head), low_type)
    narrow = jax.ShapeDtypeStruct((tokens, kv_heads * head), low_type)
    gains = jax.ShapeDtypeStruct((seqs, kv_heads, 2, head), wide_type)
    forward = pl.pallas_call(
        attention_forward,
        grid=(seqs, kv_heads),
        in_specs=specs,
        out_specs=wide_spec,
        out_shape=wide,
        interpret=interpret,
    )
    backward = pl.pallas_call(
        attention_backward,
        grid=(seqs, kv_heads),
        in_specs=specs + [wide_spec],
        out_specs=[
            wide_spec,
            head_spec,
            head_spec,
            wide_spec,
            pl.BlockSpec((1, 1, 2, head), lambda s, k: (s, k, 0, 0)),
        ],
        out_shape=[wide, narrow, narrow, wide, gains],
        interpret=interpret,
    )
    return forward, backward


def transpose_block(in_ref, out_ref):
    out_ref[...] = in_ref[...].T


def turned(grad):
    rows, cols = grad.shape
    step = min(cols, 256)
    return pl.pallas_call(
        transpose_block,
        grid=(cols // step,),
        in_specs=[pl.BlockSpec((rows, step), lambda i: (0, i))],
        out_specs=pl.BlockSpec((step, rows), lambda i: (i, 0)),
        out_shape=jax.ShapeDtypeStruct((cols, rows), grad.dtype),
    )(grad)


def matmul(left, right):
    return jnp.dot(left, right, preferred_element_type=wide_type)


def matmul_nt(left, right):
    return jnp.einsum("tf,df->td", left, right, preferred_element_type=wide_type)


def matmul_tn(left, right):
    return jnp.einsum("td,tf->df", left, right, preferred_element_type=wide_type)


def swap_pairs(size, bit):
    return [(place, place ^ bit) for place in range(size)]


def after(value, *earlier):
    if isinstance(value, tuple):
        return tuple(after(part, *earlier) for part in value)
    return lax.optimization_barrier((value,) + earlier)[0] if earlier else value


def halves(rows_of, side, extent, axis):
    half = extent // 2
    return (
        lax.dynamic_slice_in_dim(rows_of, (1 - side) * half, half, axis),
        lax.dynamic_slice_in_dim(rows_of, side * half, half, axis),
    )


def tensor_scatter(make, operands, rank, size, fill=()):
    rows = operands[0].shape[0]
    split = [halves(operand, rank % 2, rows, 0) for operand in operands]
    sent = make(*[pair[0] for pair in split]).astype(low_type)
    received = lax.ppermute(sent, "tensor", swap_pairs(size, 1))
    kept = make(*[pair[1] for pair in split])
    kept = kept + after(received, kept).astype(wide_type)
    rows, bit = rows // 2, 2
    while bit < size:
        sent, kept = halves(kept, (rank // bit) % 2, rows, 0)
        received = lax.ppermute(sent.astype(low_type), "tensor", swap_pairs(size, bit))
        kept = kept + after(received, *fill).astype(wide_type)
        rows, bit = rows // 2, bit * 2
    return kept


def share_start(rank, size, rows):
    start, bit = 0, 1
    while bit < size:
        rows = rows // 2
        start = start + ((rank // bit) % 2) * rows
        bit = bit * 2
    return start


def tensor_gather(share, rank, size, fill=()):
    bit = size // 2
    while bit >= 1:
        received = lax.ppermute(share, "tensor", swap_pairs(size, bit))
        received = after(received, *fill) if bit > 1 else received
        low_side = (rank // bit) % 2 == 0
        share = jnp.concatenate(
            [jnp.where(low_side, share, received), jnp.where(low_side, received, share)], axis=0
        )
        bit = bit // 2
    return share


def outer_route(step, inner, outer):
    return [
        (z * inner + x, ((z + step) % outer) * inner + x)
        for z in range(outer)
        for x in range(inner)
    ]


def line_send(shard, inner, outer):
    arrived = [
        lax.ppermute(shard, "dp", outer_route(step, inner, outer))
        for step in range(1, outer)
    ]
    return arrived, lax.ppermute(shard, "dp", swap_pairs(inner * outer, 1))


def pair_send(arrived, inner, outer):
    return [lax.ppermute(part, "dp", swap_pairs(inner * outer, 1)) for part in arrived]


def line_join(shard, arrived, rank, inner, outer):
    place = rank // inner
    line = lax.dynamic_update_slice_in_dim(
        jnp.zeros((outer,) + shard.shape, shard.dtype), shard[None], place, 0
    )
    for step in range(1, outer):
        line = lax.dynamic_update_slice_in_dim(
            line, arrived[step - 1][None], lax.rem(place + outer - step, outer), 0
        )
    return line


def in_order(shard, arrived, partner, passed, rank, inner, outer):
    line = line_join(shard, arrived, rank, inner, outer)
    other = line_join(partner, passed, rank, inner, outer)
    side = rank % inner
    return jnp.where(side == 0, line, other), jnp.where(side == 0, other, line)


def join_rows(pair):
    outer, rows, cols = pair[0].shape
    return jnp.stack(pair, axis=1).reshape(outer * len(pair) * rows, cols)


def join_columns(pair):
    return jnp.concatenate([part[z] for z in range(pair[0].shape[0]) for part in pair], axis=1)


def scatter_send(grad, rank, inner, outer):
    rows, cols = grad.shape[0] // (inner * outer), grad.shape[1]
    blocks = grad.reshape(outer, inner, rows, cols)
    place, side = rank // inner, rank % inner
    received = []
    for step in list(range(1, outer)) + [0]:
        sent = lax.dynamic_slice(
            blocks, (lax.rem(place + step, outer), 1 - side, 0, 0), (1, 1, rows, cols)
        ).reshape(rows, cols)
        received.append(lax.ppermute(sent, "dp", swap_pairs(inner * outer, 1)))
    return blocks, tuple(received)


def scatter_line(blocks, received, rank, inner, outer):
    place, side = rank // inner, rank % inner
    rows, cols = blocks.shape[2:]

    def block(step, theirs):
        mine = lax.dynamic_slice(
            blocks, (lax.rem(place + step, outer), side, 0, 0), (1, 1, rows, cols)
        ).reshape(rows, cols)
        return mine.astype(wide_type) + theirs.astype(wide_type)

    sent = [
        block(step, received[step - 1]).astype(low_type) for step in range(1, outer)
    ]
    arrived = tuple(
        lax.ppermute(part, "dp", outer_route(step + 1, inner, outer))
        for step, part in enumerate(sent)
    )
    return block(0, received[-1]), arrived, sent[-1]


def scatter_sum(total, arrived, *earlier):
    if earlier:
        arrived = lax.optimization_barrier(tuple(arrived) + earlier)[: len(arrived)]
    for part in arrived:
        total = total + part.astype(wide_type)
    return total


def layer(
    layer_input,
    segments,
    query_weight,
    key_matrix,
    value_matrix,
    gate_weight,
    out_weight,
    ffn_gate_weight,
    ffn_up_weight,
    ffn_down_weight,
    attn_gain,
    ffn_gain,
    query_gain,
    key_norm_gain,
    cotangent,
):
    tensor_rank, tensor_size = lax.axis_index("tensor"), lax.axis_size("tensor")
    data_rank, data_size = lax.axis_index("dp"), lax.axis_size("dp")
    inner = 2
    outer = data_size // inner
    seqs, token_length, width = layer_input.shape
    tokens = seqs * token_length
    head_size = query_gain.shape[0]
    cols_q, cols_k, cols_v = query_weight.shape[1], key_matrix.shape[1], value_matrix.shape[1]
    heads_q, heads_kv = cols_q // head_size, cols_k // head_size
    group_width = heads_q // heads_kv

    ring = (data_rank, inner, outer)
    sizes = (inner, outer)
    shard_in = jnp.concatenate([query_weight, key_matrix, value_matrix, gate_weight], axis=1)
    z_in, w_in = line_send(shard_in, *sizes)
    z_o, w_o = line_send(out_weight, *sizes)
    z_gf, w_gf = line_send(ffn_gate_weight, *sizes)
    z_up, w_up = line_send(ffn_up_weight, *sizes)
    z_dn, w_dn = line_send(ffn_down_weight, *sizes)

    flat_input = layer_input.reshape(tokens, width)
    grad_low = cotangent.reshape(tokens, width)
    first_row = share_start(tensor_rank, tensor_size, tokens)
    share_rows = tokens // tensor_size
    share_input = lax.dynamic_slice_in_dim(flat_input, first_row, share_rows, 0).astype(wide_type)
    share_cotangent = lax.dynamic_slice_in_dim(grad_low, first_row, share_rows, 0).astype(
        wide_type
    )

    cosine_table, sine_table = jax.vmap(lambda row: tables(row, head_size))(segments)
    first_normed = (norm_fwd(flat_input.astype(wide_type))[0] * attn_gain).astype(low_type)
    x_in = pair_send(z_in, *sizes)
    x_o = pair_send(z_o, *sizes)
    full_in = join_rows(in_order(shard_in, z_in, w_in, x_in, *ring))
    projected = matmul(first_normed, full_in)
    x_gf = pair_send(after(tuple(z_gf), projected), *sizes)
    attend, attend_back = attention_calls(seqs, token_length, head_size, group_width, heads_kv)
    attend_args = (
        projected,
        projected,
        projected,
        projected,
        cosine_table.reshape(tokens, head_size),
        sine_table.reshape(tokens, head_size),
        segments[:, :, None],
        segments[:, None, :],
        query_gain[None],
        key_norm_gain[None],
    )
    gated = attend(*attend_args)
    full_o = join_columns(
        in_order(
            out_weight, after(tuple(z_o), projected), w_o, after(tuple(x_o), projected), *ring
        )
    )
    x_up = pair_send(after(tuple(z_up), gated), *sizes)
    branch_one = tensor_scatter(
        lambda rows: matmul(rows, full_o), (gated,), tensor_rank, tensor_size
    )
    middle = share_input + branch_one
    normal_two, inv_two = norm_fwd(middle)
    second_normed = tensor_gather(
        (normal_two * ffn_gain).astype(low_type), tensor_rank, tensor_size
    )
    x_dn = pair_send(after(tuple(z_dn), second_normed), *sizes)
    full_gf = join_rows(in_order(ffn_gate_weight, z_gf, w_gf, after(tuple(x_gf), second_normed), *ring))
    ffn_gate = matmul(second_normed, full_gf)
    full_up = join_rows(in_order(ffn_up_weight, z_up, w_up, after(tuple(x_up), ffn_gate), *ring))
    ffn_up = matmul(second_normed, full_up)
    sig_gate = jax.nn.sigmoid(ffn_gate)
    active = ffn_gate * sig_gate
    hidden = (active * ffn_up).astype(low_type)
    weight_dn = matmul_tn(grad_low, hidden).astype(low_type)
    blocks_dn, pair_dn = scatter_send(weight_dn, *ring)
    full_dn = join_columns(
        in_order(ffn_down_weight, z_dn, w_dn, after(tuple(x_dn), weight_dn), *ring)
    )
    grad_hidden = matmul_nt(grad_low, full_dn)
    grad_ffn_gate = (grad_hidden * ffn_up * sig_gate * (1.0 + ffn_gate * (1.0 - sig_gate))).astype(
        low_type
    )
    grad_ffn_up = (grad_hidden * active).astype(low_type)
    weight_gf = matmul_tn(second_normed, grad_ffn_gate).astype(low_type)
    weight_up = matmul_tn(second_normed, grad_ffn_up).astype(low_type)
    blocks_gf, pair_gf = scatter_send(weight_gf, *ring)
    blocks_up, pair_up = scatter_send(weight_up, *ring)
    grad_second = tensor_scatter(
        lambda gate_rows, up_rows: matmul_nt(gate_rows, full_gf) + matmul_nt(up_rows, full_up),
        (grad_ffn_gate, grad_ffn_up),
        tensor_rank,
        tensor_size,
        (weight_gf,),
    )
    back_two, grad_ffn_gain = norm_back(normal_two, inv_two, ffn_gain, grad_second)
    grad_middle = share_cotangent + back_two
    share_low = grad_middle.astype(low_type)
    mine_dn, line_sum_dn, _ = scatter_line(blocks_dn, after(pair_dn, share_low), *ring)
    middle_low = tensor_gather(share_low, tensor_rank, tensor_size, (weight_up, mine_dn))

    grad_gated = matmul_nt(middle_low, full_o).astype(low_type)
    weight_o = matmul_tn(middle_low, gated).astype(low_type)
    blocks_o, pair_o = scatter_send(weight_o, *ring)
    grad_query, grad_key, grad_value, grad_gate_proj, head_gains = attend_back(
        *attend_args, grad_gated
    )
    head_gains = jnp.sum(head_gains, axis=(0, 1))
    grad_qk = jnp.concatenate([grad_query, grad_key], axis=1)
    grad_vg = jnp.concatenate([grad_value, grad_gate_proj], axis=1)
    mine_gf, line_sum_gf, _ = scatter_line(blocks_gf, after(pair_gf, grad_query), *ring)
    weight_vg = matmul_tn(first_normed, grad_vg).astype(low_type)
    weight_qk = matmul_tn(first_normed, grad_qk).astype(low_type)
    blocks_vg, pair_vg = scatter_send(weight_vg, *ring)
    blocks_qk, pair_qk = scatter_send(weight_qk, *ring)
    grad_first = tensor_scatter(
        lambda qk_rows, vg_rows: matmul_nt(qk_rows, full_in[:, : cols_q + cols_k])
        + matmul_nt(vg_rows, full_in[:, cols_q + cols_k :]),
        (grad_qk, grad_vg),
        tensor_rank,
        tensor_size,
        (weight_vg, weight_qk),
    )
    branch_two = tensor_scatter(
        lambda rows: matmul(rows, full_dn),
        (after(hidden, weight_vg, weight_qk),),
        tensor_rank,
        tensor_size,
    )
    result = tensor_gather((middle + branch_two).astype(low_type), tensor_rank, tensor_size)
    mine_up, line_sum_up, sent_up = scatter_line(blocks_up, after(pair_up, grad_first), *ring)
    mine_o, line_sum_o, sent_o = scatter_line(blocks_o, after(pair_o, sent_up), *ring)
    mine_vg, line_sum_vg, sent_vg = scatter_line(blocks_vg, after(pair_vg, sent_o), *ring)
    mine_qk, line_sum_qk, _ = scatter_line(blocks_qk, after(pair_qk, sent_vg), *ring)
    grad_dn = turned(scatter_sum(mine_dn, line_sum_dn, mine_up))
    grad_gf = scatter_sum(mine_gf, line_sum_gf, mine_up)
    grad_up = scatter_sum(mine_up, line_sum_up, mine_vg)
    grad_o = turned(scatter_sum(mine_o, line_sum_o, mine_qk))
    grads_vg = scatter_sum(mine_vg, line_sum_vg, mine_qk)
    normal_one, inv_one = norm_fwd(share_input)
    back_one, grad_attn_gain = norm_back(normal_one, inv_one, attn_gain, grad_first)
    grad_input = tensor_gather(
        (grad_middle + back_one).astype(low_type), tensor_rank, tensor_size
    ).astype(wide_type)

    grads_qk = scatter_sum(
        mine_qk, line_sum_qk, grad_input, result, grad_dn, grad_gf, grad_up, grad_o, grads_vg
    )

    gains = jnp.concatenate([grad_attn_gain, grad_ffn_gain, head_gains[0], head_gains[1]])
    for axis_name, size in (("tensor", tensor_size), ("dp", data_size)):
        bit = 1
        while bit < size:
            received = lax.ppermute(gains, axis_name, swap_pairs(size, bit))
            if axis_name == "dp" and bit > 1:
                received = after(received, grad_dn, grad_gf, grad_up, grad_o, grads_vg)
            gains = gains + received
            bit = bit * 2
    return (
        result.reshape(seqs, token_length, width),
        grad_input.reshape(seqs, token_length, width),
        grads_qk[:, :cols_q],
        grads_qk[:, cols_q:],
        grads_vg[:, :cols_v],
        grads_vg[:, cols_v:],
        grad_o,
        grad_gf,
        grad_up,
        grad_dn,
        gains[:width],
        gains[width : 2 * width],
        gains[2 * width : 2 * width + head_size],
        gains[2 * width + head_size :],
    )


def solution(mesh):
    return jax.shard_map(
        layer,
        mesh=mesh,
        in_specs=(
            P("dp", None, None),
            P("dp", None),
            P("dp", "tensor"),
            P("dp", "tensor"),
            P("dp", "tensor"),
            P("dp", "tensor"),
            P("tensor", "dp"),
            P("dp", "tensor"),
            P("dp", "tensor"),
            P("tensor", "dp"),
            P(),
            P(),
            P(),
            P(),
            P("dp", None, None),
        ),
        out_specs=(
            P("dp", None, None),
            P("dp", None, None),
            P("dp", "tensor"),
            P("dp", "tensor"),
            P("dp", "tensor"),
            P("dp", "tensor"),
            P("tensor", "dp"),
            P("dp", "tensor"),
            P("dp", "tensor"),
            P("tensor", "dp"),
            P(),
            P(),
            P(),
            P(),
        ),
        check_vma=False,
    )
```

profile of v0, /device:TPU:0, one launch (start us, length us, event | category | flops | bytes accessed | tf_op | source)
XLA Modules:
  0.0 1164.8 jit_solution(4989023426886764446)
XLA Ops:
  0.6 4.1 collective-permute-start.8
  40.9 37.8 %collective-permute-done.1 = bf16[256,1536]{1,0:T(8,128)(2,1)S(1)} collective-permute-done((bf16[256,1536]{1,0:T(8,128)(2,1)}, bf16[256,1536]{1,0:T(8,128)(2,1)S(1)}, u32[]{:S(2)}, u32[]{:S(2)}) %collective-permute-start.1) | collective-permute-done | bytes 786464 | tf_op jit(solution)/shard_map/ppermute | solution.py:301
  80.3 17.1 %collective-permute-done.2 = bf16[256,1536]{1,0:T(8,128)(2,1)S(1)} collective-permute-done((bf16[256,1536]{1,0:T(8,128)(2,1)}, bf16[256,1536]{1,0:T(8,128)(2,1)S(1)}, u32[]{:S(2)}, u32[]{:S(2)}) %collective-permute-start.2) | collective-permute-done | bytes 786464 | tf_op jit(solution)/shard_map/ppermute | solution.py:301
  99.7 18.2 %collective-permute-done.5 = bf16[256,1536]{1,0:T(8,128)(2,1)S(1)} collective-permute-done((bf16[256,1536]{1,0:T(8,128)(2,1)S(1)}, bf16[256,1536]{1,0:T(8,128)(2,1)S(1)}, u32[]{:S(2)}, u32[]{:S(2)}) %collective-permute-start.5) | collective-permute-done | bytes 786464 | tf_op jit(solution)/shard_map/ppermute | solution.py:308
  121.6 15.7 %collective-permute-start.18 = (bf16[256,1536]{1,0:T(8,128)(2,1)}, bf16[256,1536]{1,0:T(8,128)(2,1)}, u32[]{:S(2)}, u32[]{:S(2)}) collective-permute-start(bf16[256,1536]{1,0:T(8,128)(2,1)} %param.22), channel_id=1, source_target_pairs={{0,8},{4,12},{8,16},{12,20},{16,24},{20,28},{24,0},{28,4},{1,9},{5... | collective-permute-start | bytes 2359304 | tf_op jit(solution)/shard_map/ppermute | solution.py:301
  145.1 8.5 fusion.105.q_ref.k_ref.v_ref.g_ref
  156.4 12.2 %collective-permute-start.25 = (bf16[256,1536]{1,0:T(8,128)(2,1)}, bf16[256,1536]{1,0:T(8,128)(2,1)}, u32[]{:S(2)}, u32[]{:S(2)}) collective-permute-start(bf16[256,1536]{1,0:T(8,128)(2,1)} %param.23), channel_id=1, source_target_pairs={{0,8},{4,12},{8,16},{12,20},{16,24},{20,28},{24,0},{28,4},{1,9},{5... | collective-permute-start | bytes 2359304 | tf_op jit(solution)/shard_map/ppermute | solution.py:301
  176.4 17.4 %shard_map.254 = bf16[1024,512]{1,0:T(8,128)(2,1)} custom-call(f32[1024,1536]{1,0:T(8,128)} %fusion.105.q_ref.k_ref.v_ref.g_ref, f32[1024,1536]{1,0:T(8,128)} %fusion.105.q_ref.k_ref.v_ref.g_ref, f32[1024,1536]{1,0:T(8,128)} %fusion.105.q_ref.k_ref.v_ref.g_ref, f32[1024,1536]{1,0:T(8,128)} %fusion.105.q_ref.k_ref.v_ref.g_ref, ...), custom_call_target="tpu_custom_call" | custom-call | tf_op jit(solution)/shard_map/pallas_call | solution.py:446
  209.0 30.1 %collective-permute-done.26 = bf16[256,1536]{1,0:T(8,128)(2,1)} collective-permute-done((bf16[256,1536]{1,0:T(8,128)(2,1)}, bf16[256,1536]{1,0:T(8,128)(2,1)}, u32[]{:S(2)}, u32[]{:S(2)}) %collective-permute-start.26) | collective-permute-done | bytes 786464 | tf_op jit(solution)/shard_map/ppermute | solution.py:301
  243.4 17.8 %collective-permute-start.20 = (bf16[256,1536]{1,0:T(8,128)(2,1)}, bf16[256,1536]{1,0:T(8,128)(2,1)S(1)}, u32[]{:S(2)}, u32[]{:S(2)}) collective-permute-start(bf16[256,1536]{1,0:T(8,128)(2,1)} %param.22), channel_id=1, source_target_pairs={{0,24},{4,28},{8,0},{12,4},{16,8},{20,12},{24,16},{28,20},{1,25},{... | collective-permute-start | bytes 2359304 | tf_op jit(solution)/shard_map/ppermute | solution.py:301
  269.7 19.6 %collective-permute-start.32 = (bf16[1536,256]{1,0:T(8,128)(2,1)S(1)}, bf16[1536,256]{1,0:T(8,128)(2,1)}, u32[]{:S(2)}, u32[]{:S(2)}) collective-permute-start(bf16[1536,256]{1,0:T(8,128)(2,1)S(1)} %copy-done.42), channel_id=1, source_target_pairs={{0,8},{4,12},{8,16},{12,20},{16,24},{20,28},{24,0},{28,4},{1,9},{5... | collective-permute-start | bytes 2359304 | tf_op jit(solution)/shard_map/ppermute | solution.py:301
  291.8 18.1 %collective-permute-start.34 = (bf16[1536,256]{1,0:T(8,128)(2,1)S(1)}, bf16[1536,256]{1,0:T(8,128)(2,1)S(1)}, u32[]{:S(2)}, u32[]{:S(2)}) collective-permute-start(bf16[1536,256]{1,0:T(8,128)(2,1)S(1)} %copy-done.42), channel_id=1, source_target_pairs={{0,24},{4,28},{8,0},{12,4},{16,8},{20,12},{24,16},{28,20},{1,25},{... | collective-permute-start | bytes 2359304 | tf_op jit(solution)/shard_map/ppermute | solution.py:301
  311.0 7.6 collective-permute-done.32
  319.8 9.3 collective-permute-done.33
  329.2 15.2 %collective-permute-done.34 = bf16[1536,256]{1,0:T(8,128)(2,1)S(1)} collective-permute-done((bf16[1536,256]{1,0:T(8,128)(2,1)S(1)}, bf16[1536,256]{1,0:T(8,128)(2,1)S(1)}, u32[]{:S(2)}, u32[]{:S(2)}) %collective-permute-start.34) | collective-permute-done | bytes 786464 | tf_op jit(solution)/shard_map/ppermute | solution.py:301
  354.2 46.6 %collective-permute-done.24 = bf16[256,1536]{1,0:T(8,128)(2,1)S(1)} collective-permute-done((bf16[256,1536]{1,0:T(8,128)(2,1)S(1)}, bf16[256,1536]{1,0:T(8,128)(2,1)S(1)}, u32[]{:S(2)}, u32[]{:S(2)}) %collective-permute-start.24) | collective-permute-done | bytes 786464 | tf_op jit(solution)/shard_map/ppermute | solution.py:308
  405.7 11.0 fusion.101
  416.7 34.8 %collective-permute-done.31 = bf16[256,1536]{1,0:T(8,128)(2,1)} collective-permute-done((bf16[256,1536]{1,0:T(8,128)(2,1)}, bf16[256,1536]{1,0:T(8,128)(2,1)}, u32[]{:S(2)}, u32[]{:S(2)}) %collective-permute-start.31) | collective-permute-done | bytes 786464 | tf_op jit(solution)/shard_map/ppermute | solution.py:308
  458.7 12.4 %multiply_convert_fusion.1 = (bf16[1024,1536]{1,0:T(8,128)(2,1)S(1)}, f32[1024,1536]{1,0:T(8,128)}) fusion(f32[1024,1536]{1,0:T(8,128)} %fusion.101, bf16[2048,1536]{1,0:T(8,128)(2,1)S(1)} %bitcast.367, bf16[512,2048]{1,0:T(8,128)(2,1)} %get-tuple-element.229, bf16[512,2048]{1,0:T(8,128)(2,1)S(1)} %copy-done.29), kind=kOutput, calls=%fused_computation.19 | convolution fusion | flops 6460276736 | bytes 26214400 | tf_op jit(solution)/shard_map/dot_general | solution.py:224
  472.7 8.7 fusion.3
  481.4 8.6 copy.36
  490.0 11.1 collective-permute-done.36
  513.7 17.0 %fusion.7 = (bf16[1024,1536]{1,0:T(8,128)(2,1)}, bf16[1024,1536]{1,0:T(8,128)(2,1)}) fusion(f32[1024,1536]{1,0:T(8,128)} %fusion.101, f32[1024,1536]{1,0:T(8,128)} %get-tuple-element.274, bf16[1536,2048]{1,0:T(8,128)(2,1)} %copy-done.66, bf16[1024,2048]{1,0:T(8,128)(2,1)} %bitcast.388), kind=kOutput, calls=%fused_computation.18 | convolution fusion | flops 6462898176 | bytes 29360128 | tf_op jit(solution)/shard_map/tf,df->td/dot_general | solution.py:228
  530.8 6.6 fusion.42
  537.3 6.9 add_convert_fusion.1
  550.1 5.0 fusion.45
  555.1 5.8 convolution_add_fusion.1
  564.0 9.4 convolution_convert_fusion.1
  573.4 14.6 %collective-permute-done.40 = bf16[256,2048]{1,0:T(8,128)(2,1)S(1)} collective-permute-done((bf16[256,2048]{1,0:T(8,128)(2,1)S(1)}, bf16[256,2048]{1,0:T(8,128)(2,1)S(1)}, u32[]{:S(2)}, u32[]{:S(2)}) %collective-permute-start.40) | collective-permute-done | bytes 1048608 | tf_op jit(solution)/shard_map/ppermute | solution.py:263
  592.8 9.1 convolution_convert_fusion
  601.9 14.9 %collective-permute-done.42 = bf16[256,1536]{1,0:T(8,128)(2,1)} collective-permute-done((bf16[256,1536]{1,0:T(8,128)(2,1)}, bf16[256,1536]{1,0:T(8,128)(2,1)}, u32[]{:S(2)}, u32[]{:S(2)}) %collective-permute-start.42) | collective-permute-done | bytes 786464 | tf_op jit(solution)/shard_map/ppermute | solution.py:348
  616.9 4.1 fusion.34
  636.4 22.8 %shard_map.255 = (bf16[1024,512]{1,0:T(8,128)(2,1)}, bf16[1024,256]{1,0:T(8,128)(2,1)}, bf16[1024,256]{1,0:T(8,128)(2,1)}, bf16[1024,512]{1,0:T(8,128)(2,1)}, f32[2,2,2,128]{3,2,1,0:T(2,128)}) custom-call(f32[1024,1536]{1,0:T(8,128)} %fusion.105.q_ref.k_ref.v_ref.g_ref, f32[1024,1536]{1,0:T(8,128)} %fusion.105.q_ref.k_ref.v_ref.g_ref, ...), custom_call_target="tpu_custom_call" | custom-call | tf_op jit(solution)/shard_map/pallas_call | solution.py:499
  669.3 5.7 convolution_convert_fusion.3
  675.1 5.5 convolution_convert_fusion.4
  680.6 4.6 convolution_convert_fusion.6
  698.7 4.2 fusion.28
  706.3 6.2 fusion.39
  718.7 22.3 %collective-permute-done.49 = bf16[256,2048]{1,0:T(8,128)(2,1)S(1)} collective-permute-done((bf16[256,2048]{1,0:T(8,128)(2,1)S(1)}, bf16[256,2048]{1,0:T(8,128)(2,1)S(1)}, u32[]{:S(2)}, u32[]{:S(2)}) %collective-permute-start.49) | collective-permute-done | bytes 1048608 | tf_op jit(solution)/shard_map/ppermute | solution.py:263
  744.1 6.8 collective-permute-done.76
  751.4 16.3 %collective-permute-done.55 = bf16[256,1536]{1,0:T(8,128)(2,1)} collective-permute-done((bf16[256,1536]{1,0:T(8,128)(2,1)S(1)}, bf16[256,1536]{1,0:T(8,128)(2,1)}, u32[]{:S(2)}, u32[]{:S(2)}) %collective-permute-start.55) | collective-permute-done | bytes 786464 | tf_op jit(solution)/shard_map/ppermute | solution.py:348
  767.9 4.2 fusion.26
  774.2 4.7 collective-permute-done.85
  779.4 5.1 collective-permute-done.83
  790.6 7.9 collective-permute-done.52
  799.0 7.9 collective-permute-done.90
  807.4 7.9 collective-permute-done.88
  815.8 7.9 collective-permute-done.53
  825.9 14.1 %collective-permute-done.94 = f32[4352]{0:T(1024)S(1)} collective-permute-done((f32[4352]{0:T(1024)S(1)}, f32[4352]{0:T(1024)S(1)}, u32[]{:S(2)}, u32[]{:S(2)}) %collective-permute-start.94) | collective-permute-done | bytes 17440 | tf_op jit(solution)/shard_map/ppermute | solution.py:548
  840.8 6.4 collective-permute-start.86
  850.6 6.6 collective-permute-done.81
  857.2 6.4 collective-permute-start.91
  865.7 10.2 collective-permute-start.77
  876.6 53.2 %collective-permute-done.91 = bf16[256,768]{1,0:T(8,128)(2,1)S(1)} collective-permute-done((bf16[256,768]{1,0:T(8,128)(2,1)S(1)}, bf16[256,768]{1,0:T(8,128)(2,1)S(1)}, u32[]{:S(2)}, u32[]{:S(2)}) %collective-permute-start.91) | collective-permute-done | bytes 393248 | tf_op jit(solution)/shard_map/ppermute | solution.py:366
  937.0 9.8 collective-permute-done.79
  946.8 10.5 collective-permute-start.65
  957.2 45.2 %collective-permute-start.63 = (bf16[256,1536]{1,0:T(8,128)(2,1)S(1)}, bf16[256,1536]{1,0:T(8,128)(2,1)S(1)}, u32[]{:S(2)}, u32[]{:S(2)}) collective-permute-start(bf16[256,1536]{1,0:T(8,128)(2,1)S(1)} %copy-done.38), channel_id=1, source_target_pairs={{0,8},{4,12},{8,16},{12,20},{16,24},{20,28},{24,0},{28,4},{1,9},{5... | collective-permute-start | bytes 2359304 | tf_op jit(solution)/shard_map/ppermute | solution.py:366
  1008.9 11.6 collective-permute-start.73
  1020.5 44.2 %collective-permute-done.65 = bf16[256,1536]{1,0:T(8,128)(2,1)S(1)} collective-permute-done((bf16[256,1536]{1,0:T(8,128)(2,1)S(1)}, bf16[256,1536]{1,0:T(8,128)(2,1)S(1)}, u32[]{:S(2)}, u32[]{:S(2)}) %collective-permute-start.65) | collective-permute-done | bytes 786464 | tf_op jit(solution)/shard_map/ppermute | solution.py:366
  1070.5 20.0 %collective-permute-start.96 = (f32[4352]{0:T(1024)}, f32[4352]{0:T(1024)}, u32[]{:S(2)}, u32[]{:S(2)}) collective-permute-start(f32[4352]{0:T(1024)} %add.614), channel_id=1, source_target_pairs={{0,8},{4,12},{8,0},{12,4},{16,24},{20,28},{24,16},{28,20},{1,9},{5... | collective-permute-start | bytes 52232 | tf_op jit(solution)/shard_map/ppermute | solution.py:548
  1090.5 15.1 %collective-permute-done.73 = bf16[256,1536]{1,0:T(8,128)(2,1)S(1)} collective-permute-done((bf16[256,1536]{1,0:T(8,128)(2,1)S(1)}, bf16[256,1536]{1,0:T(8,128)(2,1)S(1)}, u32[]{:S(2)}, u32[]{:S(2)}) %collective-permute-start.73) | collective-permute-done | bytes 786464 | tf_op jit(solution)/shard_map/ppermute | solution.py:366
  1111.3 4.8 shard_map.256
  1131.9 23.1 %collective-permute-done.59 = bf16[256,768]{1,0:T(8,128)(2,1)S(1)} collective-permute-done((bf16[256,768]{1,0:T(8,128)(2,1)}, bf16[256,768]{1,0:T(8,128)(2,1)S(1)}, u32[]{:S(2)}, u32[]{:S(2)}) %collective-permute-start.59) | collective-permute-done | bytes 393248 | tf_op jit(solution)/shard_map/ppermute | solution.py:366
  1160.1 4.5 convert.26
  (515 shorter events, 261.3 us)
Async XLA Ops:
  0.6 121.0 %collective-permute-start.8 = (bf16[512,256]{1,0:T(8,128)(2,1)}, bf16[512,256]{1,0:T(8,128)(2,1)}, u32[]{:S(2)}, u32[]{:S(2)}) collective-permute-start(bf16[512,256]{1,0:T(8,128)(2,1)} %param.21), channel_id=1, source_target_pairs={{0,16},{4,20},{8,24},{12,28},{16,0},{20,4},{24,8},{28,12},{1,17},{... | collective-permute-start | bytes 786440 | tf_op jit(solution)/shard_map/ppermute | solution.py:301
  4.8 132.5 %collective-permute-start.7 = (bf16[512,256]{1,0:T(8,128)(2,1)}, bf16[512,256]{1,0:T(8,128)(2,1)}, u32[]{:S(2)}, u32[]{:S(2)}) collective-permute-start(bf16[512,256]{1,0:T(8,128)(2,1)} %param.21), channel_id=1, source_target_pairs={{0,8},{4,12},{8,16},{12,20},{16,24},{20,28},{24,0},{28,4},{1,9},{5... | collective-permute-start | bytes 786440 | tf_op jit(solution)/shard_map/ppermute | solution.py:301
  32.7 106.1 %collective-permute-start.9 = (bf16[512,256]{1,0:T(8,128)(2,1)S(1)}, bf16[512,256]{1,0:T(8,128)(2,1)}, u32[]{:S(2)}, u32[]{:S(2)}) collective-permute-start(bf16[512,256]{1,0:T(8,128)(2,1)S(1)} %copy-done.62), channel_id=1, source_target_pairs={{0,24},{4,28},{8,0},{12,4},{16,8},{20,12},{24,16},{28,20},{1,25},{... | collective-permute-start | bytes 786440 | tf_op jit(solution)/shard_map/ppermute | solution.py:301
  37.6 41.2 %collective-permute-start.1 = (bf16[256,1536]{1,0:T(8,128)(2,1)}, bf16[256,1536]{1,0:T(8,128)(2,1)S(1)}, u32[]{:S(2)}, u32[]{:S(2)}) collective-permute-start(bf16[256,1536]{1,0:T(8,128)(2,1)} %constant_dynamic-update-slice_fusion), channel_id=1, source_target_pairs={{0,16},{4,20},{8,24},{12,28},{16,0},{20,4},{24,8},{28,12},{1,17},{... | collective-permute-start | bytes 2359304 | tf_op jit(solution)/shard_map/ppermute | solution.py:301
  39.1 58.4 %collective-permute-start.2 = (bf16[256,1536]{1,0:T(8,128)(2,1)}, bf16[256,1536]{1,0:T(8,128)(2,1)S(1)}, u32[]{:S(2)}, u32[]{:S(2)}) collective-permute-start(bf16[256,1536]{1,0:T(8,128)(2,1)} %constant_dynamic-update-slice_fusion), channel_id=1, source_target_pairs={{0,24},{4,28},{8,0},{12,4},{16,8},{20,12},{24,16},{28,20},{1,25},{... | collective-permute-start | bytes 2359304 | tf_op jit(solution)/shard_map/ppermute | solution.py:301
  99.1 40.3 %collective-permute-start.6 = (bf16[256,1536]{1,0:T(8,128)(2,1)S(1)}, bf16[256,1536]{1,0:T(8,128)(2,1)S(1)}, u32[]{:S(2)}, u32[]{:S(2)}) collective-permute-start(bf16[256,1536]{1,0:T(8,128)(2,1)S(1)} %collective-permute-done.2), channel_id=1, source_target_pairs={{0,4},{4,0},{8,12},{12,8},{16,20},{20,16},{24,28},{28,24},{1,5},{5... | collective-permute-start | bytes 2359304 | tf_op jit(solution)/shard_map/ppermute | solution.py:308
  117.9 151.8 %collective-permute-start.19 = (bf16[256,1536]{1,0:T(8,128)(2,1)}, bf16[256,1536]{1,0:T(8,128)(2,1)}, u32[]{:S(2)}, u32[]{:S(2)}) collective-permute-start(bf16[256,1536]{1,0:T(8,128)(2,1)} %param.22), channel_id=1, source_target_pairs={{0,16},{4,20},{8,24},{12,28},{16,0},{20,4},{24,8},{28,12},{1,17},{... | collective-permute-start | bytes 2359304 | tf_op jit(solution)/shard_map/ppermute | solution.py:301
  121.6 145.9 %collective-permute-start.18 = (bf16[256,1536]{1,0:T(8,128)(2,1)}, bf16[256,1536]{1,0:T(8,128)(2,1)}, u32[]{:S(2)}, u32[]{:S(2)}) collective-permute-start(bf16[256,1536]{1,0:T(8,128)(2,1)} %param.22), channel_id=1, source_target_pairs={{0,8},{4,12},{8,16},{12,20},{16,24},{20,28},{24,0},{28,4},{1,9},{5... | collective-permute-start | bytes 2359304 | tf_op jit(solution)/shard_map/ppermute | solution.py:301
  154.9 107.6 %collective-permute-start.21 = (bf16[256,1536]{1,0:T(8,128)(2,1)}, bf16[256,1536]{1,0:T(8,128)(2,1)}, u32[]{:S(2)}, u32[]{:S(2)}) collective-permute-start(bf16[256,1536]{1,0:T(8,128)(2,1)} %param.22), channel_id=1, source_target_pairs={{0,4},{4,0},{8,12},{12,8},{16,20},{20,16},{24,28},{28,24},{1,5},{5... | collective-permute-start | bytes 2359304 | tf_op jit(solution)/shard_map/ppermute | solution.py:304
  156.4 44.4 %collective-permute-start.25 = (bf16[256,1536]{1,0:T(8,128)(2,1)}, bf16[256,1536]{1,0:T(8,128)(2,1)}, u32[]{:S(2)}, u32[]{:S(2)}) collective-permute-start(bf16[256,1536]{1,0:T(8,128)(2,1)} %param.23), channel_id=1, source_target_pairs={{0,8},{4,12},{8,16},{12,20},{16,24},{20,28},{24,0},{28,4},{1,9},{5... | collective-permute-start | bytes 2359304 | tf_op jit(solution)/shard_map/ppermute | solution.py:301
  200.8 38.3 %collective-permute-start.26 = (bf16[256,1536]{1,0:T(8,128)(2,1)}, bf16[256,1536]{1,0:T(8,128)(2,1)}, u32[]{:S(2)}, u32[]{:S(2)}) collective-permute-start(bf16[256,1536]{1,0:T(8,128)(2,1)} %param.23), channel_id=1, source_target_pairs={{0,16},{4,20},{8,24},{12,28},{16,0},{20,4},{24,8},{28,12},{1,17},{... | collective-permute-start | bytes 2359304 | tf_op jit(solution)/shard_map/ppermute | solution.py:301
  206.6 36.8 %collective-permute-start.27 = (bf16[256,1536]{1,0:T(8,128)(2,1)}, bf16[256,1536]{1,0:T(8,128)(2,1)}, u32[]{:S(2)}, u32[]{:S(2)}) collective-permute-start(bf16[256,1536]{1,0:T(8,128)(2,1)} %param.23), channel_id=1, source_target_pairs={{0,24},{4,28},{8,0},{12,4},{16,8},{20,12},{24,16},{28,20},{1,25},{... | collective-permute-start | bytes 2359304 | tf_op jit(solution)/shard_map/ppermute | solution.py:301
  243.4 47.1 %collective-permute-start.20 = (bf16[256,1536]{1,0:T(8,128)(2,1)}, bf16[256,1536]{1,0:T(8,128)(2,1)S(1)}, u32[]{:S(2)}, u32[]{:S(2)}) collective-permute-start(bf16[256,1536]{1,0:T(8,128)(2,1)} %param.22), channel_id=1, source_target_pairs={{0,24},{4,28},{8,0},{12,4},{16,8},{20,12},{24,16},{28,20},{1,25},{... | collective-permute-start | bytes 2359304 | tf_op jit(solution)/shard_map/ppermute | solution.py:301
  262.5 83.6 %collective-permute-start.28 = (bf16[256,1536]{1,0:T(8,128)(2,1)}, bf16[256,1536]{1,0:T(8,128)(2,1)S(1)}, u32[]{:S(2)}, u32[]{:S(2)}) collective-permute-start(bf16[256,1536]{1,0:T(8,128)(2,1)} %param.23), channel_id=1, source_target_pairs={{0,4},{4,0},{8,12},{12,8},{16,20},{20,16},{24,28},{28,24},{1,5},{5... | collective-permute-start | bytes 2359304 | tf_op jit(solution)/shard_map/ppermute | solution.py:304
  264.7 64.4 %collective-permute-start.33 = (bf16[1536,256]{1,0:T(8,128)(2,1)S(1)}, bf16[1536,256]{1,0:T(8,128)(2,1)S(1)}, u32[]{:S(2)}, u32[]{:S(2)}) collective-permute-start(bf16[1536,256]{1,0:T(8,128)(2,1)S(1)} %copy-done.42), channel_id=1, source_target_pairs={{0,16},{4,20},{8,24},{12,28},{16,0},{20,4},{24,8},{28,12},{1,17},{... | collective-permute-start | bytes 2359304 | tf_op jit(solution)/shard_map/ppermute | solution.py:301
  269.7 48.9 %collective-permute-start.32 = (bf16[1536,256]{1,0:T(8,128)(2,1)S(1)}, bf16[1536,256]{1,0:T(8,128)(2,1)}, u32[]{:S(2)}, u32[]{:S(2)}) collective-permute-start(bf16[1536,256]{1,0:T(8,128)(2,1)S(1)} %copy-done.42), channel_id=1, source_target_pairs={{0,8},{4,12},{8,16},{12,20},{16,24},{20,28},{24,0},{28,4},{1,9},{5... | collective-permute-start | bytes 2359304 | tf_op jit(solution)/shard_map/ppermute | solution.py:301
  291.8 52.5 %collective-permute-start.34 = (bf16[1536,256]{1,0:T(8,128)(2,1)S(1)}, bf16[1536,256]{1,0:T(8,128)(2,1)S(1)}, u32[]{:S(2)}, u32[]{:S(2)}) collective-permute-start(bf16[1536,256]{1,0:T(8,128)(2,1)S(1)} %copy-done.42), channel_id=1, source_target_pairs={{0,24},{4,28},{8,0},{12,4},{16,8},{20,12},{24,16},{28,20},{1,25},{... | collective-permute-start | bytes 2359304 | tf_op jit(solution)/shard_map/ppermute | solution.py:301
  310.7 39.9 %collective-permute-start.17 = (bf16[512,2048]{1,0:T(8,128)(2,1)S(1)}, bf16[512,2048]{1,0:T(8,128)(2,1)S(1)}, u32[]{:S(2)}, u32[]{:S(2)}) collective-permute-start(bf16[512,2048]{1,0:T(8,128)(2,1)S(1)} %pad_maximum_fusion.9), channel_id=1, source_target_pairs={{0,1},{1,0},{2,3},{3,2},{4,5},{5,4},{6,7},{7,6},{8,9},{9,8},{10,11... | collective-permute-start | bytes 6291464 | tf_op jit(solution)/shard_map/ppermute | solution.py:281
  346.4 54.9 %collective-permute-start.22 = (bf16[256,1536]{1,0:T(8,128)(2,1)}, bf16[256,1536]{1,0:T(8,128)(2,1)S(1)}, u32[]{:S(2)}, u32[]{:S(2)}) collective-permute-start(bf16[256,1536]{1,0:T(8,128)(2,1)} %collective-permute-done.18), channel_id=1, source_target_pairs={{0,4},{4,0},{8,12},{12,8},{16,20},{20,16},{24,28},{28,24},{1,5},{5... | collective-permute-start | bytes 2359304 | tf_op jit(solution)/shard_map/ppermute | solution.py:308
  347.0 54.3 %collective-permute-start.23 = (bf16[256,1536]{1,0:T(8,128)(2,1)}, bf16[256,1536]{1,0:T(8,128)(2,1)S(1)}, u32[]{:S(2)}, u32[]{:S(2)}) collective-permute-start(bf16[256,1536]{1,0:T(8,128)(2,1)} %collective-permute-done.19), channel_id=1, source_target_pairs={{0,4},{4,0},{8,12},{12,8},{16,20},{20,16},{24,28},{28,24},{1,5},{5... | collective-permute-start | bytes 2359304 | tf_op jit(solution)/shard_map/ppermute | solution.py:308
  348.5 52.3 %collective-permute-start.24 = (bf16[256,1536]{1,0:T(8,128)(2,1)S(1)}, bf16[256,1536]{1,0:T(8,128)(2,1)S(1)}, u32[]{:S(2)}, u32[]{:S(2)}) collective-permute-start(bf16[256,1536]{1,0:T(8,128)(2,1)S(1)} %collective-permute-done.20), channel_id=1, source_target_pairs={{0,4},{4,0},{8,12},{12,8},{16,20},{20,16},{24,28},{28,24},{1,5},{5... | collective-permute-start | bytes 2359304 | tf_op jit(solution)/shard_map/ppermute | solution.py:308
  349.0 103.0 %collective-permute-start.29 = (bf16[256,1536]{1,0:T(8,128)(2,1)}, bf16[256,1536]{1,0:T(8,128)(2,1)}, u32[]{:S(2)}, u32[]{:S(2)}) collective-permute-start(bf16[256,1536]{1,0:T(8,128)(2,1)} %collective-permute-done.25), channel_id=1, source_target_pairs={{0,4},{4,0},{8,12},{12,8},{16,20},{20,16},{24,28},{28,24},{1,5},{5... | collective-permute-start | bytes 2359304 | tf_op jit(solution)/shard_map/ppermute | solution.py:308
  350.5 101.5 %collective-permute-start.30 = (bf16[256,1536]{1,0:T(8,128)(2,1)}, bf16[256,1536]{1,0:T(8,128)(2,1)}, u32[]{:S(2)}, u32[]{:S(2)}) collective-permute-start(bf16[256,1536]{1,0:T(8,128)(2,1)} %collective-permute-done.26), channel_id=1, source_target_pairs={{0,4},{4,0},{8,12},{12,8},{16,20},{20,16},{24,28},{28,24},{1,5},{5... | collective-permute-start | bytes 2359304 | tf_op jit(solution)/shard_map/ppermute | solution.py:308
  400.8 50.7 %collective-permute-start.31 = (bf16[256,1536]{1,0:T(8,128)(2,1)}, bf16[256,1536]{1,0:T(8,128)(2,1)}, u32[]{:S(2)}, u32[]{:S(2)}) collective-permute-start(bf16[256,1536]{1,0:T(8,128)(2,1)} %collective-permute-done.27), channel_id=1, source_target_pairs={{0,4},{4,0},{8,12},{12,8},{16,20},{20,16},{24,28},{28,24},{1,5},{5... | collective-permute-start | bytes 2359304 | tf_op jit(solution)/shard_map/ppermute | solution.py:308
  403.7 86.3 %collective-permute-start.37 = (bf16[1536,256]{1,0:T(8,128)(2,1)S(1)}, bf16[1536,256]{1,0:T(8,128)(2,1)}, u32[]{:S(2)}, u32[]{:S(2)}) collective-permute-start(bf16[1536,256]{1,0:T(8,128)(2,1)S(1)} %copy-done.44), channel_id=1, source_target_pairs={{0,4},{4,0},{8,12},{12,8},{16,20},{20,16},{24,28},{28,24},{1,5},{5... | collective-permute-start | bytes 2359304 | tf_op jit(solution)/shard_map/ppermute | solution.py:308
  405.2 84.8 %collective-permute-start.38 = (bf16[1536,256]{1,0:T(8,128)(2,1)}, bf16[1536,256]{1,0:T(8,128)(2,1)}, u32[]{:S(2)}, u32[]{:S(2)}) collective-permute-start(bf16[1536,256]{1,0:T(8,128)(2,1)} %copy-done.45), channel_id=1, source_target_pairs={{0,4},{4,0},{8,12},{12,8},{16,20},{20,16},{24,28},{28,24},{1,5},{5... | collective-permute-start | bytes 2359304 | tf_op jit(solution)/shard_map/ppermute | solution.py:308
  451.5 49.6 %collective-permute-start.36 = (bf16[1536,256]{1,0:T(8,128)(2,1)}, bf16[1536,256]{1,0:T(8,128)(2,1)}, u32[]{:S(2)}, u32[]{:S(2)}) collective-permute-start(bf16[1536,256]{1,0:T(8,128)(2,1)} %collective-permute-done.32), channel_id=1, source_target_pairs={{0,4},{4,0},{8,12},{12,8},{16,20},{20,16},{24,28},{28,24},{1,5},{5... | collective-permute-start | bytes 2359304 | tf_op jit(solution)/shard_map/ppermute | solution.py:308
  546.0 55.9 %collective-permute-start.66 = (bf16[256,1536]{1,0:T(8,128)(2,1)}, bf16[256,1536]{1,0:T(8,128)(2,1)S(1)}, u32[]{:S(2)}, u32[]{:S(2)}) collective-permute-start(bf16[256,1536]{1,0:T(8,128)(2,1)} %get-tuple-element.209), channel_id=1, source_target_pairs={{0,4},{4,0},{8,12},{12,8},{16,20},{20,16},{24,28},{28,24},{1,5},{5... | collective-permute-start | bytes 2359304 | tf_op jit(solution)/shard_map/ppermute | solution.py:348
  546.6 55.4 %collective-permute-start.64 = (bf16[256,1536]{1,0:T(8,128)(2,1)}, bf16[256,1536]{1,0:T(8,128)(2,1)}, u32[]{:S(2)}, u32[]{:S(2)}) collective-permute-start(bf16[256,1536]{1,0:T(8,128)(2,1)} %get-tuple-element.210), channel_id=1, source_target_pairs={{0,4},{4,0},{8,12},{12,8},{16,20},{20,16},{24,28},{28,24},{1,5},{5... | collective-permute-start | bytes 2359304 | tf_op jit(solution)/shard_map/ppermute | solution.py:348
  548.1 53.9 %collective-permute-start.62 = (bf16[256,1536]{1,0:T(8,128)(2,1)}, bf16[256,1536]{1,0:T(8,128)(2,1)}, u32[]{:S(2)}, u32[]{:S(2)}) collective-permute-start(bf16[256,1536]{1,0:T(8,128)(2,1)} %get-tuple-element.211), channel_id=1, source_target_pairs={{0,4},{4,0},{8,12},{12,8},{16,20},{20,16},{24,28},{28,24},{1,5},{5... | collective-permute-start | bytes 2359304 | tf_op jit(solution)/shard_map/ppermute | solution.py:348
  548.6 68.3 %collective-permute-start.42 = (bf16[256,1536]{1,0:T(8,128)(2,1)}, bf16[256,1536]{1,0:T(8,128)(2,1)}, u32[]{:S(2)}, u32[]{:S(2)}) collective-permute-start(bf16[256,1536]{1,0:T(8,128)(2,1)} %get-tuple-element.212), channel_id=1, source_target_pairs={{0,4},{4,0},{8,12},{12,8},{16,20},{20,16},{24,28},{28,24},{1,5},{5... | collective-permute-start | bytes 2359304 | tf_op jit(solution)/shard_map/ppermute | solution.py:348
  624.2 79.8 %collective-permute-start.69 = (bf16[256,1536]{1,0:T(8,128)(2,1)}, bf16[256,1536]{1,0:T(8,128)(2,1)}, u32[]{:S(2)}, u32[]{:S(2)}) collective-permute-start(bf16[256,1536]{1,0:T(8,128)(2,1)} %get-tuple-element.191), channel_id=1, source_target_pairs={{0,4},{4,0},{8,12},{12,8},{16,20},{20,16},{24,28},{28,24},{1,5},{5... | collective-permute-start | bytes 2359304 | tf_op jit(solution)/shard_map/ppermute | solution.py:348
  624.7 71.9 %collective-permute-start.74 = (bf16[256,1536]{1,0:T(8,128)(2,1)}, bf16[256,1536]{1,0:T(8,128)(2,1)}, u32[]{:S(2)}, u32[]{:S(2)}) collective-permute-start(bf16[256,1536]{1,0:T(8,128)(2,1)} %get-tuple-element.192), channel_id=1, source_target_pairs={{0,4},{4,0},{8,12},{12,8},{16,20},{20,16},{24,28},{28,24},{1,5},{5... | collective-permute-start | bytes 2359304 | tf_op jit(solution)/shard_map/ppermute | solution.py:348
  626.2 70.9 %collective-permute-start.72 = (bf16[256,1536]{1,0:T(8,128)(2,1)}, bf16[256,1536]{1,0:T(8,128)(2,1)}, u32[]{:S(2)}, u32[]{:S(2)}) collective-permute-start(bf16[256,1536]{1,0:T(8,128)(2,1)} %get-tuple-element.193), channel_id=1, source_target_pairs={{0,4},{4,0},{8,12},{12,8},{16,20},{20,16},{24,28},{28,24},{1,5},{5... | collective-permute-start | bytes 2359304 | tf_op jit(solution)/shard_map/ppermute | solution.py:348
  626.7 71.9 %collective-permute-start.70 = (bf16[256,1536]{1,0:T(8,128)(2,1)}, bf16[256,1536]{1,0:T(8,128)(2,1)}, u32[]{:S(2)}, u32[]{:S(2)}) collective-permute-start(bf16[256,1536]{1,0:T(8,128)(2,1)} %get-tuple-element.194), channel_id=1, source_target_pairs={{0,4},{4,0},{8,12},{12,8},{16,20},{20,16},{24,28},{28,24},{1,5},{5... | collective-permute-start | bytes 2359304 | tf_op jit(solution)/shard_map/ppermute | solution.py:348
  696.6 75.5 %collective-permute-start.68 = (bf16[256,1536]{1,0:T(8,128)(2,1)S(1)}, bf16[256,1536]{1,0:T(8,128)(2,1)S(1)}, u32[]{:S(2)}, u32[]{:S(2)}) collective-permute-start(bf16[256,1536]{1,0:T(8,128)(2,1)S(1)} %get-tuple-element.198), channel_id=1, source_target_pairs={{0,4},{4,0},{8,12},{12,8},{16,20},{20,16},{24,28},{28,24},{1,5},{5... | collective-permute-start | bytes 2359304 | tf_op jit(solution)/shard_map/ppermute | solution.py:348
  697.1 45.4 %collective-permute-start.78 = (bf16[256,1536]{1,0:T(8,128)(2,1)}, bf16[256,1536]{1,0:T(8,128)(2,1)}, u32[]{:S(2)}, u32[]{:S(2)}) collective-permute-start(bf16[256,1536]{1,0:T(8,128)(2,1)} %get-tuple-element.199), channel_id=1, source_target_pairs={{0,4},{4,0},{8,12},{12,8},{16,20},{20,16},{24,28},{28,24},{1,5},{5... | collective-permute-start | bytes 2359304 | tf_op jit(solution)/shard_map/ppermute | solution.py:348
  704.0 46.8 %collective-permute-start.76 = (bf16[256,1536]{1,0:T(8,128)(2,1)S(1)}, bf16[256,1536]{1,0:T(8,128)(2,1)}, u32[]{:S(2)}, u32[]{:S(2)}) collective-permute-start(bf16[256,1536]{1,0:T(8,128)(2,1)S(1)} %copy-done.41), channel_id=1, source_target_pairs={{0,4},{4,0},{8,12},{12,8},{16,20},{20,16},{24,28},{28,24},{1,5},{5... | collective-permute-start | bytes 2359304 | tf_op jit(solution)/shard_map/ppermute | solution.py:348
  716.8 50.9 %collective-permute-start.55 = (bf16[256,1536]{1,0:T(8,128)(2,1)S(1)}, bf16[256,1536]{1,0:T(8,128)(2,1)}, u32[]{:S(2)}, u32[]{:S(2)}) collective-permute-start(bf16[256,1536]{1,0:T(8,128)(2,1)S(1)} %copy-done.40), channel_id=1, source_target_pairs={{0,4},{4,0},{8,12},{12,8},{16,20},{20,16},{24,28},{28,24},{1,5},{5... | collective-permute-start | bytes 2359304 | tf_op jit(solution)/shard_map/ppermute | solution.py:348
  742.5 36.3 %collective-permute-start.85 = (bf16[256,512]{1,0:T(8,128)(2,1)S(1)}, bf16[256,512]{1,0:T(8,128)(2,1)S(1)}, u32[]{:S(2)}, u32[]{:S(2)}) collective-permute-start(bf16[256,512]{1,0:T(8,128)(2,1)S(1)} %copy-done.64), channel_id=1, source_target_pairs={{0,4},{4,0},{8,12},{12,8},{16,20},{20,16},{24,28},{28,24},{1,5},{5... | collective-permute-start | bytes 786440 | tf_op jit(solution)/shard_map/ppermute | solution.py:348
  750.8 33.6 %collective-permute-start.83 = (bf16[256,512]{1,0:T(8,128)(2,1)S(1)}, bf16[256,512]{1,0:T(8,128)(2,1)S(1)}, u32[]{:S(2)}, u32[]{:S(2)}) collective-permute-start(bf16[256,512]{1,0:T(8,128)(2,1)S(1)} %copy-done.63), channel_id=1, source_target_pairs={{0,4},{4,0},{8,12},{12,8},{16,20},{20,16},{24,28},{28,24},{1,5},{5... | collective-permute-start | bytes 786440 | tf_op jit(solution)/shard_map/ppermute | solution.py:348
  785.0 38.8 %collective-permute-start.53 = (bf16[256,768]{1,0:T(8,128)(2,1)S(1)}, bf16[256,768]{1,0:T(8,128)(2,1)S(1)}, u32[]{:S(2)}, u32[]{:S(2)}) collective-permute-start(bf16[256,768]{1,0:T(8,128)(2,1)S(1)} %copy-done.53), channel_id=1, source_target_pairs={{0,4},{4,0},{8,12},{12,8},{16,20},{20,16},{24,28},{28,24},{1,5},{5... | collective-permute-start | bytes 1179656 | tf_op jit(solution)/shard_map/ppermute | solution.py:348
  790.1 50.8 %collective-permute-start.60 = (bf16[256,768]{1,0:T(8,128)(2,1)S(1)}, bf16[256,768]{1,0:T(8,128)(2,1)S(1)}, u32[]{:S(2)}, u32[]{:S(2)}) collective-permute-start(bf16[256,768]{1,0:T(8,128)(2,1)S(1)} %copy-done.52), channel_id=1, source_target_pairs={{0,4},{4,0},{8,12},{12,8},{16,20},{20,16},{24,28},{28,24},{1,5},{5... | collective-permute-start | bytes 1179656 | tf_op jit(solution)/shard_map/ppermute | solution.py:348
  798.5 48.8 %collective-permute-start.58 = (bf16[256,768]{1,0:T(8,128)(2,1)S(1)}, bf16[256,768]{1,0:T(8,128)(2,1)S(1)}, u32[]{:S(2)}, u32[]{:S(2)}) collective-permute-start(bf16[256,768]{1,0:T(8,128)(2,1)S(1)} %copy-done.51), channel_id=1, source_target_pairs={{0,4},{4,0},{8,12},{12,8},{16,20},{20,16},{24,28},{28,24},{1,5},{5... | collective-permute-start | bytes 1179656 | tf_op jit(solution)/shard_map/ppermute | solution.py:348
  806.9 42.1 %collective-permute-start.56 = (bf16[256,768]{1,0:T(8,128)(2,1)S(1)}, bf16[256,768]{1,0:T(8,128)(2,1)S(1)}, u32[]{:S(2)}, u32[]{:S(2)}) collective-permute-start(bf16[256,768]{1,0:T(8,128)(2,1)S(1)} %copy-done.50), channel_id=1, source_target_pairs={{0,4},{4,0},{8,12},{12,8},{16,20},{20,16},{24,28},{28,24},{1,5},{5... | collective-permute-start | bytes 1179656 | tf_op jit(solution)/shard_map/ppermute | solution.py:348
  815.3 41.9 %collective-permute-start.45 = (bf16[256,2048]{1,0:T(8,128)(2,1)S(1)}, bf16[256,2048]{1,0:T(8,128)(2,1)S(1)}, u32[]{:S(2)}, u32[]{:S(2)}) collective-permute-start(bf16[256,2048]{1,0:T(8,128)(2,1)S(1)} %dynamic-slice_convert_fusion.1), channel_id=1, source_target_pairs={{0,2},{1,3},{2,0},{3,1},{4,6},{5,7},{6,4},{7,5},{8,10},{9,11},{10,... | collective-permute-start | bytes 3145736 | tf_op jit(solution)/shard_map/ppermute | solution.py:263
  857.2 72.6 %collective-permute-start.91 = (bf16[256,768]{1,0:T(8,128)(2,1)S(1)}, bf16[256,768]{1,0:T(8,128)(2,1)S(1)}, u32[]{:S(2)}, u32[]{:S(2)}) collective-permute-start(bf16[256,768]{1,0:T(8,128)(2,1)S(1)} %get-tuple-element.242), channel_id=1, source_target_pairs={{0,16},{4,20},{8,24},{12,28},{16,0},{20,4},{24,8},{28,12},{1,17},{... | collective-permute-start | bytes 1179656 | tf_op jit(solution)/shard_map/ppermute | solution.py:366
  863.7 68.2 %collective-permute-start.89 = (bf16[256,768]{1,0:T(8,128)(2,1)S(1)}, bf16[256,768]{1,0:T(8,128)(2,1)S(1)}, u32[]{:S(2)}, u32[]{:S(2)}) collective-permute-start(bf16[256,768]{1,0:T(8,128)(2,1)S(1)} %get-tuple-element.243), channel_id=1, source_target_pairs={{0,8},{4,12},{8,16},{12,20},{16,24},{20,28},{24,0},{28,4},{1,9},{5... | collective-permute-start | bytes 1179656 | tf_op jit(solution)/shard_map/ppermute | solution.py:366
  865.6 81.1 %collective-permute-start.79 = (bf16[256,1536]{1,0:T(8,128)(2,1)}, bf16[256,1536]{1,0:T(8,128)(2,1)}, u32[]{:S(2)}, u32[]{:S(2)}) collective-permute-start(bf16[256,1536]{1,0:T(8,128)(2,1)} %get-tuple-element.202), channel_id=1, source_target_pairs={{0,16},{4,20},{8,24},{12,28},{16,0},{20,4},{24,8},{28,12},{1,17},{... | collective-permute-start | bytes 2359304 | tf_op jit(solution)/shard_map/ppermute | solution.py:366
  865.7 91.5 %collective-permute-start.77 = (bf16[256,1536]{1,0:T(8,128)(2,1)}, bf16[256,1536]{1,0:T(8,128)(2,1)}, u32[]{:S(2)}, u32[]{:S(2)}) collective-permute-start(bf16[256,1536]{1,0:T(8,128)(2,1)} %get-tuple-element.203), channel_id=1, source_target_pairs={{0,8},{4,12},{8,16},{12,20},{16,24},{20,28},{24,0},{28,4},{1,9},{5... | collective-permute-start | bytes 2359304 | tf_op jit(solution)/shard_map/ppermute | solution.py:366
  876.5 59.5 %collective-permute-start.92 = (bf16[256,768]{1,0:T(8,128)(2,1)}, bf16[256,768]{1,0:T(8,128)(2,1)}, u32[]{:S(2)}, u32[]{:S(2)}) collective-permute-start(bf16[256,768]{1,0:T(8,128)(2,1)} %get-tuple-element.244), channel_id=1, source_target_pairs={{0,24},{4,28},{8,0},{12,4},{16,8},{20,12},{24,16},{28,20},{1,25},{... | collective-permute-start | bytes 1179656 | tf_op jit(solution)/shard_map/ppermute | solution.py:366
  929.8 75.2 %collective-permute-start.80 = (bf16[256,1536]{1,0:T(8,128)(2,1)}, bf16[256,1536]{1,0:T(8,128)(2,1)}, u32[]{:S(2)}, u32[]{:S(2)}) collective-permute-start(bf16[256,1536]{1,0:T(8,128)(2,1)} %get-tuple-element.204), channel_id=1, source_target_pairs={{0,24},{4,28},{8,0},{12,4},{16,8},{20,12},{24,16},{28,20},{1,25},{... | collective-permute-start | bytes 2359304 | tf_op jit(solution)/shard_map/ppermute | solution.py:366
  932.6 132.8 %collective-permute-start.46 = (bf16[256,2048]{1,0:T(8,128)(2,1)S(1)}, bf16[256,2048]{1,0:T(8,128)(2,1)}, u32[]{:S(2)}, u32[]{:S(2)}) collective-permute-start(bf16[256,2048]{1,0:T(8,128)(2,1)S(1)} %add_convert_fusion.2), channel_id=1, source_target_pairs={{0,2},{1,3},{2,0},{3,1},{4,6},{5,7},{6,4},{7,5},{8,10},{9,11},{10,... | collective-permute-start | bytes 3145736 | tf_op jit(solution)/shard_map/ppermute | solution.py:281
  936.0 72.9 %collective-permute-start.67 = (bf16[256,1536]{1,0:T(8,128)(2,1)}, bf16[256,1536]{1,0:T(8,128)(2,1)S(1)}, u32[]{:S(2)}, u32[]{:S(2)}) collective-permute-start(bf16[256,1536]{1,0:T(8,128)(2,1)} %get-tuple-element.205), channel_id=1, source_target_pairs={{0,24},{4,28},{8,0},{12,4},{16,8},{20,12},{24,16},{28,20},{1,25},{... | collective-permute-start | bytes 2359304 | tf_op jit(solution)/shard_map/ppermute | solution.py:366
  946.8 117.9 %collective-permute-start.65 = (bf16[256,1536]{1,0:T(8,128)(2,1)S(1)}, bf16[256,1536]{1,0:T(8,128)(2,1)S(1)}, u32[]{:S(2)}, u32[]{:S(2)}) collective-permute-start(bf16[256,1536]{1,0:T(8,128)(2,1)S(1)} %copy-done.39), channel_id=1, source_target_pairs={{0,16},{4,20},{8,24},{12,28},{16,0},{20,4},{24,8},{28,12},{1,17},{... | collective-permute-start | bytes 2359304 | tf_op jit(solution)/shard_map/ppermute | solution.py:366
  957.2 107.6 %collective-permute-start.63 = (bf16[256,1536]{1,0:T(8,128)(2,1)S(1)}, bf16[256,1536]{1,0:T(8,128)(2,1)S(1)}, u32[]{:S(2)}, u32[]{:S(2)}) collective-permute-start(bf16[256,1536]{1,0:T(8,128)(2,1)S(1)} %copy-done.38), channel_id=1, source_target_pairs={{0,8},{4,12},{8,16},{12,20},{16,24},{20,28},{24,0},{28,4},{1,9},{5... | collective-permute-start | bytes 2359304 | tf_op jit(solution)/shard_map/ppermute | solution.py:366
  1005.0 65.5 %collective-permute-start.75 = (bf16[256,1536]{1,0:T(8,128)(2,1)}, bf16[256,1536]{1,0:T(8,128)(2,1)S(1)}, u32[]{:S(2)}, u32[]{:S(2)}) collective-permute-start(bf16[256,1536]{1,0:T(8,128)(2,1)} %get-tuple-element.195), channel_id=1, source_target_pairs={{0,24},{4,28},{8,0},{12,4},{16,8},{20,12},{24,16},{28,20},{1,25},{... | collective-permute-start | bytes 2359304 | tf_op jit(solution)/shard_map/ppermute | solution.py:366
  1008.9 96.7 %collective-permute-start.73 = (bf16[256,1536]{1,0:T(8,128)(2,1)S(1)}, bf16[256,1536]{1,0:T(8,128)(2,1)S(1)}, u32[]{:S(2)}, u32[]{:S(2)}) collective-permute-start(bf16[256,1536]{1,0:T(8,128)(2,1)S(1)} %copy-done.47), channel_id=1, source_target_pairs={{0,16},{4,20},{8,24},{12,28},{16,0},{20,4},{24,8},{28,12},{1,17},{... | collective-permute-start | bytes 2359304 | tf_op jit(solution)/shard_map/ppermute | solution.py:366
  1064.7 41.0 %collective-permute-start.71 = (bf16[256,1536]{1,0:T(8,128)(2,1)S(1)}, bf16[256,1536]{1,0:T(8,128)(2,1)S(1)}, u32[]{:S(2)}, u32[]{:S(2)}) collective-permute-start(bf16[256,1536]{1,0:T(8,128)(2,1)S(1)} %copy-done.46), channel_id=1, source_target_pairs={{0,8},{4,12},{8,16},{12,20},{16,24},{20,28},{24,0},{28,4},{1,9},{5... | collective-permute-start | bytes 2359304 | tf_op jit(solution)/shard_map/ppermute | solution.py:366
  1064.9 40.8 %collective-permute-start.50 = (bf16[256,2048]{1,0:T(8,128)(2,1)S(1)}, bf16[256,2048]{1,0:T(8,128)(2,1)S(1)}, u32[]{:S(2)}, u32[]{:S(2)}) collective-permute-start(bf16[256,2048]{1,0:T(8,128)(2,1)S(1)} %copy-done.19), channel_id=1, source_target_pairs={{0,2},{1,3},{2,0},{3,1},{4,6},{5,7},{6,4},{7,5},{8,10},{9,11},{10,... | collective-permute-start | bytes 3145736 | tf_op jit(solution)/shard_map/ppermute | solution.py:281
  1068.3 58.2 %collective-permute-start.47 = (bf16[512,2048]{1,0:T(8,128)(2,1)}, bf16[512,2048]{1,0:T(8,128)(2,1)}, u32[]{:S(2)}, u32[]{:S(2)}) collective-permute-start(bf16[512,2048]{1,0:T(8,128)(2,1)} %pad_maximum_fusion.11), channel_id=1, source_target_pairs={{0,1},{1,0},{2,3},{3,2},{4,5},{5,4},{6,7},{7,6},{8,9},{9,8},{10,11... | collective-permute-start | bytes 6291464 | tf_op jit(solution)/shard_map/ppermute | solution.py:281
  1070.5 45.6 %collective-permute-start.96 = (f32[4352]{0:T(1024)}, f32[4352]{0:T(1024)}, u32[]{:S(2)}, u32[]{:S(2)}) collective-permute-start(f32[4352]{0:T(1024)} %add.614), channel_id=1, source_target_pairs={{0,8},{4,12},{8,0},{12,4},{16,24},{20,28},{24,16},{28,20},{1,9},{5... | collective-permute-start | bytes 52232 | tf_op jit(solution)/shard_map/ppermute | solution.py:548
  1108.3 48.4 %collective-permute-start.51 = (bf16[512,2048]{1,0:T(8,128)(2,1)}, bf16[512,2048]{1,0:T(8,128)(2,1)}, u32[]{:S(2)}, u32[]{:S(2)}) collective-permute-start(bf16[512,2048]{1,0:T(8,128)(2,1)} %pad_maximum_fusion.12), channel_id=1, source_target_pairs={{0,1},{1,0},{2,3},{3,2},{4,5},{5,4},{6,7},{7,6},{8,9},{9,8},{10,11... | collective-permute-start | bytes 6291464 | tf_op jit(solution)/shard_map/ppermute | solution.py:281
  1116.9 38.1 %collective-permute-start.59 = (bf16[256,768]{1,0:T(8,128)(2,1)}, bf16[256,768]{1,0:T(8,128)(2,1)S(1)}, u32[]{:S(2)}, u32[]{:S(2)}) collective-permute-start(bf16[256,768]{1,0:T(8,128)(2,1)} %get-tuple-element.236), channel_id=1, source_target_pairs={{0,16},{4,20},{8,24},{12,28},{16,0},{20,4},{24,8},{28,12},{1,17},{... | collective-permute-start | bytes 1179656 | tf_op jit(solution)/shard_map/ppermute | solution.py:366
  (125 other events, 2151.0 us)
where the time goes:
time: 1170 us; the launch traced here: 1160 us
  waiting for transfers between devices  519 us (44%)
  starting transfers between devices  266 us (23%)
  matrix products  149 us (13%)
  local copies, waits for them, and re-layouts  91.2 us (8%)
  other arithmetic  89.1 us (8%)
  Pallas kernels  47 us (4%)
    ppermute x18, waiting for transfers between devices, scatter_line(): lax.ppermute(part, 'dp', outer_route(step + 1, inner, outer))  145 us
    ppermute x15, waiting for transfers between devices, line_send(): lax.ppermute(shard, 'dp', outer_route(step, inner, outer))  119 us
    ppermute x15, waiting for transfers between devices, pair_send(): lax.ppermute(part, 'dp', swap_pairs(inner * outer, 1))  112 us
    ppermute x15, starting transfers between devices, line_send(): lax.ppermute(shard, 'dp', outer_route(step, inner, outer))  101 us
    ppermute x18, starting transfers between devices, scatter_line(): lax.ppermute(part, 'dp', outer_route(step + 1, inner, outer))  98.6 us
    ppermute x24, waiting for transfers between devices, scatter_send(): received.append(lax.ppermute(sent, 'dp', swap_pairs(inner * outer, 1)))  91.8 us
    dot_general x10, matrix products, matmul_nt(): jnp.einsum('tf,df->td', left, right, preferred_element_type=wide_type)  59.2 us
    dot_general x7, matrix products, matmul(): return jnp.dot(left, right, preferred_element_type=wide_type)  47.6 us
  transfers between devices with their start and end apart: 98, of which 34 were waited for; matrix products, arithmetic and copies ran while one was open for 23% of the time, Pallas kernels for 4%

commit v1 on v0

--- a/solution.py
+++ b/solution.py
@@ -458,7 +458,6 @@
     second_normed = tensor_gather(
         (normal_two * ffn_gain).astype(low_type), tensor_rank, tensor_size
     )
-    x_dn = pair_send(after(tuple(z_dn), second_normed), *sizes)
     full_gf = join_rows(in_order(ffn_gate_weight, z_gf, w_gf, after(tuple(x_gf), second_normed), *ring))
     ffn_gate = matmul(second_normed, full_gf)
     full_up = join_rows(in_order(ffn_up_weight, z_up, w_up, after(tuple(x_up), ffn_gate), *ring))
@@ -466,6 +465,7 @@
     sig_gate = jax.nn.sigmoid(ffn_gate)
     active = ffn_gate * sig_gate
     hidden = (active * ffn_up).astype(low_type)
+    x_dn = pair_send(after(tuple(z_dn), hidden), *sizes)
     weight_dn = matmul_tn(grad_low, hidden).astype(low_type)
     blocks_dn, pair_dn = scatter_send(weight_dn, *ring)
     full_dn = join_columns(
@@ -480,18 +480,18 @@
     weight_up = matmul_tn(second_normed, grad_ffn_up).astype(low_type)
     blocks_gf, pair_gf = scatter_send(weight_gf, *ring)
     blocks_up, pair_up = scatter_send(weight_up, *ring)
+    mine_dn, line_sum_dn, sent_dn = scatter_line(blocks_dn, after(pair_dn, weight_gf), *ring)
     grad_second = tensor_scatter(
         lambda gate_rows, up_rows: matmul_nt(gate_rows, full_gf) + matmul_nt(up_rows, full_up),
         (grad_ffn_gate, grad_ffn_up),
         tensor_rank,
         tensor_size,
-        (weight_gf,),
+        (weight_gf, sent_dn),
     )
     back_two, grad_ffn_gain = norm_back(normal_two, inv_two, ffn_gain, grad_second)
     grad_middle = share_cotangent + back_two
     share_low = grad_middle.astype(low_type)
-    mine_dn, line_sum_dn, _ = scatter_line(blocks_dn, after(pair_dn, share_low), *ring)
-    middle_low = tensor_gather(share_low, tensor_rank, tensor_size, (weight_up, mine_dn))
+    middle_low = tensor_gather(share_low, tensor_rank, tensor_size, (weight_up,))
 
     grad_gated = matmul_nt(middle_low, full_o).astype(low_type)
     weight_o = matmul_tn(middle_low, gated).astype(low_type)
@@ -507,25 +507,26 @@
     weight_qk = matmul_tn(first_normed, grad_qk).astype(low_type)
     blocks_vg, pair_vg = scatter_send(weight_vg, *ring)
     blocks_qk, pair_qk = scatter_send(weight_qk, *ring)
+    mine_up, line_sum_up, sent_up = scatter_line(blocks_up, pair_up, *ring)
     grad_first = tensor_scatter(
         lambda qk_rows, vg_rows: matmul_nt(qk_rows, full_in[:, : cols_q + cols_k])
         + matmul_nt(vg_rows, full_in[:, cols_q + cols_k :]),
         (grad_qk, grad_vg),
         tensor_rank,
         tensor_size,
-        (weight_vg, weight_qk),
+        (weight_vg, weight_qk, sent_up),
     )
     branch_two = tensor_scatter(
         lambda rows: matmul(rows, full_dn),
         (after(hidden, weight_vg, weight_qk),),
         tensor_rank,
         tensor_size,
+        (sent_up,),
     )
     result = tensor_gather((middle + branch_two).astype(low_type), tensor_rank, tensor_size)
-    mine_up, line_sum_up, sent_up = scatter_line(blocks_up, after(pair_up, grad_first), *ring)
-    mine_o, line_sum_o, sent_o = scatter_line(blocks_o, after(pair_o, sent_up), *ring)
-    mine_vg, line_sum_vg, sent_vg = scatter_line(blocks_vg, after(pair_vg, sent_o), *ring)
-    mine_qk, line_sum_qk, _ = scatter_line(blocks_qk, after(pair_qk, sent_vg), *ring)
+    mine_o, line_sum_o, _ = scatter_line(blocks_o, pair_o, *ring)
+    mine_vg, line_sum_vg, _ = scatter_line(blocks_vg, pair_vg, *ring)
+    mine_qk, line_sum_qk, _ = scatter_line(blocks_qk, pair_qk, *ring)
     grad_dn = turned(scatter_sum(mine_dn, line_sum_dn, mine_up))
     grad_gf = scatter_sum(mine_gf, line_sum_gf, mine_up)
     grad_up = scatter_sum(mine_up, line_sum_up, mine_vg)

time: 1170 us -> 1220 us (1.043)
  waiting for transfers between devices: 519 us -> 601 us
  starting transfers between devices: 266 us -> 240 us
    ppermute x24, waiting for transfers between devices: 91.8 us -> 162 us  [scatter_send(): received.append(lax.ppermute(sent, 'dp', swap_pairs(inner * outer, 1)))]
    ppermute x4, waiting for transfers between devices: 36.8 us -> 0.01 us  [tensor_scatter(): lax.ppermute(sent.astype(low_type), 'tensor', swap_pairs(size, bit))]
    ppermute x8, waiting for transfers between devices: 0.62 us -> 30.5 us  [tensor_gather(): received = lax.ppermute(share, 'tensor', swap_pairs(size, bit))]
    ppermute x15, waiting for transfers between devices: 112 us -> 133 us  [pair_send(): lax.ppermute(part, 'dp', swap_pairs(inner * outer, 1))]
    ppermute x5, starting transfers between devices: 21.1 us -> 4.64 us  [layer(): received = lax.ppermute(gains, axis_name, swap_pairs(size, bit))]
    unnamed x204 -> x188, local copies, waits for them, and re-layouts: 25.5 us -> 21.5 us
  transfers between devices with their start and end apart: 98 -> 98, of which waited for: 34 -> 43; matrix products, arithmetic and copies ran while one was open for 23% -> 19% of each run, Pallas kernels for 4% -> 4%
where the time goes in v1:
time: 1220 us; the launch traced here: 1210 us
  waiting for transfers between devices  601 us (49%)
  starting transfers between devices  240 us (20%)
  matrix products  143 us (12%)
  other arithmetic  89.8 us (7%)
  local copies, waits for them, and re-layouts  83 us (7%)
  Pallas kernels  47 us (4%)
    ppermute x24, waiting for transfers between devices, scatter_send(): received.append(lax.ppermute(sent, 'dp', swap_pairs(inner * outer, 1)))  162 us
    ppermute x18, waiting for transfers between devices, scatter_line(): lax.ppermute(part, 'dp', outer_route(step + 1, inner, outer))  135 us
    ppermute x15, waiting for transfers between devices, pair_send(): lax.ppermute(part, 'dp', swap_pairs(inner * outer, 1))  133 us
    ppermute x15, waiting for transfers between devices, line_send(): lax.ppermute(shard, 'dp', outer_route(step, inner, outer))  119 us
    ppermute x15, starting transfers between devices, line_send(): lax.ppermute(shard, 'dp', outer_route(step, inner, outer))  100 us
    ppermute x18, starting transfers between devices, scatter_line(): lax.ppermute(part, 'dp', outer_route(step + 1, inner, outer))  89.3 us
    dot_general x10, matrix products, matmul_nt(): jnp.einsum('tf,df->td', left, right, preferred_element_type=wide_type)  55 us
    dot_general x7, matrix products, matmul(): return jnp.dot(left, right, preferred_element_type=wide_type)  48.4 us
  transfers between devices with their start and end apart: 98, of which 43 were waited for; matrix products, arithmetic and copies ran while one was open for 19% of the time, Pallas kernels for 4%

profile of v1, /device:TPU:0, one launch (start us, length us, event | category | flops | bytes accessed | tf_op | source)
XLA Modules:
  0.0 1206.2 jit_solution(12285336905079525229)
XLA Ops:
  40.9 37.8 %collective-permute-done.1 = bf16[256,1536]{1,0:T(8,128)(2,1)S(1)} collective-permute-done((bf16[256,1536]{1,0:T(8,128)(2,1)}, bf16[256,1536]{1,0:T(8,128)(2,1)S(1)}, u32[]{:S(2)}, u32[]{:S(2)}) %collective-permute-start.1) | collective-permute-done | bytes 786464 | tf_op jit(solution)/shard_map/ppermute | solution.py:301
  80.3 17.1 %collective-permute-done.2 = bf16[256,1536]{1,0:T(8,128)(2,1)S(1)} collective-permute-done((bf16[256,1536]{1,0:T(8,128)(2,1)}, bf16[256,1536]{1,0:T(8,128)(2,1)S(1)}, u32[]{:S(2)}, u32[]{:S(2)}) %collective-permute-start.2) | collective-permute-done | bytes 786464 | tf_op jit(solution)/shard_map/ppermute | solution.py:301
  99.7 18.2 %collective-permute-done.5 = bf16[256,1536]{1,0:T(8,128)(2,1)S(1)} collective-permute-done((bf16[256,1536]{1,0:T(8,128)(2,1)S(1)}, bf16[256,1536]{1,0:T(8,128)(2,1)S(1)}, u32[]{:S(2)}, u32[]{:S(2)}) %collective-permute-start.5) | collective-permute-done | bytes 786464 | tf_op jit(solution)/shard_map/ppermute | solution.py:308
  121.6 15.7 %collective-permute-start.18 = (bf16[256,1536]{1,0:T(8,128)(2,1)}, bf16[256,1536]{1,0:T(8,128)(2,1)}, u32[]{:S(2)}, u32[]{:S(2)}) collective-permute-start(bf16[256,1536]{1,0:T(8,128)(2,1)} %param.22), channel_id=1, source_target_pairs={{0,8},{4,12},{8,16},{12,20},{16,24},{20,28},{24,0},{28,4},{1,9},{5... | collective-permute-start | bytes 2359304 | tf_op jit(solution)/shard_map/ppermute | solution.py:301
  145.1 8.5 fusion.108.q_ref.k_ref.v_ref.g_ref
  156.4 11.9 collective-permute-start.25
  176.1 17.4 %shard_map.254 = bf16[1024,512]{1,0:T(8,128)(2,1)} custom-call(f32[1024,1536]{1,0:T(8,128)} %fusion.108.q_ref.k_ref.v_ref.g_ref, f32[1024,1536]{1,0:T(8,128)} %fusion.108.q_ref.k_ref.v_ref.g_ref, f32[1024,1536]{1,0:T(8,128)} %fusion.108.q_ref.k_ref.v_ref.g_ref, f32[1024,1536]{1,0:T(8,128)} %fusion.108.q_ref.k_ref.v_ref.g_ref, ...), custom_call_target="tpu_custom_call" | custom-call | tf_op jit(solution)/shard_map/pallas_call | solution.py:446
  208.8 30.1 %collective-permute-done.26 = bf16[256,1536]{1,0:T(8,128)(2,1)} collective-permute-done((bf16[256,1536]{1,0:T(8,128)(2,1)}, bf16[256,1536]{1,0:T(8,128)(2,1)}, u32[]{:S(2)}, u32[]{:S(2)}) %collective-permute-start.26) | collective-permute-done | bytes 786464 | tf_op jit(solution)/shard_map/ppermute | solution.py:301
  243.2 17.8 %collective-permute-start.20 = (bf16[256,1536]{1,0:T(8,128)(2,1)}, bf16[256,1536]{1,0:T(8,128)(2,1)S(1)}, u32[]{:S(2)}, u32[]{:S(2)}) collective-permute-start(bf16[256,1536]{1,0:T(8,128)(2,1)} %param.22), channel_id=1, source_target_pairs={{0,24},{4,28},{8,0},{12,4},{16,8},{20,12},{24,16},{28,20},{1,25},{... | collective-permute-start | bytes 2359304 | tf_op jit(solution)/shard_map/ppermute | solution.py:301
  269.5 19.6 %collective-permute-start.32 = (bf16[1536,256]{1,0:T(8,128)(2,1)S(1)}, bf16[1536,256]{1,0:T(8,128)(2,1)}, u32[]{:S(2)}, u32[]{:S(2)}) collective-permute-start(bf16[1536,256]{1,0:T(8,128)(2,1)S(1)} %copy-done.35), channel_id=1, source_target_pairs={{0,8},{4,12},{8,16},{12,20},{16,24},{20,28},{24,0},{28,4},{1,9},{5... | collective-permute-start | bytes 2359304 | tf_op jit(solution)/shard_map/ppermute | solution.py:301
  291.5 18.1 %collective-permute-start.34 = (bf16[1536,256]{1,0:T(8,128)(2,1)S(1)}, bf16[1536,256]{1,0:T(8,128)(2,1)}, u32[]{:S(2)}, u32[]{:S(2)}) collective-permute-start(bf16[1536,256]{1,0:T(8,128)(2,1)S(1)} %copy-done.35), channel_id=1, source_target_pairs={{0,24},{4,28},{8,0},{12,4},{16,8},{20,12},{24,16},{28,20},{1,25},{... | collective-permute-start | bytes 2359304 | tf_op jit(solution)/shard_map/ppermute | solution.py:301
  310.8 7.6 collective-permute-done.32
  319.6 9.3 collective-permute-done.33
  328.9 15.3 %collective-permute-done.34 = bf16[1536,256]{1,0:T(8,128)(2,1)} collective-permute-done((bf16[1536,256]{1,0:T(8,128)(2,1)S(1)}, bf16[1536,256]{1,0:T(8,128)(2,1)}, u32[]{:S(2)}, u32[]{:S(2)}) %collective-permute-start.34) | collective-permute-done | bytes 786464 | tf_op jit(solution)/shard_map/ppermute | solution.py:301
  355.1 46.6 %collective-permute-done.24 = bf16[256,1536]{1,0:T(8,128)(2,1)S(1)} collective-permute-done((bf16[256,1536]{1,0:T(8,128)(2,1)S(1)}, bf16[256,1536]{1,0:T(8,128)(2,1)S(1)}, u32[]{:S(2)}, u32[]{:S(2)}) %collective-permute-start.24) | collective-permute-done | bytes 786464 | tf_op jit(solution)/shard_map/ppermute | solution.py:308
  403.9 13.1 %fusion.104 = f32[1024,1536]{1,0:T(8,128)} fusion(bf16[2048,1536]{1,0:T(8,128)(2,1)S(1)} %bitcast.363, bf16[512,2048]{1,0:T(8,128)(2,1)} %get-tuple-element.197, bf16[512,2048]{1,0:T(8,128)(2,1)} %get-tuple-element.196), kind=kOutput, calls=%fused_computation.313 | convolution fusion | flops 6450839552 | bytes 16777216 | tf_op jit(solution)/shard_map/dot_general | solution.py:224
  417.0 34.4 %collective-permute-done.31 = bf16[256,1536]{1,0:T(8,128)(2,1)} collective-permute-done((bf16[256,1536]{1,0:T(8,128)(2,1)}, bf16[256,1536]{1,0:T(8,128)(2,1)}, u32[]{:S(2)}, u32[]{:S(2)}) %collective-permute-start.31) | collective-permute-done | bytes 786464 | tf_op jit(solution)/shard_map/ppermute | solution.py:308
  457.0 12.3 %multiply_convert_fusion.1 = (bf16[1024,1536]{1,0:T(8,128)(2,1)S(1)}, f32[1024,1536]{1,0:T(8,128)}) fusion(f32[1024,1536]{1,0:T(8,128)} %fusion.104, bf16[2048,1536]{1,0:T(8,128)(2,1)S(1)} %bitcast.368, bf16[512,2048]{1,0:T(8,128)(2,1)} %get-tuple-element.197, bf16[512,2048]{1,0:T(8,128)(2,1)S(1)} %copy-done.27), kind=kOutput, calls=%fused_computation.19 | convolution fusion | flops 6460276736 | bytes 26214400 | tf_op jit(solution)/shard_map/dot_general | solution.py:224
  471.9 8.7 fusion.3
  480.6 8.8 copy.36
  489.4 32.5 %collective-permute-done.38 = bf16[1536,256]{1,0:T(8,128)(2,1)} collective-permute-done((bf16[1536,256]{1,0:T(8,128)(2,1)}, bf16[1536,256]{1,0:T(8,128)(2,1)}, u32[]{:S(2)}, u32[]{:S(2)}) %collective-permute-start.38) | collective-permute-done | bytes 786464 | tf_op jit(solution)/shard_map/ppermute | solution.py:308
  534.6 16.8 %fusion.7 = (bf16[1024,1536]{1,0:T(8,128)(2,1)}, bf16[1024,1536]{1,0:T(8,128)(2,1)}) fusion(f32[1024,1536]{1,0:T(8,128)} %fusion.104, f32[1024,1536]{1,0:T(8,128)} %get-tuple-element.242, bf16[1536,2048]{1,0:T(8,128)(2,1)} %copy-done.59, bf16[1024,2048]{1,0:T(8,128)(2,1)} %bitcast.389), kind=kOutput, calls=%fused_computation.18 | convolution fusion | flops 6462898176 | bytes 29360128 | tf_op jit(solution)/shard_map/tf,df->td/dot_general | solution.py:228
  551.4 6.6 fusion.45
  558.0 6.9 add_convert_fusion.1
  569.0 5.0 fusion.48
  574.0 5.8 convolution_add_fusion.1
  583.2 9.2 convolution_convert_fusion.1
  592.4 11.6 collective-permute-done.61
  604.0 16.4 %collective-permute-done.41 = bf16[256,1536]{1,0:T(8,128)(2,1)} collective-permute-done((bf16[256,1536]{1,0:T(8,128)(2,1)}, bf16[256,1536]{1,0:T(8,128)(2,1)}, u32[]{:S(2)}, u32[]{:S(2)}) %collective-permute-start.41) | collective-permute-done | bytes 786464 | tf_op jit(solution)/shard_map/ppermute | solution.py:348
  628.6 7.9 convolution_convert_fusion
  636.5 16.3 %collective-permute-done.42 = bf16[256,2048]{1,0:T(8,128)(2,1)S(1)} collective-permute-done((bf16[256,2048]{1,0:T(8,128)(2,1)S(1)}, bf16[256,2048]{1,0:T(8,128)(2,1)S(1)}, u32[]{:S(2)}, u32[]{:S(2)}) %collective-permute-start.42) | collective-permute-done | bytes 1048608 | tf_op jit(solution)/shard_map/ppermute | solution.py:281
  660.7 12.9 %collective-permute-done.60 = bf16[256,1536]{1,0:T(8,128)(2,1)S(1)} collective-permute-done((bf16[256,1536]{1,0:T(8,128)(2,1)S(1)}, bf16[256,1536]{1,0:T(8,128)(2,1)S(1)}, u32[]{:S(2)}, u32[]{:S(2)}) %collective-permute-start.60) | collective-permute-done | bytes 786464 | tf_op jit(solution)/shard_map/ppermute | solution.py:348
  674.2 16.3 %collective-permute-done.76 = bf16[256,1536]{1,0:T(8,128)(2,1)S(1)} collective-permute-done((bf16[256,1536]{1,0:T(8,128)(2,1)S(1)}, bf16[256,1536]{1,0:T(8,128)(2,1)S(1)}, u32[]{:S(2)}, u32[]{:S(2)}) %collective-permute-start.76) | collective-permute-done | bytes 786464 | tf_op jit(solution)/shard_map/ppermute | solution.py:348
  691.0 16.3 %collective-permute-done.74 = bf16[256,1536]{1,0:T(8,128)(2,1)S(1)} collective-permute-done((bf16[256,1536]{1,0:T(8,128)(2,1)S(1)}, bf16[256,1536]{1,0:T(8,128)(2,1)S(1)}, u32[]{:S(2)}, u32[]{:S(2)}) %collective-permute-start.74) | collective-permute-done | bytes 786464 | tf_op jit(solution)/shard_map/ppermute | solution.py:348
  707.9 16.3 %collective-permute-done.46 = bf16[256,1536]{1,0:T(8,128)(2,1)S(1)} collective-permute-done((bf16[256,1536]{1,0:T(8,128)(2,1)S(1)}, bf16[256,1536]{1,0:T(8,128)(2,1)S(1)}, u32[]{:S(2)}, u32[]{:S(2)}) %collective-permute-start.46) | collective-permute-done | bytes 786464 | tf_op jit(solution)/shard_map/ppermute | solution.py:348
  733.1 22.9 %shard_map.255 = (bf16[1024,512]{1,0:T(8,128)(2,1)}, bf16[1024,256]{1,0:T(8,128)(2,1)}, bf16[1024,256]{1,0:T(8,128)(2,1)}, bf16[1024,512]{1,0:T(8,128)(2,1)}, f32[2,2,2,128]{3,2,1,0:T(2,128)}) custom-call(f32[1024,1536]{1,0:T(8,128)} %fusion.108.q_ref.k_ref.v_ref.g_ref, f32[1024,1536]{1,0:T(8,128)} %fusion.108.q_ref.k_ref.v_ref.g_ref, ...), custom_call_target="tpu_custom_call" | custom-call | tf_op jit(solution)/shard_map/pallas_call | solution.py:499
  759.4 4.7 convolution_convert_fusion.5
  764.1 10.7 collective-permute-done.70
  775.1 4.5 convolution_convert_fusion.3
  779.6 4.4 convolution_convert_fusion.4
  784.1 4.6 convolution_convert_fusion.6
  788.7 4.9 fusion.42
  814.7 5.1 collective-permute-done.81
  820.3 7.9 collective-permute-done.53
  828.7 7.9 collective-permute-done.58
  839.0 6.1 collective-permute-done.56
  845.6 7.9 collective-permute-done.54
  853.8 8.1 collective-permute-done.91
  861.9 8.4 collective-permute-done.89
  870.3 5.8 collective-permute-start.84
  885.3 4.8 collective-permute-done.84
  891.3 15.7 %collective-permute-start.88 = (bf16[256,768]{1,0:T(8,128)(2,1)}, bf16[256,768]{1,0:T(8,128)(2,1)}, u32[]{:S(2)}, u32[]{:S(2)}) collective-permute-start(bf16[256,768]{1,0:T(8,128)(2,1)} %get-tuple-element.212), channel_id=1, source_target_pairs={{0,8},{4,12},{8,16},{12,20},{16,24},{20,28},{24,0},{28,4},{1,9},{5... | collective-permute-start | bytes 1179656 | tf_op jit(solution)/shard_map/ppermute | solution.py:366
  913.3 30.2 %collective-permute-done.90 = bf16[256,768]{1,0:T(8,128)(2,1)} collective-permute-done((bf16[256,768]{1,0:T(8,128)(2,1)}, bf16[256,768]{1,0:T(8,128)(2,1)}, u32[]{:S(2)}, u32[]{:S(2)}) %collective-permute-start.90) | collective-permute-done | bytes 393248 | tf_op jit(solution)/shard_map/ppermute | solution.py:366
  957.0 20.3 %collective-permute-done.77 = bf16[256,1536]{1,0:T(8,128)(2,1)} collective-permute-done((bf16[256,1536]{1,0:T(8,128)(2,1)}, bf16[256,1536]{1,0:T(8,128)(2,1)}, u32[]{:S(2)}, u32[]{:S(2)}) %collective-permute-start.77) | collective-permute-done | bytes 786464 | tf_op jit(solution)/shard_map/ppermute | solution.py:366
  977.9 15.3 %collective-permute-start.73 = (bf16[256,1536]{1,0:T(8,128)(2,1)}, bf16[256,1536]{1,0:T(8,128)(2,1)S(1)}, u32[]{:S(2)}, u32[]{:S(2)}) collective-permute-start(bf16[256,1536]{1,0:T(8,128)(2,1)} %get-tuple-element.164), channel_id=1, source_target_pairs={{0,24},{4,28},{8,0},{12,4},{16,8},{20,12},{24,16},{28,20},{1,25},{... | collective-permute-start | bytes 2359304 | tf_op jit(solution)/shard_map/ppermute | solution.py:366
  1006.8 4.6 collective-permute-done.73
  1011.5 4.5 collective-permute-start.65
  1015.9 46.7 %collective-permute-done.71 = bf16[256,1536]{1,0:T(8,128)(2,1)S(1)} collective-permute-done((bf16[256,1536]{1,0:T(8,128)(2,1)}, bf16[256,1536]{1,0:T(8,128)(2,1)S(1)}, u32[]{:S(2)}, u32[]{:S(2)}) %collective-permute-start.71) | collective-permute-done | bytes 786464 | tf_op jit(solution)/shard_map/ppermute | solution.py:366
  1062.6 33.6 %collective-permute-start.62 = (bf16[256,1536]{1,0:T(8,128)(2,1)S(1)}, bf16[256,1536]{1,0:T(8,128)(2,1)S(1)}, u32[]{:S(2)}, u32[]{:S(2)}) collective-permute-start(bf16[256,1536]{1,0:T(8,128)(2,1)S(1)} %copy-done.39), channel_id=1, source_target_pairs={{0,8},{4,12},{8,16},{12,20},{16,24},{20,28},{24,0},{28,4},{1,9},{5... | collective-permute-start | bytes 2359304 | tf_op jit(solution)/shard_map/ppermute | solution.py:366
  1101.9 20.1 %collective-permute-done.94 = f32[4352]{0:T(1024)S(1)} collective-permute-done((f32[4352]{0:T(1024)S(1)}, f32[4352]{0:T(1024)S(1)}, u32[]{:S(2)}, u32[]{:S(2)}) %collective-permute-start.94) | collective-permute-done | bytes 17440 | tf_op jit(solution)/shard_map/ppermute | solution.py:549
  1132.3 13.6 %collective-permute-done.51 = bf16[256,2048]{1,0:T(8,128)(2,1)S(1)} collective-permute-done((bf16[256,2048]{1,0:T(8,128)(2,1)S(1)}, bf16[256,2048]{1,0:T(8,128)(2,1)S(1)}, u32[]{:S(2)}, u32[]{:S(2)}) %collective-permute-start.51) | collective-permute-done | bytes 1048608 | tf_op jit(solution)/shard_map/ppermute | solution.py:281
  1151.3 4.8 shard_map.256
  1172.3 24.0 %collective-permute-done.57 = bf16[256,768]{1,0:T(8,128)(2,1)S(1)} collective-permute-done((bf16[256,768]{1,0:T(8,128)(2,1)}, bf16[256,768]{1,0:T(8,128)(2,1)S(1)}, u32[]{:S(2)}, u32[]{:S(2)}) %collective-permute-start.57) | collective-permute-done | bytes 393248 | tf_op jit(solution)/shard_map/ppermute | solution.py:366
  1201.3 4.5 convert.27
  (499 shorter events, 281.4 us)
Async XLA Ops:
  0.6 121.0 %collective-permute-start.8 = (bf16[512,256]{1,0:T(8,128)(2,1)}, bf16[512,256]{1,0:T(8,128)(2,1)}, u32[]{:S(2)}, u32[]{:S(2)}) collective-permute-start(bf16[512,256]{1,0:T(8,128)(2,1)} %param.21), channel_id=1, source_target_pairs={{0,16},{4,20},{8,24},{12,28},{16,0},{20,4},{24,8},{28,12},{1,17},{... | collective-permute-start | bytes 786440 | tf_op jit(solution)/shard_map/ppermute | solution.py:301
  4.8 132.5 %collective-permute-start.7 = (bf16[512,256]{1,0:T(8,128)(2,1)}, bf16[512,256]{1,0:T(8,128)(2,1)}, u32[]{:S(2)}, u32[]{:S(2)}) collective-permute-start(bf16[512,256]{1,0:T(8,128)(2,1)} %param.21), channel_id=1, source_target_pairs={{0,8},{4,12},{8,16},{12,20},{16,24},{20,28},{24,0},{28,4},{1,9},{5... | collective-permute-start | bytes 786440 | tf_op jit(solution)/shard_map/ppermute | solution.py:301
  32.7 106.1 %collective-permute-start.9 = (bf16[512,256]{1,0:T(8,128)(2,1)S(1)}, bf16[512,256]{1,0:T(8,128)(2,1)}, u32[]{:S(2)}, u32[]{:S(2)}) collective-permute-start(bf16[512,256]{1,0:T(8,128)(2,1)S(1)} %copy-done.57), channel_id=1, source_target_pairs={{0,24},{4,28},{8,0},{12,4},{16,8},{20,12},{24,16},{28,20},{1,25},{... | collective-permute-start | bytes 786440 | tf_op jit(solution)/shard_map/ppermute | solution.py:301
  37.6 41.2 %collective-permute-start.1 = (bf16[256,1536]{1,0:T(8,128)(2,1)}, bf16[256,1536]{1,0:T(8,128)(2,1)S(1)}, u32[]{:S(2)}, u32[]{:S(2)}) collective-permute-start(bf16[256,1536]{1,0:T(8,128)(2,1)} %constant_dynamic-update-slice_fusion), channel_id=1, source_target_pairs={{0,16},{4,20},{8,24},{12,28},{16,0},{20,4},{24,8},{28,12},{1,17},{... | collective-permute-start | bytes 2359304 | tf_op jit(solution)/shard_map/ppermute | solution.py:301
  39.1 58.4 %collective-permute-start.2 = (bf16[256,1536]{1,0:T(8,128)(2,1)}, bf16[256,1536]{1,0:T(8,128)(2,1)S(1)}, u32[]{:S(2)}, u32[]{:S(2)}) collective-permute-start(bf16[256,1536]{1,0:T(8,128)(2,1)} %constant_dynamic-update-slice_fusion), channel_id=1, source_target_pairs={{0,24},{4,28},{8,0},{12,4},{16,8},{20,12},{24,16},{28,20},{1,25},{... | collective-permute-start | bytes 2359304 | tf_op jit(solution)/shard_map/ppermute | solution.py:301
  99.1 40.3 %collective-permute-start.6 = (bf16[256,1536]{1,0:T(8,128)(2,1)S(1)}, bf16[256,1536]{1,0:T(8,128)(2,1)S(1)}, u32[]{:S(2)}, u32[]{:S(2)}) collective-permute-start(bf16[256,1536]{1,0:T(8,128)(2,1)S(1)} %collective-permute-done.2), channel_id=1, source_target_pairs={{0,4},{4,0},{8,12},{12,8},{16,20},{20,16},{24,28},{28,24},{1,5},{5... | collective-permute-start | bytes 2359304 | tf_op jit(solution)/shard_map/ppermute | solution.py:308
  117.9 151.6 %collective-permute-start.19 = (bf16[256,1536]{1,0:T(8,128)(2,1)}, bf16[256,1536]{1,0:T(8,128)(2,1)}, u32[]{:S(2)}, u32[]{:S(2)}) collective-permute-start(bf16[256,1536]{1,0:T(8,128)(2,1)} %param.22), channel_id=1, source_target_pairs={{0,16},{4,20},{8,24},{12,28},{16,0},{20,4},{24,8},{28,12},{1,17},{... | collective-permute-start | bytes 2359304 | tf_op jit(solution)/shard_map/ppermute | solution.py:301
  121.6 145.7 %collective-permute-start.18 = (bf16[256,1536]{1,0:T(8,128)(2,1)}, bf16[256,1536]{1,0:T(8,128)(2,1)}, u32[]{:S(2)}, u32[]{:S(2)}) collective-permute-start(bf16[256,1536]{1,0:T(8,128)(2,1)} %param.22), channel_id=1, source_target_pairs={{0,8},{4,12},{8,16},{12,20},{16,24},{20,28},{24,0},{28,4},{1,9},{5... | collective-permute-start | bytes 2359304 | tf_op jit(solution)/shard_map/ppermute | solution.py:301
  154.9 107.3 %collective-permute-start.21 = (bf16[256,1536]{1,0:T(8,128)(2,1)}, bf16[256,1536]{1,0:T(8,128)(2,1)}, u32[]{:S(2)}, u32[]{:S(2)}) collective-permute-start(bf16[256,1536]{1,0:T(8,128)(2,1)} %param.22), channel_id=1, source_target_pairs={{0,4},{4,0},{8,12},{12,8},{16,20},{20,16},{24,28},{28,24},{1,5},{5... | collective-permute-start | bytes 2359304 | tf_op jit(solution)/shard_map/ppermute | solution.py:304
  156.4 44.2 %collective-permute-start.25 = (bf16[256,1536]{1,0:T(8,128)(2,1)}, bf16[256,1536]{1,0:T(8,128)(2,1)}, u32[]{:S(2)}, u32[]{:S(2)}) collective-permute-start(bf16[256,1536]{1,0:T(8,128)(2,1)} %param.23), channel_id=1, source_target_pairs={{0,8},{4,12},{8,16},{12,20},{16,24},{20,28},{24,0},{28,4},{1,9},{5... | collective-permute-start | bytes 2359304 | tf_op jit(solution)/shard_map/ppermute | solution.py:301
  200.6 38.3 %collective-permute-start.26 = (bf16[256,1536]{1,0:T(8,128)(2,1)}, bf16[256,1536]{1,0:T(8,128)(2,1)}, u32[]{:S(2)}, u32[]{:S(2)}) collective-permute-start(bf16[256,1536]{1,0:T(8,128)(2,1)} %param.23), channel_id=1, source_target_pairs={{0,16},{4,20},{8,24},{12,28},{16,0},{20,4},{24,8},{28,12},{1,17},{... | collective-permute-start | bytes 2359304 | tf_op jit(solution)/shard_map/ppermute | solution.py:301
  206.4 36.8 %collective-permute-start.27 = (bf16[256,1536]{1,0:T(8,128)(2,1)}, bf16[256,1536]{1,0:T(8,128)(2,1)}, u32[]{:S(2)}, u32[]{:S(2)}) collective-permute-start(bf16[256,1536]{1,0:T(8,128)(2,1)} %param.23), channel_id=1, source_target_pairs={{0,24},{4,28},{8,0},{12,4},{16,8},{20,12},{24,16},{28,20},{1,25},{... | collective-permute-start | bytes 2359304 | tf_op jit(solution)/shard_map/ppermute | solution.py:301
  243.2 47.1 %collective-permute-start.20 = (bf16[256,1536]{1,0:T(8,128)(2,1)}, bf16[256,1536]{1,0:T(8,128)(2,1)S(1)}, u32[]{:S(2)}, u32[]{:S(2)}) collective-permute-start(bf16[256,1536]{1,0:T(8,128)(2,1)} %param.22), channel_id=1, source_target_pairs={{0,24},{4,28},{8,0},{12,4},{16,8},{20,12},{24,16},{28,20},{1,25},{... | collective-permute-start | bytes 2359304 | tf_op jit(solution)/shard_map/ppermute | solution.py:301
  262.2 84.8 %collective-permute-start.28 = (bf16[256,1536]{1,0:T(8,128)(2,1)}, bf16[256,1536]{1,0:T(8,128)(2,1)S(1)}, u32[]{:S(2)}, u32[]{:S(2)}) collective-permute-start(bf16[256,1536]{1,0:T(8,128)(2,1)} %param.23), channel_id=1, source_target_pairs={{0,4},{4,0},{8,12},{12,8},{16,20},{20,16},{24,28},{28,24},{1,5},{5... | collective-permute-start | bytes 2359304 | tf_op jit(solution)/shard_map/ppermute | solution.py:304
  264.5 64.4 %collective-permute-start.33 = (bf16[1536,256]{1,0:T(8,128)(2,1)S(1)}, bf16[1536,256]{1,0:T(8,128)(2,1)S(1)}, u32[]{:S(2)}, u32[]{:S(2)}) collective-permute-start(bf16[1536,256]{1,0:T(8,128)(2,1)S(1)} %copy-done.35), channel_id=1, source_target_pairs={{0,16},{4,20},{8,24},{12,28},{16,0},{20,4},{24,8},{28,12},{1,17},{... | collective-permute-start | bytes 2359304 | tf_op jit(solution)/shard_map/ppermute | solution.py:301
  269.5 48.9 %collective-permute-start.32 = (bf16[1536,256]{1,0:T(8,128)(2,1)S(1)}, bf16[1536,256]{1,0:T(8,128)(2,1)}, u32[]{:S(2)}, u32[]{:S(2)}) collective-permute-start(bf16[1536,256]{1,0:T(8,128)(2,1)S(1)} %copy-done.35), channel_id=1, source_target_pairs={{0,8},{4,12},{8,16},{12,20},{16,24},{20,28},{24,0},{28,4},{1,9},{5... | collective-permute-start | bytes 2359304 | tf_op jit(solution)/shard_map/ppermute | solution.py:301
  291.5 52.6 %collective-permute-start.34 = (bf16[1536,256]{1,0:T(8,128)(2,1)S(1)}, bf16[1536,256]{1,0:T(8,128)(2,1)}, u32[]{:S(2)}, u32[]{:S(2)}) collective-permute-start(bf16[1536,256]{1,0:T(8,128)(2,1)S(1)} %copy-done.35), channel_id=1, source_target_pairs={{0,24},{4,28},{8,0},{12,4},{16,8},{20,12},{24,16},{28,20},{1,25},{... | collective-permute-start | bytes 2359304 | tf_op jit(solution)/shard_map/ppermute | solution.py:301
  310.4 41.0 %collective-permute-start.17 = (bf16[512,2048]{1,0:T(8,128)(2,1)S(1)}, bf16[512,2048]{1,0:T(8,128)(2,1)S(1)}, u32[]{:S(2)}, u32[]{:S(2)}) collective-permute-start(bf16[512,2048]{1,0:T(8,128)(2,1)S(1)} %pad_maximum_fusion.9), channel_id=1, source_target_pairs={{0,1},{1,0},{2,3},{3,2},{4,5},{5,4},{6,7},{7,6},{8,9},{9,8},{10,11... | collective-permute-start | bytes 6291464 | tf_op jit(solution)/shard_map/ppermute | solution.py:281
  347.3 54.9 %collective-permute-start.22 = (bf16[256,1536]{1,0:T(8,128)(2,1)}, bf16[256,1536]{1,0:T(8,128)(2,1)S(1)}, u32[]{:S(2)}, u32[]{:S(2)}) collective-permute-start(bf16[256,1536]{1,0:T(8,128)(2,1)} %collective-permute-done.18), channel_id=1, source_target_pairs={{0,4},{4,0},{8,12},{12,8},{16,20},{20,16},{24,28},{28,24},{1,5},{5... | collective-permute-start | bytes 2359304 | tf_op jit(solution)/shard_map/ppermute | solution.py:308
  347.9 54.3 %collective-permute-start.23 = (bf16[256,1536]{1,0:T(8,128)(2,1)}, bf16[256,1536]{1,0:T(8,128)(2,1)S(1)}, u32[]{:S(2)}, u32[]{:S(2)}) collective-permute-start(bf16[256,1536]{1,0:T(8,128)(2,1)} %collective-permute-done.19), channel_id=1, source_target_pairs={{0,4},{4,0},{8,12},{12,8},{16,20},{20,16},{24,28},{28,24},{1,5},{5... | collective-permute-start | bytes 2359304 | tf_op jit(solution)/shard_map/ppermute | solution.py:308
  349.4 52.3 %collective-permute-start.24 = (bf16[256,1536]{1,0:T(8,128)(2,1)S(1)}, bf16[256,1536]{1,0:T(8,128)(2,1)S(1)}, u32[]{:S(2)}, u32[]{:S(2)}) collective-permute-start(bf16[256,1536]{1,0:T(8,128)(2,1)S(1)} %collective-permute-done.20), channel_id=1, source_target_pairs={{0,4},{4,0},{8,12},{12,8},{16,20},{20,16},{24,28},{28,24},{1,5},{5... | collective-permute-start | bytes 2359304 | tf_op jit(solution)/shard_map/ppermute | solution.py:308
  350.0 101.5 %collective-permute-start.29 = (bf16[256,1536]{1,0:T(8,128)(2,1)}, bf16[256,1536]{1,0:T(8,128)(2,1)S(1)}, u32[]{:S(2)}, u32[]{:S(2)}) collective-permute-start(bf16[256,1536]{1,0:T(8,128)(2,1)} %collective-permute-done.25), channel_id=1, source_target_pairs={{0,4},{4,0},{8,12},{12,8},{16,20},{20,16},{24,28},{28,24},{1,5},{5... | collective-permute-start | bytes 2359304 | tf_op jit(solution)/shard_map/ppermute | solution.py:308
  351.4 100.0 %collective-permute-start.30 = (bf16[256,1536]{1,0:T(8,128)(2,1)}, bf16[256,1536]{1,0:T(8,128)(2,1)}, u32[]{:S(2)}, u32[]{:S(2)}) collective-permute-start(bf16[256,1536]{1,0:T(8,128)(2,1)} %collective-permute-done.26), channel_id=1, source_target_pairs={{0,4},{4,0},{8,12},{12,8},{16,20},{20,16},{24,28},{28,24},{1,5},{5... | collective-permute-start | bytes 2359304 | tf_op jit(solution)/shard_map/ppermute | solution.py:308
  401.7 49.7 %collective-permute-start.31 = (bf16[256,1536]{1,0:T(8,128)(2,1)}, bf16[256,1536]{1,0:T(8,128)(2,1)}, u32[]{:S(2)}, u32[]{:S(2)}) collective-permute-start(bf16[256,1536]{1,0:T(8,128)(2,1)} %collective-permute-done.27), channel_id=1, source_target_pairs={{0,4},{4,0},{8,12},{12,8},{16,20},{20,16},{24,28},{28,24},{1,5},{5... | collective-permute-start | bytes 2359304 | tf_op jit(solution)/shard_map/ppermute | solution.py:308
  469.3 52.6 %collective-permute-start.36 = (bf16[1536,256]{1,0:T(8,128)(2,1)}, bf16[1536,256]{1,0:T(8,128)(2,1)}, u32[]{:S(2)}, u32[]{:S(2)}) collective-permute-start(bf16[1536,256]{1,0:T(8,128)(2,1)} %collective-permute-done.32), channel_id=1, source_target_pairs={{0,4},{4,0},{8,12},{12,8},{16,20},{20,16},{24,28},{28,24},{1,5},{5... | collective-permute-start | bytes 2359304 | tf_op jit(solution)/shard_map/ppermute | solution.py:308
  469.8 52.1 %collective-permute-start.37 = (bf16[1536,256]{1,0:T(8,128)(2,1)S(1)}, bf16[1536,256]{1,0:T(8,128)(2,1)}, u32[]{:S(2)}, u32[]{:S(2)}) collective-permute-start(bf16[1536,256]{1,0:T(8,128)(2,1)S(1)} %copy-done.37), channel_id=1, source_target_pairs={{0,4},{4,0},{8,12},{12,8},{16,20},{20,16},{24,28},{28,24},{1,5},{5... | collective-permute-start | bytes 2359304 | tf_op jit(solution)/shard_map/ppermute | solution.py:308
  471.3 50.6 %collective-permute-start.38 = (bf16[1536,256]{1,0:T(8,128)(2,1)}, bf16[1536,256]{1,0:T(8,128)(2,1)}, u32[]{:S(2)}, u32[]{:S(2)}) collective-permute-start(bf16[1536,256]{1,0:T(8,128)(2,1)} %collective-permute-done.34), channel_id=1, source_target_pairs={{0,4},{4,0},{8,12},{12,8},{16,20},{20,16},{24,28},{28,24},{1,5},{5... | collective-permute-start | bytes 2359304 | tf_op jit(solution)/shard_map/ppermute | solution.py:308
  567.0 37.0 %collective-permute-start.61 = (bf16[256,1536]{1,0:T(8,128)(2,1)}, bf16[256,1536]{1,0:T(8,128)(2,1)}, u32[]{:S(2)}, u32[]{:S(2)}) collective-permute-start(bf16[256,1536]{1,0:T(8,128)(2,1)} %get-tuple-element.169), channel_id=1, source_target_pairs={{0,4},{4,0},{8,12},{12,8},{16,20},{20,16},{24,28},{28,24},{1,5},{5... | collective-permute-start | bytes 2359304 | tf_op jit(solution)/shard_map/ppermute | solution.py:348
  568.5 51.9 %collective-permute-start.41 = (bf16[256,1536]{1,0:T(8,128)(2,1)}, bf16[256,1536]{1,0:T(8,128)(2,1)}, u32[]{:S(2)}, u32[]{:S(2)}) collective-permute-start(bf16[256,1536]{1,0:T(8,128)(2,1)} %get-tuple-element.170), channel_id=1, source_target_pairs={{0,4},{4,0},{8,12},{12,8},{16,20},{20,16},{24,28},{28,24},{1,5},{5... | collective-permute-start | bytes 2359304 | tf_op jit(solution)/shard_map/ppermute | solution.py:348
  582.6 41.2 %collective-permute-start.40 = (bf16[256,2048]{1,0:T(8,128)(2,1)S(1)}, bf16[256,2048]{1,0:T(8,128)(2,1)S(1)}, u32[]{:S(2)}, u32[]{:S(2)}) collective-permute-start(bf16[256,2048]{1,0:T(8,128)(2,1)S(1)} %dynamic-slice_convert_fusion.2), channel_id=1, source_target_pairs={{0,2},{1,3},{2,0},{3,1},{4,6},{5,7},{6,4},{7,5},{8,10},{9,11},{10,... | collective-permute-start | bytes 3145736 | tf_op jit(solution)/shard_map/ppermute | solution.py:263
  653.1 73.4 %collective-permute-start.43 = (bf16[512,2048]{1,0:T(8,128)(2,1)S(1)}, bf16[512,2048]{1,0:T(8,128)(2,1)S(1)}, u32[]{:S(2)}, u32[]{:S(2)}) collective-permute-start(bf16[512,2048]{1,0:T(8,128)(2,1)S(1)} %pad_maximum_fusion.10), channel_id=1, source_target_pairs={{0,1},{1,0},{2,3},{3,2},{4,5},{5,4},{6,7},{7,6},{8,9},{9,8},{10,11... | collective-permute-start | bytes 6291464 | tf_op jit(solution)/shard_map/ppermute | solution.py:281
  654.8 35.6 %collective-permute-start.76 = (bf16[256,1536]{1,0:T(8,128)(2,1)S(1)}, bf16[256,1536]{1,0:T(8,128)(2,1)S(1)}, u32[]{:S(2)}, u32[]{:S(2)}) collective-permute-start(bf16[256,1536]{1,0:T(8,128)(2,1)S(1)} %get-tuple-element.172), channel_id=1, source_target_pairs={{0,4},{4,0},{8,12},{12,8},{16,20},{20,16},{24,28},{28,24},{1,5},{5... | collective-permute-start | bytes 2359304 | tf_op jit(solution)/shard_map/ppermute | solution.py:348
  656.3 51.0 %collective-permute-start.74 = (bf16[256,1536]{1,0:T(8,128)(2,1)S(1)}, bf16[256,1536]{1,0:T(8,128)(2,1)S(1)}, u32[]{:S(2)}, u32[]{:S(2)}) collective-permute-start(bf16[256,1536]{1,0:T(8,128)(2,1)S(1)} %get-tuple-element.173), channel_id=1, source_target_pairs={{0,4},{4,0},{8,12},{12,8},{16,20},{20,16},{24,28},{28,24},{1,5},{5... | collective-permute-start | bytes 2359304 | tf_op jit(solution)/shard_map/ppermute | solution.py:348
  656.9 67.3 %collective-permute-start.46 = (bf16[256,1536]{1,0:T(8,128)(2,1)S(1)}, bf16[256,1536]{1,0:T(8,128)(2,1)S(1)}, u32[]{:S(2)}, u32[]{:S(2)}) collective-permute-start(bf16[256,1536]{1,0:T(8,128)(2,1)S(1)} %get-tuple-element.174), channel_id=1, source_target_pairs={{0,4},{4,0},{8,12},{12,8},{16,20},{20,16},{24,28},{28,24},{1,5},{5... | collective-permute-start | bytes 2359304 | tf_op jit(solution)/shard_map/ppermute | solution.py:348
  673.6 130.2 %collective-permute-start.67 = (bf16[256,1536]{1,0:T(8,128)(2,1)}, bf16[256,1536]{1,0:T(8,128)(2,1)}, u32[]{:S(2)}, u32[]{:S(2)}) collective-permute-start(bf16[256,1536]{1,0:T(8,128)(2,1)} %get-tuple-element.160), channel_id=1, source_target_pairs={{0,4},{4,0},{8,12},{12,8},{16,20},{20,16},{24,28},{28,24},{1,5},{5... | collective-permute-start | bytes 2359304 | tf_op jit(solution)/shard_map/ppermute | solution.py:348
  690.5 67.5 %collective-permute-start.72 = (bf16[256,1536]{1,0:T(8,128)(2,1)}, bf16[256,1536]{1,0:T(8,128)(2,1)}, u32[]{:S(2)}, u32[]{:S(2)}) collective-permute-start(bf16[256,1536]{1,0:T(8,128)(2,1)} %get-tuple-element.161), channel_id=1, source_target_pairs={{0,4},{4,0},{8,12},{12,8},{16,20},{20,16},{24,28},{28,24},{1,5},{5... | collective-permute-start | bytes 2359304 | tf_op jit(solution)/shard_map/ppermute | solution.py:348
  707.3 67.5 %collective-permute-start.70 = (bf16[256,1536]{1,0:T(8,128)(2,1)}, bf16[256,1536]{1,0:T(8,128)(2,1)}, u32[]{:S(2)}, u32[]{:S(2)}) collective-permute-start(bf16[256,1536]{1,0:T(8,128)(2,1)} %get-tuple-element.162), channel_id=1, source_target_pairs={{0,4},{4,0},{8,12},{12,8},{16,20},{20,16},{24,28},{28,24},{1,5},{5... | collective-permute-start | bytes 2359304 | tf_op jit(solution)/shard_map/ppermute | solution.py:348
  724.2 69.4 %collective-permute-start.68 = (bf16[256,1536]{1,0:T(8,128)(2,1)}, bf16[256,1536]{1,0:T(8,128)(2,1)}, u32[]{:S(2)}, u32[]{:S(2)}) collective-permute-start(bf16[256,1536]{1,0:T(8,128)(2,1)} %get-tuple-element.163), channel_id=1, source_target_pairs={{0,4},{4,0},{8,12},{12,8},{16,20},{20,16},{24,28},{28,24},{1,5},{5... | collective-permute-start | bytes 2359304 | tf_op jit(solution)/shard_map/ppermute | solution.py:348
  805.1 31.5 %collective-permute-start.58 = (bf16[256,768]{1,0:T(8,128)(2,1)S(1)}, bf16[256,768]{1,0:T(8,128)(2,1)S(1)}, u32[]{:S(2)}, u32[]{:S(2)}) collective-permute-start(bf16[256,768]{1,0:T(8,128)(2,1)S(1)} %get-tuple-element.207), channel_id=1, source_target_pairs={{0,4},{4,0},{8,12},{12,8},{16,20},{20,16},{24,28},{28,24},{1,5},{5... | collective-permute-start | bytes 1179656 | tf_op jit(solution)/shard_map/ppermute | solution.py:348
  809.8 35.2 %collective-permute-start.56 = (bf16[256,768]{1,0:T(8,128)(2,1)S(1)}, bf16[256,768]{1,0:T(8,128)(2,1)S(1)}, u32[]{:S(2)}, u32[]{:S(2)}) collective-permute-start(bf16[256,768]{1,0:T(8,128)(2,1)S(1)} %get-tuple-element.208), channel_id=1, source_target_pairs={{0,4},{4,0},{8,12},{12,8},{16,20},{20,16},{24,28},{28,24},{1,5},{5... | collective-permute-start | bytes 1179656 | tf_op jit(solution)/shard_map/ppermute | solution.py:348
  814.1 39.3 %collective-permute-start.54 = (bf16[256,768]{1,0:T(8,128)(2,1)S(1)}, bf16[256,768]{1,0:T(8,128)(2,1)S(1)}, u32[]{:S(2)}, u32[]{:S(2)}) collective-permute-start(bf16[256,768]{1,0:T(8,128)(2,1)S(1)} %get-tuple-element.209), channel_id=1, source_target_pairs={{0,4},{4,0},{8,12},{12,8},{16,20},{20,16},{24,28},{28,24},{1,5},{5... | collective-permute-start | bytes 1179656 | tf_op jit(solution)/shard_map/ppermute | solution.py:348
  819.8 42.1 %collective-permute-start.91 = (bf16[256,768]{1,0:T(8,128)(2,1)S(1)}, bf16[256,768]{1,0:T(8,128)(2,1)S(1)}, u32[]{:S(2)}, u32[]{:S(2)}) collective-permute-start(bf16[256,768]{1,0:T(8,128)(2,1)S(1)} %get-tuple-element.199), channel_id=1, source_target_pairs={{0,4},{4,0},{8,12},{12,8},{16,20},{20,16},{24,28},{28,24},{1,5},{5... | collective-permute-start | bytes 1179656 | tf_op jit(solution)/shard_map/ppermute | solution.py:348
  828.2 42.1 %collective-permute-start.89 = (bf16[256,768]{1,0:T(8,128)(2,1)S(1)}, bf16[256,768]{1,0:T(8,128)(2,1)S(1)}, u32[]{:S(2)}, u32[]{:S(2)}) collective-permute-start(bf16[256,768]{1,0:T(8,128)(2,1)S(1)} %get-tuple-element.200), channel_id=1, source_target_pairs={{0,4},{4,0},{8,12},{12,8},{16,20},{20,16},{24,28},{28,24},{1,5},{5... | collective-permute-start | bytes 1179656 | tf_op jit(solution)/shard_map/ppermute | solution.py:348
  836.6 42.1 %collective-permute-start.87 = (bf16[256,768]{1,0:T(8,128)(2,1)S(1)}, bf16[256,768]{1,0:T(8,128)(2,1)S(1)}, u32[]{:S(2)}, u32[]{:S(2)}) collective-permute-start(bf16[256,768]{1,0:T(8,128)(2,1)S(1)} %get-tuple-element.201), channel_id=1, source_target_pairs={{0,4},{4,0},{8,12},{12,8},{16,20},{20,16},{24,28},{28,24},{1,5},{5... | collective-permute-start | bytes 1179656 | tf_op jit(solution)/shard_map/ppermute | solution.py:348
  845.0 40.2 %collective-permute-start.79 = (bf16[256,768]{1,0:T(8,128)(2,1)S(1)}, bf16[256,768]{1,0:T(8,128)(2,1)S(1)}, u32[]{:S(2)}, u32[]{:S(2)}) collective-permute-start(bf16[256,768]{1,0:T(8,128)(2,1)S(1)} %get-tuple-element.198), channel_id=1, source_target_pairs={{0,4},{4,0},{8,12},{12,8},{16,20},{20,16},{24,28},{28,24},{1,5},{5... | collective-permute-start | bytes 1179656 | tf_op jit(solution)/shard_map/ppermute | solution.py:348
  853.5 140.5 %collective-permute-start.44 = (bf16[512,2048]{1,0:T(8,128)(2,1)}, bf16[512,2048]{1,0:T(8,128)(2,1)}, u32[]{:S(2)}, u32[]{:S(2)}) collective-permute-start(bf16[512,2048]{1,0:T(8,128)(2,1)} %convolution_convert_fusion.6), channel_id=1, source_target_pairs={{0,1},{1,0},{2,3},{3,2},{4,5},{5,4},{6,7},{7,6},{8,9},{9,8},{10,11... | collective-permute-start | bytes 6291464 | tf_op jit(solution)/shard_map/ppermute | solution.py:257
  885.2 113.3 %collective-permute-start.49 = (bf16[512,2048]{1,0:T(8,128)(2,1)}, bf16[512,2048]{1,0:T(8,128)(2,1)}, u32[]{:S(2)}, u32[]{:S(2)}) collective-permute-start(bf16[512,2048]{1,0:T(8,128)(2,1)} %add_convert_fusion), channel_id=1, source_target_pairs={{0,1},{1,0},{2,3},{3,2},{4,5},{5,4},{6,7},{7,6},{8,9},{9,8},{10,11... | collective-permute-start | bytes 6291464 | tf_op jit(solution)/shard_map/ppermute | solution.py:257
  890.1 53.5 %collective-permute-start.90 = (bf16[256,768]{1,0:T(8,128)(2,1)}, bf16[256,768]{1,0:T(8,128)(2,1)}, u32[]{:S(2)}, u32[]{:S(2)}) collective-permute-start(bf16[256,768]{1,0:T(8,128)(2,1)} %get-tuple-element.211), channel_id=1, source_target_pairs={{0,16},{4,20},{8,24},{12,28},{16,0},{20,4},{24,8},{28,12},{1,17},{... | collective-permute-start | bytes 1179656 | tf_op jit(solution)/shard_map/ppermute | solution.py:366
  891.3 52.3 %collective-permute-start.88 = (bf16[256,768]{1,0:T(8,128)(2,1)}, bf16[256,768]{1,0:T(8,128)(2,1)}, u32[]{:S(2)}, u32[]{:S(2)}) collective-permute-start(bf16[256,768]{1,0:T(8,128)(2,1)} %get-tuple-element.212), channel_id=1, source_target_pairs={{0,8},{4,12},{8,16},{12,20},{16,24},{20,28},{24,0},{28,4},{1,9},{5... | collective-permute-start | bytes 1179656 | tf_op jit(solution)/shard_map/ppermute | solution.py:366
  911.4 65.9 %collective-permute-start.77 = (bf16[256,1536]{1,0:T(8,128)(2,1)}, bf16[256,1536]{1,0:T(8,128)(2,1)}, u32[]{:S(2)}, u32[]{:S(2)}) collective-permute-start(bf16[256,1536]{1,0:T(8,128)(2,1)} %get-tuple-element.175), channel_id=1, source_target_pairs={{0,16},{4,20},{8,24},{12,28},{16,0},{20,4},{24,8},{28,12},{1,17},{... | collective-permute-start | bytes 2359304 | tf_op jit(solution)/shard_map/ppermute | solution.py:366
  943.6 34.3 %collective-permute-start.75 = (bf16[256,1536]{1,0:T(8,128)(2,1)}, bf16[256,1536]{1,0:T(8,128)(2,1)}, u32[]{:S(2)}, u32[]{:S(2)}) collective-permute-start(bf16[256,1536]{1,0:T(8,128)(2,1)} %get-tuple-element.176), channel_id=1, source_target_pairs={{0,8},{4,12},{8,16},{12,20},{16,24},{20,28},{24,0},{28,4},{1,9},{5... | collective-permute-start | bytes 2359304 | tf_op jit(solution)/shard_map/ppermute | solution.py:366
  943.6 50.4 %collective-permute-start.78 = (bf16[256,1536]{1,0:T(8,128)(2,1)}, bf16[256,1536]{1,0:T(8,128)(2,1)}, u32[]{:S(2)}, u32[]{:S(2)}) collective-permute-start(bf16[256,1536]{1,0:T(8,128)(2,1)} %get-tuple-element.177), channel_id=1, source_target_pairs={{0,24},{4,28},{8,0},{12,4},{16,8},{20,12},{24,16},{28,20},{1,25},{... | collective-permute-start | bytes 2359304 | tf_op jit(solution)/shard_map/ppermute | solution.py:366
  977.9 33.6 %collective-permute-start.73 = (bf16[256,1536]{1,0:T(8,128)(2,1)}, bf16[256,1536]{1,0:T(8,128)(2,1)S(1)}, u32[]{:S(2)}, u32[]{:S(2)}) collective-permute-start(bf16[256,1536]{1,0:T(8,128)(2,1)} %get-tuple-element.164), channel_id=1, source_target_pairs={{0,24},{4,28},{8,0},{12,4},{16,8},{20,12},{24,16},{28,20},{1,25},{... | collective-permute-start | bytes 2359304 | tf_op jit(solution)/shard_map/ppermute | solution.py:366
  994.0 68.6 %collective-permute-start.71 = (bf16[256,1536]{1,0:T(8,128)(2,1)}, bf16[256,1536]{1,0:T(8,128)(2,1)S(1)}, u32[]{:S(2)}, u32[]{:S(2)}) collective-permute-start(bf16[256,1536]{1,0:T(8,128)(2,1)} %get-tuple-element.165), channel_id=1, source_target_pairs={{0,16},{4,20},{8,24},{12,28},{16,0},{20,4},{24,8},{28,12},{1,17},{... | collective-permute-start | bytes 2359304 | tf_op jit(solution)/shard_map/ppermute | solution.py:366
  994.0 68.6 %collective-permute-start.69 = (bf16[256,1536]{1,0:T(8,128)(2,1)}, bf16[256,1536]{1,0:T(8,128)(2,1)S(1)}, u32[]{:S(2)}, u32[]{:S(2)}) collective-permute-start(bf16[256,1536]{1,0:T(8,128)(2,1)} %get-tuple-element.166), channel_id=1, source_target_pairs={{0,8},{4,12},{8,16},{12,20},{16,24},{20,28},{24,0},{28,4},{1,9},{5... | collective-permute-start | bytes 2359304 | tf_op jit(solution)/shard_map/ppermute | solution.py:366
  998.5 97.8 %collective-permute-start.45 = (bf16[256,2048]{1,0:T(8,128)(2,1)S(1)}, bf16[256,2048]{1,0:T(8,128)(2,1)S(1)}, u32[]{:S(2)}, u32[]{:S(2)}) collective-permute-start(bf16[256,2048]{1,0:T(8,128)(2,1)S(1)} %dynamic-slice_convert_fusion.1), channel_id=1, source_target_pairs={{0,2},{1,3},{2,0},{3,1},{4,6},{5,7},{6,4},{7,5},{8,10},{9,11},{10,... | collective-permute-start | bytes 3145736 | tf_op jit(solution)/shard_map/ppermute | solution.py:263
  1001.8 95.7 %collective-permute-start.50 = (bf16[256,2048]{1,0:T(8,128)(2,1)S(1)}, bf16[256,2048]{1,0:T(8,128)(2,1)S(1)}, u32[]{:S(2)}, u32[]{:S(2)}) collective-permute-start(bf16[256,2048]{1,0:T(8,128)(2,1)S(1)} %dynamic-slice_convert_fusion), channel_id=1, source_target_pairs={{0,2},{1,3},{2,0},{3,1},{4,6},{5,7},{6,4},{7,5},{8,10},{9,11},{10,... | collective-permute-start | bytes 3145736 | tf_op jit(solution)/shard_map/ppermute | solution.py:263
  1011.5 120.2 %collective-permute-start.65 = (bf16[256,1536]{1,0:T(8,128)(2,1)S(1)}, bf16[256,1536]{1,0:T(8,128)(2,1)S(1)}, u32[]{:S(2)}, u32[]{:S(2)}) collective-permute-start(bf16[256,1536]{1,0:T(8,128)(2,1)S(1)} %copy-done.38), channel_id=1, source_target_pairs={{0,24},{4,28},{8,0},{12,4},{16,8},{20,12},{24,16},{28,20},{1,25},{... | collective-permute-start | bytes 2359304 | tf_op jit(solution)/shard_map/ppermute | solution.py:366
  1062.6 66.1 %collective-permute-start.64 = (bf16[256,1536]{1,0:T(8,128)(2,1)S(1)}, bf16[256,1536]{1,0:T(8,128)(2,1)S(1)}, u32[]{:S(2)}, u32[]{:S(2)}) collective-permute-start(bf16[256,1536]{1,0:T(8,128)(2,1)S(1)} %copy-done.42), channel_id=1, source_target_pairs={{0,16},{4,20},{8,24},{12,28},{16,0},{20,4},{24,8},{28,12},{1,17},{... | collective-permute-start | bytes 2359304 | tf_op jit(solution)/shard_map/ppermute | solution.py:366
  1062.6 69.0 %collective-permute-start.62 = (bf16[256,1536]{1,0:T(8,128)(2,1)S(1)}, bf16[256,1536]{1,0:T(8,128)(2,1)S(1)}, u32[]{:S(2)}, u32[]{:S(2)}) collective-permute-start(bf16[256,1536]{1,0:T(8,128)(2,1)S(1)} %copy-done.39), channel_id=1, source_target_pairs={{0,8},{4,12},{8,16},{12,20},{16,24},{20,28},{24,0},{28,4},{1,9},{5... | collective-permute-start | bytes 2359304 | tf_op jit(solution)/shard_map/ppermute | solution.py:366
  1128.7 38.2 %collective-permute-start.48 = (bf16[512,2048]{1,0:T(8,128)(2,1)}, bf16[512,2048]{1,0:T(8,128)(2,1)}, u32[]{:S(2)}, u32[]{:S(2)}) collective-permute-start(bf16[512,2048]{1,0:T(8,128)(2,1)} %pad_maximum_fusion.11), channel_id=1, source_target_pairs={{0,1},{1,0},{2,3},{3,2},{4,5},{5,4},{6,7},{7,6},{8,9},{9,8},{10,11... | collective-permute-start | bytes 6291464 | tf_op jit(solution)/shard_map/ppermute | solution.py:281
  1148.6 49.4 %collective-permute-start.52 = (bf16[512,2048]{1,0:T(8,128)(2,1)}, bf16[512,2048]{1,0:T(8,128)(2,1)}, u32[]{:S(2)}, u32[]{:S(2)}) collective-permute-start(bf16[512,2048]{1,0:T(8,128)(2,1)} %pad_maximum_fusion.12), channel_id=1, source_target_pairs={{0,1},{1,0},{2,3},{3,2},{4,5},{5,4},{6,7},{7,6},{8,9},{9,8},{10,11... | collective-permute-start | bytes 6291464 | tf_op jit(solution)/shard_map/ppermute | solution.py:281
  1161.6 34.6 %collective-permute-start.57 = (bf16[256,768]{1,0:T(8,128)(2,1)}, bf16[256,768]{1,0:T(8,128)(2,1)S(1)}, u32[]{:S(2)}, u32[]{:S(2)}) collective-permute-start(bf16[256,768]{1,0:T(8,128)(2,1)} %get-tuple-element.204), channel_id=1, source_target_pairs={{0,16},{4,20},{8,24},{12,28},{16,0},{20,4},{24,8},{28,12},{1,17},{... | collective-permute-start | bytes 1179656 | tf_op jit(solution)/shard_map/ppermute | solution.py:366
  1165.2 31.0 %collective-permute-start.55 = (bf16[256,768]{1,0:T(8,128)(2,1)S(1)}, bf16[256,768]{1,0:T(8,128)(2,1)S(1)}, u32[]{:S(2)}, u32[]{:S(2)}) collective-permute-start(bf16[256,768]{1,0:T(8,128)(2,1)S(1)} %get-tuple-element.205), channel_id=1, source_target_pairs={{0,8},{4,12},{8,16},{12,20},{16,24},{20,28},{24,0},{28,4},{1,9},{5... | collective-permute-start | bytes 1179656 | tf_op jit(solution)/shard_map/ppermute | solution.py:366
  (117 other events, 2319.1 us)

commit v2 on v1

--- a/solution.py
+++ b/solution.py
@@ -296,33 +296,71 @@
     ]
 
 
+def moves(pairs, inner):
+    return [(a * inner + x, b * inner + x) for a, b in pairs for x in range(inner)]
+
+
 def line_send(shard, inner, outer):
-    arrived = [
-        lax.ppermute(shard, "dp", outer_route(step, inner, outer))
-        for step in range(1, outer)
+    if outer != 4:
+        return tuple(
+            lax.ppermute(shard, "dp", outer_route(step, inner, outer))
+            for step in range(1, outer)
+        )
+    routes = (((0, 1), (1, 2), (2, 3)), ((1, 0), (2, 1), (3, 2)), ((0, 2), (3, 1)))
+    return tuple(lax.ppermute(shard, "dp", moves(route, inner)) for route in routes)
+
+
+def own_send(shard, inner, outer):
+    return lax.ppermute(shard, "dp", swap_pairs(inner * outer, 1))
+
+
+def line_relay(arrived, inner, outer):
+    if outer != 4:
+        return ()
+    below, above, beyond = arrived
+    return (
+        lax.ppermute(below, "dp", moves(((2, 3),), inner)),
+        lax.ppermute(above, "dp", moves(((1, 0),), inner)),
+        lax.ppermute(beyond, "dp", moves(((2, 3), (1, 0)), inner)),
+    )
+
+
+def line_parts(arrived, relayed, rank, inner, outer):
+    place = rank // inner
+    if outer != 4:
+        return arrived, [lax.rem(place + outer - step, outer) for step in range(1, outer)]
+    below, above, beyond = arrived
+    first, last = place == 0, place == 3
+    ends = first | last
+    parts = (
+        jnp.where(first, above, below),
+        jnp.where(first, relayed[1], jnp.where(last, relayed[0], above)),
+        jnp.where(ends, relayed[2], beyond),
+    )
+    places = [
+        jnp.where(first, 1, place - 1),
+        jnp.where(first, 2, jnp.where(last, 1, place + 1)),
+        jnp.where(place < 2, 3, 0),
     ]
-    return arrived, lax.ppermute(shard, "dp", swap_pairs(inner * outer, 1))
-
-
-def pair_send(arrived, inner, outer):
-    return [lax.ppermute(part, "dp", swap_pairs(inner * outer, 1)) for part in arrived]
-
-
-def line_join(shard, arrived, rank, inner, outer):
-    place = rank // inner
+    return parts, places
+
+
+def pair_send(parts, inner, outer):
+    return tuple(lax.ppermute(part, "dp", swap_pairs(inner * outer, 1)) for part in parts)
+
+
+def line_join(shard, parts, places, rank, inner, outer):
     line = lax.dynamic_update_slice_in_dim(
-        jnp.zeros((outer,) + shard.shape, shard.dtype), shard[None], place, 0
-    )
-    for step in range(1, outer):
-        line = lax.dynamic_update_slice_in_dim(
-            line, arrived[step - 1][None], lax.rem(place + outer - step, outer), 0
-        )
+        jnp.zeros((outer,) + shard.shape, shard.dtype), shard[None], rank // inner, 0
+    )
+    for part, which in zip(parts, places):
+        line = lax.dynamic_update_slice_in_dim(line, part[None], which, 0)
     return line
 
 
-def in_order(shard, arrived, partner, passed, rank, inner, outer):
-    line = line_join(shard, arrived, rank, inner, outer)
-    other = line_join(partner, passed, rank, inner, outer)
+def in_order(shard, parts, places, partner, passed, rank, inner, outer):
+    line = line_join(shard, parts, places, rank, inner, outer)
+    other = line_join(partner, passed, places, rank, inner, outer)
     side = rank % inner
     return jnp.where(side == 0, line, other), jnp.where(side == 0, other, line)
 
@@ -408,11 +446,26 @@
     ring = (data_rank, inner, outer)
     sizes = (inner, outer)
     shard_in = jnp.concatenate([query_weight, key_matrix, value_matrix, gate_weight], axis=1)
-    z_in, w_in = line_send(shard_in, *sizes)
-    z_o, w_o = line_send(out_weight, *sizes)
-    z_gf, w_gf = line_send(ffn_gate_weight, *sizes)
-    z_up, w_up = line_send(ffn_up_weight, *sizes)
-    z_dn, w_dn = line_send(ffn_down_weight, *sizes)
+    held = (
+        ("in", shard_in),
+        ("o", out_weight),
+        ("gf", ffn_gate_weight),
+        ("up", ffn_up_weight),
+        ("dn", ffn_down_weight),
+    )
+    near = {name: line_send(shard, *sizes) for name, shard in held}
+    owned = {name: own_send(shard, *sizes) for name, shard in held}
+
+    def pass_on(name, *earlier):
+        arrived = after(near[name], *earlier)
+        parts, places = line_parts(arrived, line_relay(arrived, *sizes), *ring)
+        return parts, places, pair_send(parts, *sizes)
+
+    def ordered(name, shard, gathered, *earlier):
+        parts, places, passed = gathered
+        return in_order(
+            shard, after(parts, *earlier), places, owned[name], after(passed, *earlier), *ring
+        )
 
     flat_input = layer_input.reshape(tokens, width)
     grad_low = cotangent.reshape(tokens, width)
@@ -425,11 +478,11 @@
 
     cosine_table, sine_table = jax.vmap(lambda row: tables(row, head_size))(segments)
     first_normed = (norm_fwd(flat_input.astype(wide_type))[0] * attn_gain).astype(low_type)
-    x_in = pair_send(z_in, *sizes)
-    x_o = pair_send(z_o, *sizes)
-    full_in = join_rows(in_order(shard_in, z_in, w_in, x_in, *ring))
+    got_in = pass_on("in")
+    got_o = pass_on("o")
+    got_gf = pass_on("gf")
+    full_in = join_rows(ordered("in", shard_in, got_in))
     projected = matmul(first_normed, full_in)
-    x_gf = pair_send(after(tuple(z_gf), projected), *sizes)
     attend, attend_back = attention_calls(seqs, token_length, head_size, group_width, heads_kv)
     attend_args = (
         projected,
@@ -444,33 +497,26 @@
         key_norm_gain[None],
     )
     gated = attend(*attend_args)
-    full_o = join_columns(
-        in_order(
-            out_weight, after(tuple(z_o), projected), w_o, after(tuple(x_o), projected), *ring
-        )
-    )
-    x_up = pair_send(after(tuple(z_up), gated), *sizes)
+    full_o = join_columns(ordered("o", out_weight, got_o, projected))
+    got_up = pass_on("up", gated)
     branch_one = tensor_scatter(
         lambda rows: matmul(rows, full_o), (gated,), tensor_rank, tensor_size
     )
     middle = share_input + branch_one
     normal_two, inv_two = norm_fwd(middle)
-    second_normed = tensor_gather(
-        (normal_two * ffn_gain).astype(low_type), tensor_rank, tensor_size
-    )
-    full_gf = join_rows(in_order(ffn_gate_weight, z_gf, w_gf, after(tuple(x_gf), second_normed), *ring))
+    second_share = (normal_two * ffn_gain).astype(low_type)
+    second_normed = tensor_gather(second_share, tensor_rank, tensor_size)
+    got_dn = pass_on("dn", second_share)
+    full_gf = join_rows(ordered("gf", ffn_gate_weight, got_gf, second_normed))
     ffn_gate = matmul(second_normed, full_gf)
-    full_up = join_rows(in_order(ffn_up_weight, z_up, w_up, after(tuple(x_up), ffn_gate), *ring))
+    full_up = join_rows(ordered("up", ffn_up_weight, got_up, ffn_gate))
     ffn_up = matmul(second_normed, full_up)
     sig_gate = jax.nn.sigmoid(ffn_gate)
     active = ffn_gate * sig_gate
     hidden = (active * ffn_up).astype(low_type)
-    x_dn = pair_send(after(tuple(z_dn), hidden), *sizes)
     weight_dn = matmul_tn(grad_low, hidden).astype(low_type)
     blocks_dn, pair_dn = scatter_send(weight_dn, *ring)
-    full_dn = join_columns(
-        in_order(ffn_down_weight, z_dn, w_dn, after(tuple(x_dn), weight_dn), *ring)
-    )
+    full_dn = join_columns(ordered("dn", ffn_down_weight, got_dn, weight_dn))
     grad_hidden = matmul_nt(grad_low, full_dn)
     grad_ffn_gate = (grad_hidden * ffn_up * sig_gate * (1.0 + ffn_gate * (1.0 - sig_gate))).astype(
         low_type

time: 1220 us -> 1190 us (0.975)
  starting transfers between devices: 240 us -> 172 us
  waiting for transfers between devices: 601 us -> 625 us
    ppermute x20 -> x35, waiting for transfers between devices: 119 us -> 188 us  [the longest x5 90.3 us: line_relay(): lax.ppermute(above, 'dp', moves(((1, 0),), inner))]
    ppermute x20 -> x35, starting transfers between devices: 105 us -> 61.4 us  [the longest x15 38.8 us: line_send(): lax.ppermute(shard, 'dp', moves(route, inner))]
    ppermute x15, waiting for transfers between devices: 133 us -> 96.2 us  [pair_send(): lax.ppermute(part, 'dp', swap_pairs(inner * outer, 1))]
    ppermute x18, waiting for transfers between devices: 135 us -> 166 us  [scatter_line(): lax.ppermute(part, 'dp', outer_route(step + 1, inner, outer))]
    ppermute x18, starting transfers between devices: 89.3 us -> 64.9 us  [scatter_line(): lax.ppermute(part, 'dp', outer_route(step + 1, inner, outer))]
    ppermute x24, waiting for transfers between devices: 162 us -> 138 us  [scatter_send(): received.append(lax.ppermute(sent, 'dp', swap_pairs(inner * outer, 1)))]
    ppermute x8, waiting for transfers between devices: 30.5 us -> 17 us  [tensor_gather(): received = lax.ppermute(share, 'tensor', swap_pairs(size, bit))]
    dynamic_update_slice x29 -> x26, local copies, waits for them, and re-layouts: 24.8 us -> 19 us  [line_join(): line = lax.dynamic_update_slice_in_dim(line, part[None], which, 0)]
  transfers between devices with their start and end apart: 98 -> 113, of which waited for: 43 -> 50; matrix products, arithmetic and copies ran while one was open for 19% -> 20% of each run, Pallas kernels for 4% -> 3%
where the time goes in v2:
time: 1190 us; the launch traced here: 1180 us
  waiting for transfers between devices  625 us (53%)
  starting transfers between devices  172 us (14%)
  matrix products  144 us (12%)
  other arithmetic  101 us (8%)
  local copies, waits for them, and re-layouts  84.7 us (7%)
  Pallas kernels  47.3 us (4%)
    ppermute x18, waiting for transfers between devices, scatter_line(): lax.ppermute(part, 'dp', outer_route(step + 1, inner, outer))  166 us
    ppermute x24, waiting for transfers between devices, scatter_send(): received.append(lax.ppermute(sent, 'dp', swap_pairs(inner * outer, 1)))  138 us
    ppermute x15, waiting for transfers between devices, pair_send(): lax.ppermute(part, 'dp', swap_pairs(inner * outer, 1))  96.2 us
    ppermute x5, waiting for transfers between devices, line_relay(): lax.ppermute(above, 'dp', moves(((1, 0),), inner))  90.3 us
    ppermute x18, starting transfers between devices, scatter_line(): lax.ppermute(part, 'dp', outer_route(step + 1, inner, outer))  64.9 us
    dot_general x10, matrix products, matmul_nt(): jnp.einsum('tf,df->td', left, right, preferred_element_type=wide_type)  57.3 us
    dot_general x7, matrix products, matmul(): return jnp.dot(left, right, preferred_element_type=wide_type)  49 us
    ppermute x5, waiting for transfers between devices, line_relay(): lax.ppermute(beyond, 'dp', moves(((2, 3), (1, 0)), inner))  44.2 us
  transfers between devices with their start and end apart: 113, of which 50 were waited for; matrix products, arithmetic and copies ran while one was open for 20% of the time, Pallas kernels for 3%

profile of v2, /device:TPU:0, one launch (start us, length us, event | category | flops | bytes accessed | tf_op | source)
XLA Modules:
  0.0 1178.1 jit_solution(1566885491491013675)
XLA Ops:
  8.4 6.5 collective-permute-start.1
  16.2 5.3 collective-permute-start.11
  38.5 5.3 collective-permute-start.14
  57.9 5.4 collective-permute-done.15
  73.5 14.6 %collective-permute-done.2 = bf16[256,1536]{1,0:T(8,128)(2,1)S(1)} collective-permute-done((bf16[256,1536]{1,0:T(8,128)(2,1)}, bf16[256,1536]{1,0:T(8,128)(2,1)S(1)}, u32[]{:S(2)}, u32[]{:S(2)}) %collective-permute-start.2) | collective-permute-done | bytes 786464 | tf_op jit(solution)/shard_map/ppermute | solution.py:323
  91.5 8.9 collective-permute-done.5
  101.1 9.2 collective-permute-done.7
  110.9 16.3 %collective-permute-done.8 = bf16[256,1536]{1,0:T(8,128)(2,1)S(1)} collective-permute-done((bf16[256,1536]{1,0:T(8,128)(2,1)S(1)}, bf16[256,1536]{1,0:T(8,128)(2,1)S(1)}, u32[]{:S(2)}, u32[]{:S(2)}) %collective-permute-start.8) | collective-permute-done | bytes 786464 | tf_op jit(solution)/shard_map/ppermute | solution.py:349
  127.3 11.0 collective-permute-done.9
  142.5 8.5 fusion.108.q_ref.k_ref.v_ref.g_ref
  159.7 17.4 %shard_map.254 = bf16[1024,512]{1,0:T(8,128)(2,1)} custom-call(f32[1024,1536]{1,0:T(8,128)} %fusion.108.q_ref.k_ref.v_ref.g_ref, f32[1024,1536]{1,0:T(8,128)} %fusion.108.q_ref.k_ref.v_ref.g_ref, f32[1024,1536]{1,0:T(8,128)} %fusion.108.q_ref.k_ref.v_ref.g_ref, f32[1024,1536]{1,0:T(8,128)} %fusion.108.q_ref.k_ref.v_ref.g_ref, ...), custom_call_target="tpu_custom_call" | custom-call | tf_op jit(solution)/shard_map/pallas_call | solution.py:499
  182.1 5.5 collective-permute-start.25
  198.5 9.8 collective-permute-done.30
  211.3 13.8 %collective-permute-done.40 = bf16[256,1536]{1,0:T(8,128)(2,1)S(1)} collective-permute-done((bf16[256,1536]{1,0:T(8,128)(2,1)}, bf16[256,1536]{1,0:T(8,128)(2,1)S(1)}, u32[]{:S(2)}, u32[]{:S(2)}) %collective-permute-start.40) | collective-permute-done | bytes 786464 | tf_op jit(solution)/shard_map/ppermute | solution.py:314
  226.9 14.0 %collective-permute-done.50 = bf16[1536,256]{1,0:T(8,128)(2,1)S(1)} collective-permute-done((bf16[1536,256]{1,0:T(8,128)(2,1)S(1)}, bf16[1536,256]{1,0:T(8,128)(2,1)S(1)}, u32[]{:S(2)}, u32[]{:S(2)}) %collective-permute-start.50) | collective-permute-done | bytes 786464 | tf_op jit(solution)/shard_map/ppermute | solution.py:314
  249.9 32.0 %collective-permute-done.26 = bf16[256,1536]{1,0:T(8,128)(2,1)S(1)} collective-permute-done((bf16[256,1536]{1,0:T(8,128)(2,1)}, bf16[256,1536]{1,0:T(8,128)(2,1)S(1)}, u32[]{:S(2)}, u32[]{:S(2)}) %collective-permute-start.26) | collective-permute-done | bytes 786464 | tf_op jit(solution)/shard_map/ppermute | solution.py:323
  284.9 12.0 %collective-permute-done.29 = bf16[256,1536]{1,0:T(8,128)(2,1)S(1)} collective-permute-done((bf16[256,1536]{1,0:T(8,128)(2,1)S(1)}, bf16[256,1536]{1,0:T(8,128)(2,1)S(1)}, u32[]{:S(2)}, u32[]{:S(2)}) %collective-permute-start.29) | collective-permute-done | bytes 786464 | tf_op jit(solution)/shard_map/ppermute | solution.py:324
  304.2 14.3 %collective-permute-done.48 = bf16[1536,256]{1,0:T(8,128)(2,1)S(1)} collective-permute-done((bf16[1536,256]{1,0:T(8,128)(2,1)S(1)}, bf16[1536,256]{1,0:T(8,128)(2,1)S(1)}, u32[]{:S(2)}, u32[]{:S(2)}) %collective-permute-start.48) | collective-permute-done | bytes 786464 | tf_op jit(solution)/shard_map/ppermute | solution.py:310
  321.8 32.5 %collective-permute-done.36 = bf16[256,1536]{1,0:T(8,128)(2,1)S(1)} collective-permute-done((bf16[256,1536]{1,0:T(8,128)(2,1)S(1)}, bf16[256,1536]{1,0:T(8,128)(2,1)S(1)}, u32[]{:S(2)}, u32[]{:S(2)}) %collective-permute-start.36) | collective-permute-done | bytes 786464 | tf_op jit(solution)/shard_map/ppermute | solution.py:323
  358.6 18.0 %collective-permute-done.49 = bf16[1536,256]{1,0:T(8,128)(2,1)S(1)} collective-permute-done((bf16[1536,256]{1,0:T(8,128)(2,1)S(1)}, bf16[1536,256]{1,0:T(8,128)(2,1)S(1)}, u32[]{:S(2)}, u32[]{:S(2)}) %collective-permute-start.49) | collective-permute-done | bytes 786464 | tf_op jit(solution)/shard_map/ppermute | solution.py:324
  379.6 9.7 collective-permute-done.46
  397.8 16.0 %collective-permute-done.33 = bf16[256,1536]{1,0:T(8,128)(2,1)S(1)} collective-permute-done((bf16[256,1536]{1,0:T(8,128)(2,1)S(1)}, bf16[256,1536]{1,0:T(8,128)(2,1)S(1)}, u32[]{:S(2)}, u32[]{:S(2)}) %collective-permute-start.33) | collective-permute-done | bytes 786464 | tf_op jit(solution)/shard_map/ppermute | solution.py:349
  416.2 13.5 %fusion.104 = f32[1024,1536]{1,0:T(8,128)} fusion(bf16[2048,1536]{1,0:T(8,128)(2,1)S(1)} %bitcast.363, bf16[512,2048]{1,0:T(8,128)(2,1)} %get-tuple-element.215, bf16[512,2048]{1,0:T(8,128)(2,1)} %get-tuple-element.214), kind=kOutput, calls=%fused_computation.328 | convolution fusion | flops 6450839552 | bytes 16777216 | tf_op jit(solution)/shard_map/dot_general | solution.py:224
  431.3 16.4 %collective-permute-done.42 = bf16[256,1536]{1,0:T(8,128)(2,1)} collective-permute-done((bf16[256,1536]{1,0:T(8,128)(2,1)S(1)}, bf16[256,1536]{1,0:T(8,128)(2,1)}, u32[]{:S(2)}, u32[]{:S(2)}) %collective-permute-start.42) | collective-permute-done | bytes 786464 | tf_op jit(solution)/shard_map/ppermute | solution.py:349
  447.6 16.9 %collective-permute-done.41 = bf16[256,1536]{1,0:T(8,128)(2,1)} collective-permute-done((bf16[256,1536]{1,0:T(8,128)(2,1)S(1)}, bf16[256,1536]{1,0:T(8,128)(2,1)}, u32[]{:S(2)}, u32[]{:S(2)}) %collective-permute-start.41) | collective-permute-done | bytes 786464 | tf_op jit(solution)/shard_map/ppermute | solution.py:349
  470.3 12.3 %multiply_convert_fusion.1 = (bf16[1024,1536]{1,0:T(8,128)(2,1)S(1)}, f32[1024,1536]{1,0:T(8,128)}) fusion(f32[1024,1536]{1,0:T(8,128)} %fusion.104, bf16[2048,1536]{1,0:T(8,128)(2,1)S(1)} %bitcast.368, bf16[512,2048]{1,0:T(8,128)(2,1)} %get-tuple-element.215, bf16[512,2048]{1,0:T(8,128)(2,1)S(1)} %copy-done.33), kind=kOutput, calls=%fused_computation.19 | convolution fusion | flops 6460276736 | bytes 26214400 | tf_op jit(solution)/shard_map/dot_general | solution.py:224
  484.2 8.7 fusion.3
  492.9 9.0 copy.36
  502.0 8.8 collective-permute-done.53
  526.6 15.5 %fusion.7 = (bf16[1024,1536]{1,0:T(8,128)(2,1)}, bf16[1024,1536]{1,0:T(8,128)(2,1)}) fusion(f32[1024,1536]{1,0:T(8,128)} %fusion.104, f32[1024,1536]{1,0:T(8,128)} %get-tuple-element.268, bf16[1536,2048]{1,0:T(8,128)(2,1)} %copy-done.61, bf16[1024,2048]{1,0:T(8,128)(2,1)S(1)} %bitcast.391), kind=kOutput, calls=%fused_computation.18 | convolution fusion | flops 6462898176 | bytes 29360128 | tf_op jit(solution)/shard_map/tf,df->td/dot_general | solution.py:228
  542.2 6.6 fusion.45
  548.8 6.5 add_convert_fusion.1
  564.3 5.8 convolution_add_fusion.1
  572.3 9.1 convolution_convert_fusion.1
  581.5 12.9 %collective-permute-done.76 = bf16[256,1536]{1,0:T(8,128)(2,1)} collective-permute-done((bf16[256,1536]{1,0:T(8,128)(2,1)}, bf16[256,1536]{1,0:T(8,128)(2,1)}, u32[]{:S(2)}, u32[]{:S(2)}) %collective-permute-start.76) | collective-permute-done | bytes 786464 | tf_op jit(solution)/shard_map/ppermute | solution.py:386
  594.4 16.4 %collective-permute-done.78 = bf16[256,1536]{1,0:T(8,128)(2,1)} collective-permute-done((bf16[256,1536]{1,0:T(8,128)(2,1)S(1)}, bf16[256,1536]{1,0:T(8,128)(2,1)}, u32[]{:S(2)}, u32[]{:S(2)}) %collective-permute-start.78) | collective-permute-done | bytes 786464 | tf_op jit(solution)/shard_map/ppermute | solution.py:386
  618.9 7.6 convolution_convert_fusion
  626.5 16.6 %collective-permute-done.57 = bf16[256,2048]{1,0:T(8,128)(2,1)S(1)} collective-permute-done((bf16[256,2048]{1,0:T(8,128)(2,1)S(1)}, bf16[256,2048]{1,0:T(8,128)(2,1)S(1)}, u32[]{:S(2)}, u32[]{:S(2)}) %collective-permute-start.57) | collective-permute-done | bytes 1048608 | tf_op jit(solution)/shard_map/ppermute | solution.py:281
  650.2 14.0 %collective-permute-done.75 = bf16[256,1536]{1,0:T(8,128)(2,1)S(1)} collective-permute-done((bf16[256,1536]{1,0:T(8,128)(2,1)}, bf16[256,1536]{1,0:T(8,128)(2,1)S(1)}, u32[]{:S(2)}, u32[]{:S(2)}) %collective-permute-start.75) | collective-permute-done | bytes 786464 | tf_op jit(solution)/shard_map/ppermute | solution.py:386
  664.8 16.3 %collective-permute-done.61 = bf16[256,1536]{1,0:T(8,128)(2,1)S(1)} collective-permute-done((bf16[256,1536]{1,0:T(8,128)(2,1)S(1)}, bf16[256,1536]{1,0:T(8,128)(2,1)S(1)}, u32[]{:S(2)}, u32[]{:S(2)}) %collective-permute-start.61) | collective-permute-done | bytes 786464 | tf_op jit(solution)/shard_map/ppermute | solution.py:386
  681.6 16.3 %collective-permute-done.89 = bf16[256,1536]{1,0:T(8,128)(2,1)S(1)} collective-permute-done((bf16[256,1536]{1,0:T(8,128)(2,1)S(1)}, bf16[256,1536]{1,0:T(8,128)(2,1)S(1)}, u32[]{:S(2)}, u32[]{:S(2)}) %collective-permute-start.89) | collective-permute-done | bytes 786464 | tf_op jit(solution)/shard_map/ppermute | solution.py:386
  698.5 16.3 %collective-permute-done.91 = bf16[256,1536]{1,0:T(8,128)(2,1)S(1)} collective-permute-done((bf16[256,1536]{1,0:T(8,128)(2,1)S(1)}, bf16[256,1536]{1,0:T(8,128)(2,1)S(1)}, u32[]{:S(2)}, u32[]{:S(2)}) %collective-permute-start.91) | collective-permute-done | bytes 786464 | tf_op jit(solution)/shard_map/ppermute | solution.py:386
  723.9 23.2 %shard_map.255 = (bf16[1024,512]{1,0:T(8,128)(2,1)}, bf16[1024,256]{1,0:T(8,128)(2,1)}, bf16[1024,256]{1,0:T(8,128)(2,1)}, bf16[1024,512]{1,0:T(8,128)(2,1)}, f32[2,2,2,128]{3,2,1,0:T(2,128)}) custom-call(f32[1024,1536]{1,0:T(8,128)} %fusion.108.q_ref.k_ref.v_ref.g_ref, f32[1024,1536]{1,0:T(8,128)} %fusion.108.q_ref.k_ref.v_ref.g_ref, ...), custom_call_target="tpu_custom_call" | custom-call | tf_op jit(solution)/shard_map/pallas_call | solution.py:545
  753.5 5.2 add_convert_fusion
  769.7 5.5 convolution_convert_fusion.4
  775.3 7.1 collective-permute-done.87
  791.7 5.1 fusion.42
  802.7 6.1 collective-permute-done.68
  819.3 6.4 collective-permute-done.71
  827.2 6.9 collective-permute-done.73
  837.1 5.4 collective-permute-done.102
  845.4 5.5 collective-permute-done.104
  852.4 6.9 collective-permute-done.106
  863.6 6.6 collective-permute-done.97
  872.3 38.6 %collective-permute-done.99 = bf16[256,512]{1,0:T(8,128)(2,1)S(1)} collective-permute-done((bf16[256,512]{1,0:T(8,128)(2,1)S(1)}, bf16[256,512]{1,0:T(8,128)(2,1)S(1)}, u32[]{:S(2)}, u32[]{:S(2)}) %collective-permute-start.99) | collective-permute-done | bytes 262176 | tf_op jit(solution)/shard_map/ppermute | solution.py:404
  926.6 27.7 %collective-permute-done.103 = bf16[256,768]{1,0:T(8,128)(2,1)S(1)} collective-permute-done((bf16[256,768]{1,0:T(8,128)(2,1)S(1)}, bf16[256,768]{1,0:T(8,128)(2,1)S(1)}, u32[]{:S(2)}, u32[]{:S(2)}) %collective-permute-start.103) | collective-permute-done | bytes 393248 | tf_op jit(solution)/shard_map/ppermute | solution.py:404
  956.0 18.6 %collective-permute-done.105 = bf16[256,768]{1,0:T(8,128)(2,1)} collective-permute-done((bf16[256,768]{1,0:T(8,128)(2,1)S(1)}, bf16[256,768]{1,0:T(8,128)(2,1)}, u32[]{:S(2)}, u32[]{:S(2)}) %collective-permute-start.105) | collective-permute-done | bytes 393248 | tf_op jit(solution)/shard_map/ppermute | solution.py:404
  981.3 6.4 collective-permute-start.84
  997.1 11.6 collective-permute-done.84
  1010.5 30.6 %collective-permute-done.86 = bf16[256,1536]{1,0:T(8,128)(2,1)S(1)} collective-permute-done((bf16[256,1536]{1,0:T(8,128)(2,1)}, bf16[256,1536]{1,0:T(8,128)(2,1)S(1)}, u32[]{:S(2)}, u32[]{:S(2)}) %collective-permute-start.86) | collective-permute-done | bytes 786464 | tf_op jit(solution)/shard_map/ppermute | solution.py:404
  1041.1 31.4 %collective-permute-start.77 = (bf16[256,1536]{1,0:T(8,128)(2,1)}, bf16[256,1536]{1,0:T(8,128)(2,1)S(1)}, u32[]{:S(2)}, u32[]{:S(2)}) collective-permute-start(bf16[256,1536]{1,0:T(8,128)(2,1)} %get-tuple-element.197), channel_id=1, source_target_pairs={{0,8},{4,12},{8,16},{12,20},{16,24},{20,28},{24,0},{28,4},{1,9},{5... | collective-permute-start | bytes 2359304 | tf_op jit(solution)/shard_map/ppermute | solution.py:404
  1082.6 18.8 %collective-permute-done.109 = f32[4352]{0:T(1024)S(1)} collective-permute-done((f32[4352]{0:T(1024)S(1)}, f32[4352]{0:T(1024)S(1)}, u32[]{:S(2)}, u32[]{:S(2)}) %collective-permute-start.109) | collective-permute-done | bytes 17440 | tf_op jit(solution)/shard_map/ppermute | solution.py:595
  1108.3 17.0 %collective-permute-done.79 = bf16[256,1536]{1,0:T(8,128)(2,1)S(1)} collective-permute-done((bf16[256,1536]{1,0:T(8,128)(2,1)S(1)}, bf16[256,1536]{1,0:T(8,128)(2,1)S(1)}, u32[]{:S(2)}, u32[]{:S(2)}) %collective-permute-start.79) | collective-permute-done | bytes 786464 | tf_op jit(solution)/shard_map/ppermute | solution.py:404
  1152.9 15.4 %collective-permute-done.72 = bf16[256,768]{1,0:T(8,128)(2,1)S(1)} collective-permute-done((bf16[256,768]{1,0:T(8,128)(2,1)}, bf16[256,768]{1,0:T(8,128)(2,1)S(1)}, u32[]{:S(2)}, u32[]{:S(2)}) %collective-permute-start.72) | collective-permute-done | bytes 393248 | tf_op jit(solution)/shard_map/ppermute | solution.py:404
  (552 shorter events, 338.3 us)
Async XLA Ops:
  7.1 58.4 %collective-permute-start = (bf16[256,1536]{1,0:T(8,128)(2,1)}, bf16[256,1536]{1,0:T(8,128)(2,1)}, u32[]{:S(2)}, u32[]{:S(2)}) collective-permute-start(bf16[256,1536]{1,0:T(8,128)(2,1)} %constant_dynamic-update-slice_fusion), channel_id=1, source_target_pairs={{8,0},{12,4},{16,8},{20,12},{24,16},{28,20},{9,1},{13,5},{17,9},{2... | collective-permute-start | bytes 2359304 | tf_op jit(solution)/shard_map/ppermute | solution.py:310
  8.4 58.4 %collective-permute-start.1 = (bf16[256,1536]{1,0:T(8,128)(2,1)}, bf16[256,1536]{1,0:T(8,128)(2,1)}, u32[]{:S(2)}, u32[]{:S(2)}) collective-permute-start(bf16[256,1536]{1,0:T(8,128)(2,1)} %constant_dynamic-update-slice_fusion), channel_id=1, source_target_pairs={{0,8},{4,12},{8,16},{12,20},{16,24},{20,28},{1,9},{5,13},{9,17},{1... | collective-permute-start | bytes 2359304 | tf_op jit(solution)/shard_map/ppermute | solution.py:310
  63.3 87.8 %collective-permute-start.18 = (bf16[512,256]{1,0:T(8,128)(2,1)S(1)}, bf16[512,256]{1,0:T(8,128)(2,1)}, u32[]{:S(2)}, u32[]{:S(2)}) collective-permute-start(bf16[512,256]{1,0:T(8,128)(2,1)S(1)} %get-tuple-element.87), channel_id=1, source_target_pairs={{0,4},{4,0},{8,12},{12,8},{16,20},{20,16},{24,28},{28,24},{1,5},{5... | collective-permute-start | bytes 786440 | tf_op jit(solution)/shard_map/ppermute | solution.py:349
  70.9 80.2 %collective-permute-start.17 = (bf16[512,256]{1,0:T(8,128)(2,1)}, bf16[512,256]{1,0:T(8,128)(2,1)}, u32[]{:S(2)}, u32[]{:S(2)}) collective-permute-start(bf16[512,256]{1,0:T(8,128)(2,1)} %get-tuple-element.86), channel_id=1, source_target_pairs={{0,4},{4,0},{8,12},{12,8},{16,20},{20,16},{24,28},{28,24},{1,5},{5... | collective-permute-start | bytes 786440 | tf_op jit(solution)/shard_map/ppermute | solution.py:349
  88.0 63.0 %collective-permute-start.19 = (bf16[512,256]{1,0:T(8,128)(2,1)}, bf16[512,256]{1,0:T(8,128)(2,1)}, u32[]{:S(2)}, u32[]{:S(2)}) collective-permute-start(bf16[512,256]{1,0:T(8,128)(2,1)} %broadcast_select_fusion.28), channel_id=1, source_target_pairs={{0,4},{4,0},{8,12},{12,8},{16,20},{20,16},{24,28},{28,24},{1,5},{5... | collective-permute-start | bytes 786440 | tf_op jit(solution)/shard_map/ppermute | solution.py:349
  180.8 61.7 %collective-permute-start.24 = (bf16[256,1536]{1,0:T(8,128)(2,1)}, bf16[256,1536]{1,0:T(8,128)(2,1)}, u32[]{:S(2)}, u32[]{:S(2)}) collective-permute-start(bf16[256,1536]{1,0:T(8,128)(2,1)} %param.22), channel_id=1, source_target_pairs={{8,0},{12,4},{16,8},{20,12},{24,16},{28,20},{9,1},{13,5},{17,9},{2... | collective-permute-start | bytes 2359304 | tf_op jit(solution)/shard_map/ppermute | solution.py:310
  182.1 61.7 %collective-permute-start.25 = (bf16[256,1536]{1,0:T(8,128)(2,1)}, bf16[256,1536]{1,0:T(8,128)(2,1)}, u32[]{:S(2)}, u32[]{:S(2)}) collective-permute-start(bf16[256,1536]{1,0:T(8,128)(2,1)} %param.22), channel_id=1, source_target_pairs={{0,8},{4,12},{8,16},{12,20},{16,24},{20,28},{1,9},{5,13},{9,17},{1... | collective-permute-start | bytes 2359304 | tf_op jit(solution)/shard_map/ppermute | solution.py:310
  188.1 36.9 %collective-permute-start.40 = (bf16[256,1536]{1,0:T(8,128)(2,1)}, bf16[256,1536]{1,0:T(8,128)(2,1)S(1)}, u32[]{:S(2)}, u32[]{:S(2)}) collective-permute-start(bf16[256,1536]{1,0:T(8,128)(2,1)} %param.23), channel_id=1, source_target_pairs={{0,4},{4,0},{8,12},{12,8},{16,20},{20,16},{24,28},{28,24},{1,5},{5... | collective-permute-start | bytes 2359304 | tf_op jit(solution)/shard_map/ppermute | solution.py:314
  195.4 45.5 %collective-permute-start.50 = (bf16[1536,256]{1,0:T(8,128)(2,1)S(1)}, bf16[1536,256]{1,0:T(8,128)(2,1)S(1)}, u32[]{:S(2)}, u32[]{:S(2)}) collective-permute-start(bf16[1536,256]{1,0:T(8,128)(2,1)S(1)} %copy-done.42), channel_id=1, source_target_pairs={{0,4},{4,0},{8,12},{12,8},{16,20},{20,16},{24,28},{28,24},{1,5},{5... | collective-permute-start | bytes 2359304 | tf_op jit(solution)/shard_map/ppermute | solution.py:314
  208.3 37.6 %collective-permute-start.21 = (bf16[256,2048]{1,0:T(8,128)(2,1)S(1)}, bf16[256,2048]{1,0:T(8,128)(2,1)S(1)}, u32[]{:S(2)}, u32[]{:S(2)}) collective-permute-start(bf16[256,2048]{1,0:T(8,128)(2,1)S(1)} %dynamic-slice_convert_fusion.3), channel_id=1, source_target_pairs={{0,2},{1,3},{2,0},{3,1},{4,6},{5,7},{6,4},{7,5},{8,10},{9,11},{10,... | collective-permute-start | bytes 3145736 | tf_op jit(solution)/shard_map/ppermute | solution.py:263
  240.9 58.9 %collective-permute-start.38 = (bf16[256,1536]{1,0:T(8,128)(2,1)}, bf16[256,1536]{1,0:T(8,128)(2,1)S(1)}, u32[]{:S(2)}, u32[]{:S(2)}) collective-permute-start(bf16[256,1536]{1,0:T(8,128)(2,1)} %param.23), channel_id=1, source_target_pairs={{0,16},{4,20},{24,8},{28,12},{1,17},{5,21},{25,9},{29,13},{2,18},{... | collective-permute-start | bytes 2359304 | tf_op jit(solution)/shard_map/ppermute | solution.py:310
  242.5 59.0 %collective-permute-start.34 = (bf16[256,1536]{1,0:T(8,128)(2,1)}, bf16[256,1536]{1,0:T(8,128)(2,1)S(1)}, u32[]{:S(2)}, u32[]{:S(2)}) collective-permute-start(bf16[256,1536]{1,0:T(8,128)(2,1)} %param.23), channel_id=1, source_target_pairs={{8,0},{12,4},{16,8},{20,12},{24,16},{28,20},{9,1},{13,5},{17,9},{2... | collective-permute-start | bytes 2359304 | tf_op jit(solution)/shard_map/ppermute | solution.py:310
  243.8 38.1 %collective-permute-start.26 = (bf16[256,1536]{1,0:T(8,128)(2,1)}, bf16[256,1536]{1,0:T(8,128)(2,1)S(1)}, u32[]{:S(2)}, u32[]{:S(2)}) collective-permute-start(bf16[256,1536]{1,0:T(8,128)(2,1)} %collective-permute-done.24), channel_id=1, source_target_pairs={{8,0},{12,4},{9,1},{13,5},{10,2},{14,6},{11,3},{15,7}} | collective-permute-start | bytes 2359304 | tf_op jit(solution)/shard_map/ppermute | solution.py:323
  245.1 38.4 %collective-permute-start.27 = (bf16[256,1536]{1,0:T(8,128)(2,1)}, bf16[256,1536]{1,0:T(8,128)(2,1)S(1)}, u32[]{:S(2)}, u32[]{:S(2)}) collective-permute-start(bf16[256,1536]{1,0:T(8,128)(2,1)} %collective-permute-done.25), channel_id=1, source_target_pairs={{16,24},{20,28},{17,25},{21,29},{18,26},{22,30},{19,27},{23,31}} | collective-permute-start | bytes 2359304 | tf_op jit(solution)/shard_map/ppermute | solution.py:322
  245.9 51.0 %collective-permute-start.29 = (bf16[256,1536]{1,0:T(8,128)(2,1)S(1)}, bf16[256,1536]{1,0:T(8,128)(2,1)S(1)}, u32[]{:S(2)}, u32[]{:S(2)}) collective-permute-start(bf16[256,1536]{1,0:T(8,128)(2,1)S(1)} %collective-permute-done.28), channel_id=1, source_target_pairs={{16,24},{20,28},{8,0},{12,4},{17,25},{21,29},{9,1},{13,5},{18,26},... | collective-permute-start | bytes 2359304 | tf_op jit(solution)/shard_map/ppermute | solution.py:324
  283.5 35.0 %collective-permute-start.48 = (bf16[1536,256]{1,0:T(8,128)(2,1)S(1)}, bf16[1536,256]{1,0:T(8,128)(2,1)S(1)}, u32[]{:S(2)}, u32[]{:S(2)}) collective-permute-start(bf16[1536,256]{1,0:T(8,128)(2,1)S(1)} %copy-done.42), channel_id=1, source_target_pairs={{0,16},{4,20},{24,8},{28,12},{1,17},{5,21},{25,9},{29,13},{2,18},{... | collective-permute-start | bytes 2359304 | tf_op jit(solution)/shard_map/ppermute | solution.py:310
  299.8 56.1 %collective-permute-start.45 = (bf16[1536,256]{1,0:T(8,128)(2,1)S(1)}, bf16[1536,256]{1,0:T(8,128)(2,1)S(1)}, u32[]{:S(2)}, u32[]{:S(2)}) collective-permute-start(bf16[1536,256]{1,0:T(8,128)(2,1)S(1)} %copy-done.42), channel_id=1, source_target_pairs={{0,8},{4,12},{8,16},{12,20},{16,24},{20,28},{1,9},{5,13},{9,17},{1... | collective-permute-start | bytes 2359304 | tf_op jit(solution)/shard_map/ppermute | solution.py:310
  301.6 54.9 %collective-permute-start.44 = (bf16[1536,256]{1,0:T(8,128)(2,1)S(1)}, bf16[1536,256]{1,0:T(8,128)(2,1)S(1)}, u32[]{:S(2)}, u32[]{:S(2)}) collective-permute-start(bf16[1536,256]{1,0:T(8,128)(2,1)S(1)} %copy-done.42), channel_id=1, source_target_pairs={{8,0},{12,4},{16,8},{20,12},{24,16},{28,20},{9,1},{13,5},{17,9},{2... | collective-permute-start | bytes 2359304 | tf_op jit(solution)/shard_map/ppermute | solution.py:310
  302.9 54.3 %collective-permute-start.39 = (bf16[256,1536]{1,0:T(8,128)(2,1)S(1)}, bf16[256,1536]{1,0:T(8,128)(2,1)S(1)}, u32[]{:S(2)}, u32[]{:S(2)}) collective-permute-start(bf16[256,1536]{1,0:T(8,128)(2,1)S(1)} %collective-permute-done.38), channel_id=1, source_target_pairs={{16,24},{20,28},{8,0},{12,4},{17,25},{21,29},{9,1},{13,5},{18,26},... | collective-permute-start | bytes 2359304 | tf_op jit(solution)/shard_map/ppermute | solution.py:324
  318.5 35.8 %collective-permute-start.36 = (bf16[256,1536]{1,0:T(8,128)(2,1)S(1)}, bf16[256,1536]{1,0:T(8,128)(2,1)S(1)}, u32[]{:S(2)}, u32[]{:S(2)}) collective-permute-start(bf16[256,1536]{1,0:T(8,128)(2,1)S(1)} %collective-permute-done.34), channel_id=1, source_target_pairs={{8,0},{12,4},{9,1},{13,5},{10,2},{14,6},{11,3},{15,7}} | collective-permute-start | bytes 2359304 | tf_op jit(solution)/shard_map/ppermute | solution.py:323
  320.2 35.4 %collective-permute-start.37 = (bf16[256,1536]{1,0:T(8,128)(2,1)S(1)}, bf16[256,1536]{1,0:T(8,128)(2,1)S(1)}, u32[]{:S(2)}, u32[]{:S(2)}) collective-permute-start(bf16[256,1536]{1,0:T(8,128)(2,1)S(1)} %collective-permute-done.35), channel_id=1, source_target_pairs={{16,24},{20,28},{17,25},{21,29},{18,26},{22,30},{19,27},{23,31}} | collective-permute-start | bytes 2359304 | tf_op jit(solution)/shard_map/ppermute | solution.py:322
  355.6 35.6 %collective-permute-start.23 = (bf16[512,2048]{1,0:T(8,128)(2,1)S(1)}, bf16[512,2048]{1,0:T(8,128)(2,1)S(1)}, u32[]{:S(2)}, u32[]{:S(2)}) collective-permute-start(bf16[512,2048]{1,0:T(8,128)(2,1)S(1)} %pad_maximum_fusion.9), channel_id=1, source_target_pairs={{0,1},{1,0},{2,3},{3,2},{4,5},{5,4},{6,7},{7,6},{8,9},{9,8},{10,11... | collective-permute-start | bytes 6291464 | tf_op jit(solution)/shard_map/ppermute | solution.py:281
  355.9 39.9 %collective-permute-start.31 = (bf16[256,1536]{1,0:T(8,128)(2,1)S(1)}, bf16[256,1536]{1,0:T(8,128)(2,1)S(1)}, u32[]{:S(2)}, u32[]{:S(2)}) collective-permute-start(bf16[256,1536]{1,0:T(8,128)(2,1)S(1)} %get-tuple-element.93), channel_id=1, source_target_pairs={{0,4},{4,0},{8,12},{12,8},{16,20},{20,16},{24,28},{28,24},{1,5},{5... | collective-permute-start | bytes 2359304 | tf_op jit(solution)/shard_map/ppermute | solution.py:349
  357.2 32.1 %collective-permute-start.46 = (bf16[1536,256]{1,0:T(8,128)(2,1)S(1)}, bf16[1536,256]{1,0:T(8,128)(2,1)S(1)}, u32[]{:S(2)}, u32[]{:S(2)}) collective-permute-start(bf16[1536,256]{1,0:T(8,128)(2,1)S(1)} %collective-permute-done.44), channel_id=1, source_target_pairs={{8,0},{12,4},{9,1},{13,5},{10,2},{14,6},{11,3},{15,7}} | collective-permute-start | bytes 2359304 | tf_op jit(solution)/shard_map/ppermute | solution.py:323
  378.1 35.7 %collective-permute-start.33 = (bf16[256,1536]{1,0:T(8,128)(2,1)S(1)}, bf16[256,1536]{1,0:T(8,128)(2,1)S(1)}, u32[]{:S(2)}, u32[]{:S(2)}) collective-permute-start(bf16[256,1536]{1,0:T(8,128)(2,1)S(1)} %broadcast_select_fusion.23), channel_id=1, source_target_pairs={{0,4},{4,0},{8,12},{12,8},{16,20},{20,16},{24,28},{28,24},{1,5},{5... | collective-permute-start | bytes 2359304 | tf_op jit(solution)/shard_map/ppermute | solution.py:349
  389.3 41.4 %collective-permute-start.43 = (bf16[256,1536]{1,0:T(8,128)(2,1)S(1)}, bf16[256,1536]{1,0:T(8,128)(2,1)S(1)}, u32[]{:S(2)}, u32[]{:S(2)}) collective-permute-start(bf16[256,1536]{1,0:T(8,128)(2,1)S(1)} %broadcast_select_fusion.22), channel_id=1, source_target_pairs={{0,4},{4,0},{8,12},{12,8},{16,20},{20,16},{24,28},{28,24},{1,5},{5... | collective-permute-start | bytes 2359304 | tf_op jit(solution)/shard_map/ppermute | solution.py:349
  391.2 56.5 %collective-permute-start.42 = (bf16[256,1536]{1,0:T(8,128)(2,1)S(1)}, bf16[256,1536]{1,0:T(8,128)(2,1)}, u32[]{:S(2)}, u32[]{:S(2)}) collective-permute-start(bf16[256,1536]{1,0:T(8,128)(2,1)S(1)} %get-tuple-element.102), channel_id=1, source_target_pairs={{0,4},{4,0},{8,12},{12,8},{16,20},{20,16},{24,28},{28,24},{1,5},{5... | collective-permute-start | bytes 2359304 | tf_op jit(solution)/shard_map/ppermute | solution.py:349
  395.8 68.7 %collective-permute-start.41 = (bf16[256,1536]{1,0:T(8,128)(2,1)S(1)}, bf16[256,1536]{1,0:T(8,128)(2,1)}, u32[]{:S(2)}, u32[]{:S(2)}) collective-permute-start(bf16[256,1536]{1,0:T(8,128)(2,1)S(1)} %get-tuple-element.101), channel_id=1, source_target_pairs={{0,4},{4,0},{8,12},{12,8},{16,20},{20,16},{24,28},{28,24},{1,5},{5... | collective-permute-start | bytes 2359304 | tf_op jit(solution)/shard_map/ppermute | solution.py:349
  397.0 105.0 %collective-permute-start.52 = (bf16[1536,256]{1,0:T(8,128)(2,1)}, bf16[1536,256]{1,0:T(8,128)(2,1)}, u32[]{:S(2)}, u32[]{:S(2)}) collective-permute-start(bf16[1536,256]{1,0:T(8,128)(2,1)} %get-tuple-element.111), channel_id=1, source_target_pairs={{0,4},{4,0},{8,12},{12,8},{16,20},{20,16},{24,28},{28,24},{1,5},{5... | collective-permute-start | bytes 2359304 | tf_op jit(solution)/shard_map/ppermute | solution.py:349
  413.8 88.1 %collective-permute-start.51 = (bf16[1536,256]{1,0:T(8,128)(2,1)}, bf16[1536,256]{1,0:T(8,128)(2,1)}, u32[]{:S(2)}, u32[]{:S(2)}) collective-permute-start(bf16[1536,256]{1,0:T(8,128)(2,1)} %get-tuple-element.110), channel_id=1, source_target_pairs={{0,4},{4,0},{8,12},{12,8},{16,20},{20,16},{24,28},{28,24},{1,5},{5... | collective-permute-start | bytes 2359304 | tf_op jit(solution)/shard_map/ppermute | solution.py:349
  430.7 80.1 %collective-permute-start.53 = (bf16[1536,256]{1,0:T(8,128)(2,1)}, bf16[1536,256]{1,0:T(8,128)(2,1)}, u32[]{:S(2)}, u32[]{:S(2)}) collective-permute-start(bf16[1536,256]{1,0:T(8,128)(2,1)} %broadcast_select_fusion.20), channel_id=1, source_target_pairs={{0,4},{4,0},{8,12},{12,8},{16,20},{20,16},{24,28},{28,24},{1,5},{5... | collective-permute-start | bytes 2359304 | tf_op jit(solution)/shard_map/ppermute | solution.py:349
  557.3 37.0 %collective-permute-start.76 = (bf16[256,1536]{1,0:T(8,128)(2,1)}, bf16[256,1536]{1,0:T(8,128)(2,1)}, u32[]{:S(2)}, u32[]{:S(2)}) collective-permute-start(bf16[256,1536]{1,0:T(8,128)(2,1)} %get-tuple-element.187), channel_id=1, source_target_pairs={{0,4},{4,0},{8,12},{12,8},{16,20},{20,16},{24,28},{28,24},{1,5},{5... | collective-permute-start | bytes 2359304 | tf_op jit(solution)/shard_map/ppermute | solution.py:386
  558.8 51.9 %collective-permute-start.78 = (bf16[256,1536]{1,0:T(8,128)(2,1)S(1)}, bf16[256,1536]{1,0:T(8,128)(2,1)}, u32[]{:S(2)}, u32[]{:S(2)}) collective-permute-start(bf16[256,1536]{1,0:T(8,128)(2,1)S(1)} %get-tuple-element.186), channel_id=1, source_target_pairs={{0,4},{4,0},{8,12},{12,8},{16,20},{20,16},{24,28},{28,24},{1,5},{5... | collective-permute-start | bytes 2359304 | tf_op jit(solution)/shard_map/ppermute | solution.py:386
  570.9 43.2 %collective-permute-start.55 = (bf16[256,2048]{1,0:T(8,128)(2,1)S(1)}, bf16[256,2048]{1,0:T(8,128)(2,1)S(1)}, u32[]{:S(2)}, u32[]{:S(2)}) collective-permute-start(bf16[256,2048]{1,0:T(8,128)(2,1)S(1)} %dynamic-slice_convert_fusion.2), channel_id=1, source_target_pairs={{0,2},{1,3},{2,0},{3,1},{4,6},{5,7},{6,4},{7,5},{8,10},{9,11},{10,... | collective-permute-start | bytes 3145736 | tf_op jit(solution)/shard_map/ppermute | solution.py:263
  643.5 73.7 %collective-permute-start.58 = (bf16[512,2048]{1,0:T(8,128)(2,1)S(1)}, bf16[512,2048]{1,0:T(8,128)(2,1)S(1)}, u32[]{:S(2)}, u32[]{:S(2)}) collective-permute-start(bf16[512,2048]{1,0:T(8,128)(2,1)S(1)} %pad_maximum_fusion.10), channel_id=1, source_target_pairs={{0,1},{1,0},{2,3},{3,2},{4,5},{5,4},{6,7},{7,6},{8,9},{9,8},{10,11... | collective-permute-start | bytes 6291464 | tf_op jit(solution)/shard_map/ppermute | solution.py:281
  644.4 36.7 %collective-permute-start.61 = (bf16[256,1536]{1,0:T(8,128)(2,1)S(1)}, bf16[256,1536]{1,0:T(8,128)(2,1)S(1)}, u32[]{:S(2)}, u32[]{:S(2)}) collective-permute-start(bf16[256,1536]{1,0:T(8,128)(2,1)S(1)} %get-tuple-element.192), channel_id=1, source_target_pairs={{0,4},{4,0},{8,12},{12,8},{16,20},{20,16},{24,28},{28,24},{1,5},{5... | collective-permute-start | bytes 2359304 | tf_op jit(solution)/shard_map/ppermute | solution.py:386
  645.9 52.0 %collective-permute-start.89 = (bf16[256,1536]{1,0:T(8,128)(2,1)S(1)}, bf16[256,1536]{1,0:T(8,128)(2,1)S(1)}, u32[]{:S(2)}, u32[]{:S(2)}) collective-permute-start(bf16[256,1536]{1,0:T(8,128)(2,1)S(1)} %get-tuple-element.191), channel_id=1, source_target_pairs={{0,4},{4,0},{8,12},{12,8},{16,20},{20,16},{24,28},{28,24},{1,5},{5... | collective-permute-start | bytes 2359304 | tf_op jit(solution)/shard_map/ppermute | solution.py:386
  646.5 68.3 %collective-permute-start.91 = (bf16[256,1536]{1,0:T(8,128)(2,1)S(1)}, bf16[256,1536]{1,0:T(8,128)(2,1)S(1)}, u32[]{:S(2)}, u32[]{:S(2)}) collective-permute-start(bf16[256,1536]{1,0:T(8,128)(2,1)S(1)} %get-tuple-element.190), channel_id=1, source_target_pairs={{0,4},{4,0},{8,12},{12,8},{16,20},{20,16},{24,28},{28,24},{1,5},{5... | collective-permute-start | bytes 2359304 | tf_op jit(solution)/shard_map/ppermute | solution.py:386
  664.3 132.5 %collective-permute-start.82 = (bf16[256,1536]{1,0:T(8,128)(2,1)}, bf16[256,1536]{1,0:T(8,128)(2,1)}, u32[]{:S(2)}, u32[]{:S(2)}) collective-permute-start(bf16[256,1536]{1,0:T(8,128)(2,1)} %get-tuple-element.178), channel_id=1, source_target_pairs={{0,4},{4,0},{8,12},{12,8},{16,20},{20,16},{24,28},{28,24},{1,5},{5... | collective-permute-start | bytes 2359304 | tf_op jit(solution)/shard_map/ppermute | solution.py:386
  681.1 81.0 %collective-permute-start.83 = (bf16[256,1536]{1,0:T(8,128)(2,1)}, bf16[256,1536]{1,0:T(8,128)(2,1)}, u32[]{:S(2)}, u32[]{:S(2)}) collective-permute-start(bf16[256,1536]{1,0:T(8,128)(2,1)} %get-tuple-element.181), channel_id=1, source_target_pairs={{0,4},{4,0},{8,12},{12,8},{16,20},{20,16},{24,28},{28,24},{1,5},{5... | collective-permute-start | bytes 2359304 | tf_op jit(solution)/shard_map/ppermute | solution.py:386
  698.0 71.2 %collective-permute-start.85 = (bf16[256,1536]{1,0:T(8,128)(2,1)}, bf16[256,1536]{1,0:T(8,128)(2,1)}, u32[]{:S(2)}, u32[]{:S(2)}) collective-permute-start(bf16[256,1536]{1,0:T(8,128)(2,1)} %get-tuple-element.180), channel_id=1, source_target_pairs={{0,4},{4,0},{8,12},{12,8},{16,20},{20,16},{24,28},{28,24},{1,5},{5... | collective-permute-start | bytes 2359304 | tf_op jit(solution)/shard_map/ppermute | solution.py:386
  714.8 67.5 %collective-permute-start.87 = (bf16[256,1536]{1,0:T(8,128)(2,1)}, bf16[256,1536]{1,0:T(8,128)(2,1)}, u32[]{:S(2)}, u32[]{:S(2)}) collective-permute-start(bf16[256,1536]{1,0:T(8,128)(2,1)} %get-tuple-element.179), channel_id=1, source_target_pairs={{0,4},{4,0},{8,12},{12,8},{16,20},{20,16},{24,28},{28,24},{1,5},{5... | collective-permute-start | bytes 2359304 | tf_op jit(solution)/shard_map/ppermute | solution.py:386
  758.7 152.1 %collective-permute-start.64 = (bf16[512,2048]{1,0:T(8,128)(2,1)}, bf16[512,2048]{1,0:T(8,128)(2,1)}, u32[]{:S(2)}, u32[]{:S(2)}) collective-permute-start(bf16[512,2048]{1,0:T(8,128)(2,1)} %add_convert_fusion), channel_id=1, source_target_pairs={{0,1},{1,0},{2,3},{3,2},{4,5},{5,4},{6,7},{7,6},{8,9},{9,8},{10,11... | collective-permute-start | bytes 6291464 | tf_op jit(solution)/shard_map/ppermute | solution.py:257
  762.1 38.0 %collective-permute-start.100 = (bf16[256,512]{1,0:T(8,128)(2,1)S(1)}, bf16[256,512]{1,0:T(8,128)(2,1)S(1)}, u32[]{:S(2)}, u32[]{:S(2)}) collective-permute-start(bf16[256,512]{1,0:T(8,128)(2,1)S(1)} %get-tuple-element.232), channel_id=1, source_target_pairs={{0,4},{4,0},{8,12},{12,8},{16,20},{20,16},{24,28},{28,24},{1,5},{5... | collective-permute-start | bytes 786440 | tf_op jit(solution)/shard_map/ppermute | solution.py:386
  802.2 31.9 %collective-permute-start.73 = (bf16[256,768]{1,0:T(8,128)(2,1)S(1)}, bf16[256,768]{1,0:T(8,128)(2,1)}, u32[]{:S(2)}, u32[]{:S(2)}) collective-permute-start(bf16[256,768]{1,0:T(8,128)(2,1)S(1)} %get-tuple-element.225), channel_id=1, source_target_pairs={{0,4},{4,0},{8,12},{12,8},{16,20},{20,16},{24,28},{28,24},{1,5},{5... | collective-permute-start | bytes 1179656 | tf_op jit(solution)/shard_map/ppermute | solution.py:386
  808.9 104.7 %collective-permute-start.59 = (bf16[512,2048]{1,0:T(8,128)(2,1)}, bf16[512,2048]{1,0:T(8,128)(2,1)}, u32[]{:S(2)}, u32[]{:S(2)}) collective-permute-start(bf16[512,2048]{1,0:T(8,128)(2,1)} %convolution_convert_fusion.6), channel_id=1, source_target_pairs={{0,1},{1,0},{2,3},{3,2},{4,5},{5,4},{6,7},{7,6},{8,9},{9,8},{10,11... | collective-permute-start | bytes 6291464 | tf_op jit(solution)/shard_map/ppermute | solution.py:257
  850.9 63.4 %collective-permute-start.81 = (bf16[256,1536]{1,0:T(8,128)(2,1)S(1)}, bf16[256,1536]{1,0:T(8,128)(2,1)S(1)}, u32[]{:S(2)}, u32[]{:S(2)}) collective-permute-start(bf16[256,1536]{1,0:T(8,128)(2,1)S(1)} %get-tuple-element.189), channel_id=1, source_target_pairs={{0,4},{4,0},{8,12},{12,8},{16,20},{20,16},{24,28},{28,24},{1,5},{5... | collective-permute-start | bytes 2359304 | tf_op jit(solution)/shard_map/ppermute | solution.py:386
  862.0 48.8 %collective-permute-start.99 = (bf16[256,512]{1,0:T(8,128)(2,1)S(1)}, bf16[256,512]{1,0:T(8,128)(2,1)S(1)}, u32[]{:S(2)}, u32[]{:S(2)}) collective-permute-start(bf16[256,512]{1,0:T(8,128)(2,1)S(1)} %get-tuple-element.236), channel_id=1, source_target_pairs={{0,16},{4,20},{8,24},{12,28},{16,0},{20,4},{24,8},{28,12},{1,17},{... | collective-permute-start | bytes 786440 | tf_op jit(solution)/shard_map/ppermute | solution.py:404
  870.1 48.5 %collective-permute-start.90 = (bf16[256,1536]{1,0:T(8,128)(2,1)S(1)}, bf16[256,1536]{1,0:T(8,128)(2,1)S(1)}, u32[]{:S(2)}, u32[]{:S(2)}) collective-permute-start(bf16[256,1536]{1,0:T(8,128)(2,1)S(1)} %copy-done.47), channel_id=1, source_target_pairs={{0,8},{4,12},{8,16},{12,20},{16,24},{20,28},{24,0},{28,4},{1,9},{5... | collective-permute-start | bytes 2359304 | tf_op jit(solution)/shard_map/ppermute | solution.py:404
  910.8 70.4 %collective-permute-start.92 = (bf16[256,1536]{1,0:T(8,128)(2,1)}, bf16[256,1536]{1,0:T(8,128)(2,1)}, u32[]{:S(2)}, u32[]{:S(2)}) collective-permute-start(bf16[256,1536]{1,0:T(8,128)(2,1)} %get-tuple-element.193), channel_id=1, source_target_pairs={{0,16},{4,20},{8,24},{12,28},{16,0},{20,4},{24,8},{28,12},{1,17},{... | collective-permute-start | bytes 2359304 | tf_op jit(solution)/shard_map/ppermute | solution.py:404
  910.8 76.8 %collective-permute-start.93 = (bf16[256,1536]{1,0:T(8,128)(2,1)}, bf16[256,1536]{1,0:T(8,128)(2,1)}, u32[]{:S(2)}, u32[]{:S(2)}) collective-permute-start(bf16[256,1536]{1,0:T(8,128)(2,1)} %get-tuple-element.195), channel_id=1, source_target_pairs={{0,24},{4,28},{8,0},{12,4},{16,8},{20,12},{24,16},{28,20},{1,25},{... | collective-permute-start | bytes 2359304 | tf_op jit(solution)/shard_map/ppermute | solution.py:404
  914.3 40.0 %collective-permute-start.103 = (bf16[256,768]{1,0:T(8,128)(2,1)S(1)}, bf16[256,768]{1,0:T(8,128)(2,1)S(1)}, u32[]{:S(2)}, u32[]{:S(2)}) collective-permute-start(bf16[256,768]{1,0:T(8,128)(2,1)S(1)} %get-tuple-element.230), channel_id=1, source_target_pairs={{0,8},{4,12},{8,16},{12,20},{16,24},{20,28},{24,0},{28,4},{1,9},{5... | collective-permute-start | bytes 1179656 | tf_op jit(solution)/shard_map/ppermute | solution.py:404
  918.7 56.0 %collective-permute-start.105 = (bf16[256,768]{1,0:T(8,128)(2,1)S(1)}, bf16[256,768]{1,0:T(8,128)(2,1)}, u32[]{:S(2)}, u32[]{:S(2)}) collective-permute-start(bf16[256,768]{1,0:T(8,128)(2,1)S(1)} %get-tuple-element.229), channel_id=1, source_target_pairs={{0,16},{4,20},{8,24},{12,28},{16,0},{20,4},{24,8},{28,12},{1,17},{... | collective-permute-start | bytes 1179656 | tf_op jit(solution)/shard_map/ppermute | solution.py:404
  921.9 53.2 %collective-permute-start.107 = (bf16[256,768]{1,0:T(8,128)(2,1)S(1)}, bf16[256,768]{1,0:T(8,128)(2,1)S(1)}, u32[]{:S(2)}, u32[]{:S(2)}) collective-permute-start(bf16[256,768]{1,0:T(8,128)(2,1)S(1)} %get-tuple-element.228), channel_id=1, source_target_pairs={{0,24},{4,28},{8,0},{12,4},{16,8},{20,12},{24,16},{28,20},{1,25},{... | collective-permute-start | bytes 1179656 | tf_op jit(solution)/shard_map/ppermute | solution.py:404
  954.3 36.2 %collective-permute-start.94 = (bf16[256,768]{1,0:T(8,128)(2,1)}, bf16[256,768]{1,0:T(8,128)(2,1)}, u32[]{:S(2)}, u32[]{:S(2)}) collective-permute-start(bf16[256,768]{1,0:T(8,128)(2,1)} %get-tuple-element.216), channel_id=1, source_target_pairs={{0,4},{4,0},{8,12},{12,8},{16,20},{20,16},{24,28},{28,24},{1,5},{5... | collective-permute-start | bytes 1179656 | tf_op jit(solution)/shard_map/ppermute | solution.py:386
  974.6 101.2 %collective-permute-start.65 = (bf16[256,2048]{1,0:T(8,128)(2,1)}, bf16[256,2048]{1,0:T(8,128)(2,1)S(1)}, u32[]{:S(2)}, u32[]{:S(2)}) collective-permute-start(bf16[256,2048]{1,0:T(8,128)(2,1)} %dynamic-slice_convert_fusion), channel_id=1, source_target_pairs={{0,2},{1,3},{2,0},{3,1},{4,6},{5,7},{6,4},{7,5},{8,10},{9,11},{10,... | collective-permute-start | bytes 3145736 | tf_op jit(solution)/shard_map/ppermute | solution.py:263
  975.9 100.0 %collective-permute-start.60 = (bf16[256,2048]{1,0:T(8,128)(2,1)}, bf16[256,2048]{1,0:T(8,128)(2,1)}, u32[]{:S(2)}, u32[]{:S(2)}) collective-permute-start(bf16[256,2048]{1,0:T(8,128)(2,1)} %dynamic-slice_convert_fusion.1), channel_id=1, source_target_pairs={{0,2},{1,3},{2,0},{3,1},{4,6},{5,7},{6,4},{7,5},{8,10},{9,11},{10,... | collective-permute-start | bytes 3145736 | tf_op jit(solution)/shard_map/ppermute | solution.py:263
  987.7 53.5 %collective-permute-start.86 = (bf16[256,1536]{1,0:T(8,128)(2,1)}, bf16[256,1536]{1,0:T(8,128)(2,1)S(1)}, u32[]{:S(2)}, u32[]{:S(2)}) collective-permute-start(bf16[256,1536]{1,0:T(8,128)(2,1)} %get-tuple-element.183), channel_id=1, source_target_pairs={{0,16},{4,20},{8,24},{12,28},{16,0},{20,4},{24,8},{28,12},{1,17},{... | collective-permute-start | bytes 2359304 | tf_op jit(solution)/shard_map/ppermute | solution.py:404
  990.4 82.1 %collective-permute-start.88 = (bf16[256,1536]{1,0:T(8,128)(2,1)}, bf16[256,1536]{1,0:T(8,128)(2,1)S(1)}, u32[]{:S(2)}, u32[]{:S(2)}) collective-permute-start(bf16[256,1536]{1,0:T(8,128)(2,1)} %get-tuple-element.182), channel_id=1, source_target_pairs={{0,24},{4,28},{8,0},{12,4},{16,8},{20,12},{24,16},{28,20},{1,25},{... | collective-permute-start | bytes 2359304 | tf_op jit(solution)/shard_map/ppermute | solution.py:404
  1008.6 116.7 %collective-permute-start.80 = (bf16[256,1536]{1,0:T(8,128)(2,1)S(1)}, bf16[256,1536]{1,0:T(8,128)(2,1)S(1)}, u32[]{:S(2)}, u32[]{:S(2)}) collective-permute-start(bf16[256,1536]{1,0:T(8,128)(2,1)S(1)} %copy-done.43), channel_id=1, source_target_pairs={{0,24},{4,28},{8,0},{12,4},{16,8},{20,12},{24,16},{28,20},{1,25},{... | collective-permute-start | bytes 2359304 | tf_op jit(solution)/shard_map/ppermute | solution.py:404
  1041.1 64.1 %collective-permute-start.77 = (bf16[256,1536]{1,0:T(8,128)(2,1)}, bf16[256,1536]{1,0:T(8,128)(2,1)S(1)}, u32[]{:S(2)}, u32[]{:S(2)}) collective-permute-start(bf16[256,1536]{1,0:T(8,128)(2,1)} %get-tuple-element.197), channel_id=1, source_target_pairs={{0,8},{4,12},{8,16},{12,20},{16,24},{20,28},{24,0},{28,4},{1,9},{5... | collective-permute-start | bytes 2359304 | tf_op jit(solution)/shard_map/ppermute | solution.py:404
  1072.5 52.8 %collective-permute-start.79 = (bf16[256,1536]{1,0:T(8,128)(2,1)S(1)}, bf16[256,1536]{1,0:T(8,128)(2,1)S(1)}, u32[]{:S(2)}, u32[]{:S(2)}) collective-permute-start(bf16[256,1536]{1,0:T(8,128)(2,1)S(1)} %copy-done.44), channel_id=1, source_target_pairs={{0,16},{4,20},{8,24},{12,28},{16,0},{20,4},{24,8},{28,12},{1,17},{... | collective-permute-start | bytes 2359304 | tf_op jit(solution)/shard_map/ppermute | solution.py:404
  1105.3 42.3 %collective-permute-start.63 = (bf16[512,2048]{1,0:T(8,128)(2,1)}, bf16[512,2048]{1,0:T(8,128)(2,1)}, u32[]{:S(2)}, u32[]{:S(2)}) collective-permute-start(bf16[512,2048]{1,0:T(8,128)(2,1)} %pad_maximum_fusion.11), channel_id=1, source_target_pairs={{0,1},{1,0},{2,3},{3,2},{4,5},{5,4},{6,7},{7,6},{8,9},{9,8},{10,11... | collective-permute-start | bytes 6291464 | tf_op jit(solution)/shard_map/ppermute | solution.py:281
  1128.7 41.4 %collective-permute-start.67 = (bf16[512,2048]{1,0:T(8,128)(2,1)}, bf16[512,2048]{1,0:T(8,128)(2,1)}, u32[]{:S(2)}, u32[]{:S(2)}) collective-permute-start(bf16[512,2048]{1,0:T(8,128)(2,1)} %pad_maximum_fusion.12), channel_id=1, source_target_pairs={{0,1},{1,0},{2,3},{3,2},{4,5},{5,4},{6,7},{7,6},{8,9},{9,8},{10,11... | collective-permute-start | bytes 6291464 | tf_op jit(solution)/shard_map/ppermute | solution.py:281
  (139 other events, 2625.4 us)
